TPU v7x, 128 devices: a whole 4x4x4 slice. The times are simulated.
128 devices in a mesh: scan: 4 (over y), slab: 32 (over x, z, core).
Axes of the slice: x: 4, y: 4, z: 4, core: 2. Of those that a mesh axis runs over, the one named last changes fastest.
Arguments:
- solution: float32 [6144, 2048], P(('scan', 'slab')), parts along dimension 0, may hold values from -6 to 6
- direction: float32 [6144, 2048], P(('scan', 'slab')), parts along dimension 0, may hold values from -20 to 20
- gradient: float32 [6144, 2048], P(('scan', 'slab')), parts along dimension 0, may hold values from -40 to 40
- residual: float32 [2048, 64, 896], P(('scan', 'slab')), parts along dimension 0, may hold values from -20 to 20
- tiles: bfloat16 [4, 2048, 896], replicated, may hold values from -0.125 to 0.125
- offsets: int32 [2048], P(('scan', 'slab')), parts along dimension 0, may hold values from 1 to 1472, as said below
Outputs:
- solution_next: float32 [6144, 2048], P(('scan', 'slab')), parts along dimension 0
- residual_next: float32 [2048, 64, 896], P(('scan', 'slab')), parts along dimension 0
- gradient_next: float32 [6144, 2048], P(('scan', 'slab')), parts along dimension 0
- direction_next: float32 [6144, 2048], P(('scan', 'slab')), parts along dimension 0
There are 4 independent parts, one for each index of `scan`. A program takes and returns all parts, laid end to end along the dimension named above; an argument that names none is the same for every part. Nothing has to cross between parts.
Inputs may be any that keep to these rules, and one draw needn't show every extreme that they name: View v belongs to slab v // 16, whose planes are s * 48 to s * 48 + 47 for slab s; its window offsets[v] to offsets[v] + 63 meets that slab and lies within the slab before it, the slab itself and the slab after it; offsets are 1 or more.
All inputs are finite; a program needn't handle non-finite values.
Results may differ from a plain program's by a relative error of at most 0.0029.
Values may be sent and summed in bfloat16 or wider, within the bound.
No kernel may reach another device: no remote copies, remote signals or barrier semaphores. Data moves between devices by JAX's collectives and lax.ppermute only.
A program may use at most 192 MiB of HBM per device.

v0:
```python
import jax
import jax.numpy as jnp
from jax import lax
from jax.sharding import PartitionSpec as P

ANGLES = 4


def with_halo(block, sides, width):
    for axis, dim in sides:
        count = lax.axis_size(axis)
        forward = [(i, i + 1) for i in range(count - 1)]
        backward = [(target, source) for source, target in forward]
        low = lax.ppermute(
            lax.slice_in_dim(block, block.shape[dim] - width, None, axis=dim), axis, forward
        )
        high = lax.ppermute(lax.slice_in_dim(block, 0, width, axis=dim), axis, backward)
        block = jnp.concatenate([low, block, high], axis=dim)
    return block


def sent_to_all(x, axis):
    copies = jnp.broadcast_to(x, (lax.axis_size(axis), *x.shape))
    return lax.all_to_all(copies, axis, split_axis=0, concat_axis=0, tiled=True)


def of_everyone(x, axis):
    everything = sent_to_all(x, axis)
    return jnp.sum(everything, axis=0)


def in_one(arrays, axis):
    ends = [0]
    for a in arrays:
        ends.append(ends[-1] + a.size)
    total = of_everyone(jnp.concatenate([a.ravel() for a in arrays]), axis)
    return tuple((total[b:e].reshape(a.shape) for a, b, e in zip(arrays, ends, ends[1:])))


def from_behind(block, axis, distance):
    devices = range(lax.axis_size(axis))
    route = [(i - distance, i) for i in devices if i - distance in devices]
    return lax.ppermute(block, axis, route)


def project(volume_rows, firsts, tiles, detector_rows):

    def take_window(first_row):
        return lax.dynamic_slice_in_dim(volume_rows, first_row, detector_rows, 0)

    windows = jax.vmap(take_window)(firsts)
    grouped = windows.reshape(-1, ANGLES, detector_rows, windows.shape[-1])
    images = jnp.einsum("gkir,krc->gkic", grouped, tiles, preferred_element_type=jnp.float32)
    return images.reshape(windows.shape[0], detector_rows, tiles.shape[2])


def backproject(accumulated, firsts, sinogram, tiles):
    detector_rows = sinogram.shape[1]
    grouped = sinogram.reshape(-1, ANGLES, detector_rows, sinogram.shape[2])
    contribution = jnp.einsum("gkic,krc->gkir", grouped, tiles, preferred_element_type=jnp.float32)
    contribution = contribution.reshape(sinogram.shape[0] * detector_rows, tiles.shape[1])
    target_rows = (firsts[:, None] + jnp.arange(detector_rows, dtype=jnp.int32)[None, :]).reshape(
        -1
    )
    return accumulated.at[target_rows].add(contribution)


def local(solution, direction, gradient, residual, tiles, offsets):
    slab_rows = solution.shape[0]
    plane_cells = solution.shape[1]
    detector_rows = residual.shape[1]
    slab_index = lax.axis_index("slab")
    slab_start = slab_index * slab_rows
    direction_half = direction.astype(jnp.bfloat16)
    grad_part = jnp.sum(gradient * gradient)
    nearby = with_halo(direction_half, (("slab", 0),), slab_rows)
    own_firsts = offsets - slab_start + slab_rows
    projected = project(nearby, own_firsts, tiles, detector_rows)
    image_part = jnp.sum(projected * projected)
    grad_norm, image_norm = in_one((grad_part, image_part), "slab")
    step_size = grad_norm / image_norm
    solution_next = solution + step_size * direction
    residual_next = residual - step_size * projected
    residual_half = residual_next.astype(jnp.bfloat16)
    accumulated = backproject(
        jnp.zeros((3 * slab_rows, plane_cells), jnp.float32), own_firsts, residual_half, tiles
    )
    from_above = from_behind(accumulated[:slab_rows], "slab", -1)
    from_below = from_behind(accumulated[2 * slab_rows :], "slab", 1)
    gradient_next = accumulated[slab_rows : 2 * slab_rows] + from_above + from_below
    new_norm = of_everyone(jnp.sum(gradient_next * gradient_next), "slab")
    direction_next = gradient_next + new_norm / grad_norm * direction
    return (solution_next, residual_next, gradient_next, direction_next)


def solution(mesh):
    placed = (
        P(("scan", "slab"), None),
        P(("scan", "slab"), None),
        P(("scan", "slab"), None),
        P(("scan", "slab"), None, None),
        P(),
        P(("scan", "slab")),
    )
    return jax.shard_map(
        local,
        mesh=mesh,
        in_specs=placed,
        out_specs=(
            P(("scan", "slab"), None),
            P(("scan", "slab"), None, None),
            P(("scan", "slab"), None),
            P(("scan", "slab"), None),
        ),
        check_vma=False,
    )
```

profile of v0, /device:TPU:0, one launch (start us, length us, event | category | flops | bytes accessed | tf_op | source)
XLA Modules:
  0.0 153.0 jit_solution(2572535324166380680)
XLA Ops:
  0.6 1.0 convert_element_type.6
  1.7 1.3 collective-permute-start
  3.0 1.3 collective-permute-start.1
  4.3 0.7 subtract_add_fusion
  5.1 1.7 %multiply_reduce_fusion.2 = f32[]{:T(128)} fusion(f32[48,2048]{1,0:T(8,128)} %param.8), kind=kLoop, calls=%fused_computation.21 | loop fusion | flops 196607 | bytes 393220 | tf_op jit(solution)/shard_map/reduce_sum | solution.py:75
  6.8 1.7 %collective-permute-done.1 = bf16[48,2048]{1,0:T(8,128)(2,1)S(1)} collective-permute-done((bf16[48,2048]{1,0:T(8,128)(2,1)S(1)}, bf16[48,2048]{1,0:T(8,128)(2,1)S(1)}, u32[]{:S(2)}, u32[]{:S(2)}) %collective-permute-start.1) | collective-permute-done | bytes 196640 | tf_op jit(solution)/shard_map/ppermute | solution.py:17
  8.6 32.2 %while.1 = (s32[]{:T(128)}, bf16[144,2048]{1,0:T(8,128)(2,1)S(1)}, s32[16,2]{0,1:T(2,128)S(1)}, bf16[16,64,2048]{2,1,0:T(8,128)(2,1)}, s32[]{:T(128)}) while((s32[]{:T(128)}, bf16[144,2048]{1,0:T(8,128)(2,1)S(1)}, s32[16,2]{0,1:T(2,128)S(1)}, bf16[16,64,2048]{2,1,0:T(8,128)(2,1)}, s32[]{:T(128)}) %tuple.27), condition=%wide.while_cond, body=%wide.while_body.sunk | while | flops 2 | bytes 525401 | solution.py:49
  8.7 0.5 slice.43
  9.2 1.4 bitcast_dynamic-update-slice_fusion.2
  11.2 1.4 bitcast_dynamic-update-slice_fusion.2
  13.2 1.4 bitcast_dynamic-update-slice_fusion.2
  14.7 0.5 slice.43
  15.2 1.4 bitcast_dynamic-update-slice_fusion.2
  16.7 0.5 slice.43
  17.2 1.4 bitcast_dynamic-update-slice_fusion.2
  18.7 0.5 slice.43
  19.2 1.4 bitcast_dynamic-update-slice_fusion.2
  20.7 0.5 slice.43
  21.2 1.4 bitcast_dynamic-update-slice_fusion.2
  23.2 1.4 bitcast_dynamic-update-slice_fusion.2
  25.2 1.5 bitcast_dynamic-update-slice_fusion.2
  27.3 1.4 bitcast_dynamic-update-slice_fusion.2
  29.3 1.4 bitcast_dynamic-update-slice_fusion.2
  31.3 1.4 bitcast_dynamic-update-slice_fusion.2
  33.3 1.4 bitcast_dynamic-update-slice_fusion.2
  35.4 1.4 bitcast_dynamic-update-slice_fusion.2
  37.4 1.4 bitcast_dynamic-update-slice_fusion.2
  39.4 1.4 bitcast_dynamic-update-slice_fusion.2
  40.8 13.4 %multiply_reduce_fusion = (f32[]{:T(128)}, f32[4,4,64,896]{3,2,1,0:T(8,128)}) fusion(bf16[4,2048,896]{2,1,0:T(8,128)(2,1)} %param.10, bf16[4,4,64,2048]{3,2,1,0:T(8,128)(2,1)} %bitcast.38), kind=kOutput, calls=%fused_computation.11 | convolution fusion | flops 3759931392 | bytes 22544388 | tf_op jit(solution)/shard_map/gkir,krc->gkic/dot_general | solution.py:53
  54.2 1.4 pad_maximum_fusion.1
  55.5 0.6 broadcast_in_dim.16
  56.2 12.1 %all-to-all-start = ((f32[32,1,2]{2,1,0:T(1,128)}), f32[32,1,2]{2,1,0:T(1,128)S(1)}, u32[]{:S(2)}, u32[]{:S(2)}) async-start(f32[32,1,2]{2,1,0:T(1,128)} %broadcast_in_dim.16), calls=%async_computation | async-start | bytes 32768 | tf_op jit(solution)/shard_map/all_to_all | solution.py:24
  68.3 7.1 %all-to-all-done = f32[32,1,2]{2,1,0:T(1,128)S(1)} async-done(((f32[32,1,2]{2,1,0:T(1,128)}), f32[32,1,2]{2,1,0:T(1,128)S(1)}, u32[]{:S(2)}, u32[]{:S(2)}) %all-to-all-start) | async-done | bytes 288 | tf_op jit(solution)/shard_map/all_to_all | solution.py:24
  75.5 0.6 fusion.16
  77.4 2.3 %multiply_bitcast_fusion = f32[4,4,64,896]{3,2,0,1:T(8,128)S(1)} fusion(f32[4,4,64,896]{3,2,1,0:T(8,128)} %get-tuple-element.33, f32[]{:T(128)S(6)} %div.6), kind=kLoop, calls=%fused_computation.10 | loop fusion | flops 917504 | bytes 7340036 | tf_op jit(solution)/shard_map/mul | solution.py:83
  80.1 1.7 %copy-done = f32[16,64,896]{2,1,0:T(8,128)S(1)} copy-done((f32[16,64,896]{2,1,0:T(8,128)S(1)}, f32[16,64,896]{2,1,0:T(8,128)}, u32[]{:S(2)}) %copy-start) | copy-done | bytes 3670040
  81.8 2.6 %fusion.14 = (bf16[16,64,896]{2,1,0:T(8,128)(2,1)S(1)}, f32[16,64,896]{2,1,0:T(8,128)}) fusion(f32[16,64,896]{2,1,0:T(8,128)S(1)} %copy-done, f32[4,4,64,896]{3,2,1,0:T(8,128)S(1)} %copy.22), kind=kLoop, calls=%fused_computation.28 | loop fusion | flops 1835008 | bytes 12845056 | tf_op jit(solution)/shard_map/convert_element_type | solution.py:84
  84.4 16.7 %fusion.4 = f32[4,4,64,2048]{3,2,0,1:T(8,128)} fusion(bf16[4,2048,896]{2,1,0:T(8,128)(2,1)} %param.10, bf16[4,4,64,896]{3,2,1,0:T(8,128)(2,1)S(1)} %bitcast.36), kind=kOutput, calls=%fused_computation.7 | convolution fusion | flops 3758096384 | bytes 24903680 | tf_op jit(solution)/shard_map/gkic,krc->gkir/dot_general | solution.py:60
  101.1 7.7 %copy.24 = f32[4,4,64,2048]{3,2,1,0:T(8,128)} copy(f32[4,4,64,2048]{3,2,0,1:T(8,128)} %fusion.4) | data formatting | bytes 16777216 | tf_op jit(solution)/shard_map/gkic,krc->gkir/transpose | solution.py:60
  108.8 15.0 %scatter_custom_fusion = f32[144,2048]{1,0:T(8,128)S(1)} fusion(s32[1024]{0:T(1024)S(1)} %bitcast.37, f32[1024,2048]{1,0:T(8,128)} %bitcast.35, f32[]{:T(128)} %constant.6.clone.1), kind=kCustom, calls=%fused_computation.14 | custom fusion | flops 2097152 | bytes 1180160 | tf_op jit(solution)/shard_map/scatter-add | solution.py:65
  123.9 1.3 collective-permute-start.2
  125.2 3.1 %collective-permute-start.3 = (f32[48,2048]{1,0:T(8,128)S(1)}, f32[48,2048]{1,0:T(8,128)S(1)}, u32[]{:S(2)}, u32[]{:S(2)}) collective-permute-start(f32[48,2048]{1,0:T(8,128)S(1)} %get-tuple-element.25), channel_id=1, source_target_pairs={{0,1},{1,2},{2,3},{3,4},{4,5},{5,6},{6,7},{7,8},{8,9},{9,10},{10,1... | collective-permute-start | bytes 1179656 | tf_op jit(solution)/shard_map/ppermute | solution.py:43
  128.3 1.3 collective-permute-done.3
  129.6 0.7 multiply_reduce_fusion.1
  130.3 0.7 broadcast_in_dim.18
  131.0 19.1 %all_to_all.12 = f32[32,1,1]{2,1,0:T(1,128)S(1)} all-to-all(f32[32,1,1]{2,1,0:T(1,128)S(1)} %broadcast_in_dim.18), channel_id=1, replica_groups=mesh['scan'=4,'slab'=32] {'slab'}, dimensions={0} | all-to-all | bytes 256 | tf_op jit(solution)/shard_map/all_to_all | solution.py:24
  150.0 0.6 reduce_sum.49
  152.0 0.9 multiply_add_fusion
  (45 shorter events, 7.5 us)
Async XLA Ops:
  1.7 5.1 %collective-permute-start = (bf16[48,2048]{1,0:T(8,128)(2,1)S(1)}, bf16[48,2048]{1,0:T(8,128)(2,1)S(1)}, u32[]{:S(2)}, u32[]{:S(2)}) collective-permute-start(bf16[48,2048]{1,0:T(8,128)(2,1)S(1)} %convert_element_type.6), channel_id=1, source_target_pairs={{0,1},{1,2},{2,3},{3,4},{4,5},{5,6},{6,7},{7,8},{8,9},{9,10},{10,1... | collective-permute-start | bytes 589832 | tf_op jit(solution)/shard_map/ppermute | solution.py:14
  3.0 5.6 %collective-permute-start.1 = (bf16[48,2048]{1,0:T(8,128)(2,1)S(1)}, bf16[48,2048]{1,0:T(8,128)(2,1)S(1)}, u32[]{:S(2)}, u32[]{:S(2)}) collective-permute-start(bf16[48,2048]{1,0:T(8,128)(2,1)S(1)} %convert_element_type.6), channel_id=1, source_target_pairs={{1,0},{2,1},{3,2},{4,3},{5,4},{6,5},{7,6},{8,7},{9,8},{10,9},{11,1... | collective-permute-start | bytes 589832 | tf_op jit(solution)/shard_map/ppermute | solution.py:17
  56.2 19.2 %all-to-all-start = ((f32[32,1,2]{2,1,0:T(1,128)}), f32[32,1,2]{2,1,0:T(1,128)S(1)}, u32[]{:S(2)}, u32[]{:S(2)}) async-start(f32[32,1,2]{2,1,0:T(1,128)} %broadcast_in_dim.16), calls=%async_computation | async-start | bytes 32768 | tf_op jit(solution)/shard_map/all_to_all | solution.py:24
  79.7 2.0 %copy-start = (f32[16,64,896]{2,1,0:T(8,128)S(1)}, f32[16,64,896]{2,1,0:T(8,128)}, u32[]{:S(2)}) copy-start(f32[16,64,896]{2,1,0:T(8,128)} %param.9) | copy-start | bytes 11010052
  108.8 43.2 %copy-start.1 = (f32[48,2048]{1,0:T(8,128)S(1)}, f32[48,2048]{1,0:T(8,128)}, u32[]{:S(2)}) copy-start(f32[48,2048]{1,0:T(8,128)} %param.7) | copy-start | bytes 1179652
  108.8 43.2 %copy-start.3 = (f32[48,2048]{1,0:T(8,128)S(1)}, f32[48,2048]{1,0:T(8,128)}, u32[]{:S(2)}) copy-start(f32[48,2048]{1,0:T(8,128)} %param.6) | copy-start | bytes 1179652
  123.9 4.4 %collective-permute-start.2 = (f32[48,2048]{1,0:T(8,128)S(1)}, f32[48,2048]{1,0:T(8,128)S(1)}, u32[]{:S(2)}, u32[]{:S(2)}) collective-permute-start(f32[48,2048]{1,0:T(8,128)S(1)} %get-tuple-element.24), channel_id=1, source_target_pairs={{1,0},{2,1},{3,2},{4,3},{5,4},{6,5},{7,6},{8,7},{9,8},{10,9},{11,1... | collective-permute-start | bytes 1179656 | tf_op jit(solution)/shard_map/ppermute | solution.py:43
  125.2 4.4 %collective-permute-start.3 = (f32[48,2048]{1,0:T(8,128)S(1)}, f32[48,2048]{1,0:T(8,128)S(1)}, u32[]{:S(2)}, u32[]{:S(2)}) collective-permute-start(f32[48,2048]{1,0:T(8,128)S(1)} %get-tuple-element.25), channel_id=1, source_target_pairs={{0,1},{1,2},{2,3},{3,4},{4,5},{5,6},{6,7},{7,8},{8,9},{9,10},{10,1... | collective-permute-start | bytes 1179656 | tf_op jit(solution)/shard_map/ppermute | solution.py:43
  130.3 22.7 %copy-start.2 = (f32[48,2048]{1,0:T(8,128)}, f32[48,2048]{1,0:T(8,128)S(1)}, u32[]{:S(2)}) copy-start(f32[48,2048]{1,0:T(8,128)S(1)} %get-tuple-element.21) | copy-start | bytes 1179652
where the time goes:
time: 154 us; the launch traced here: 153 us
  local copies, waits for them, and re-layouts  43.9 us (29%)
  matrix products  30.1 us (20%)
  other arithmetic  27.2 us (18%)
  starting transfers between devices  19.1 us (12%)
  blocking collectives  19.1 us (12%)
  waiting for transfers between devices  10.1 us (7%)
  between operations  3.46 us (2%)
    gather x48, local copies, waits for them, and re-layouts  32.2 us
    all_to_all x1, blocking collectives, sent_to_all(): return lax.all_to_all(copies, axis, split_axis=0, concat_axis=0, tiled=True)  19.1 us
    dot_general x1, matrix products, backproject(): jnp.einsum('gkic,krc->gkir', grouped, tiles, preferred_element_type=jnp.f...  16.7 us
    scatter-add x1, other arithmetic, backproject(): return accumulated.at[target_rows].add(contribution)  15 us
    dot_general x1, matrix products, project(): jnp.einsum('gkir,krc->gkic', grouped, tiles, preferred_element_type=jnp.f...  13.4 us
    all_to_all x1, starting transfers between devices, sent_to_all(): return lax.all_to_all(copies, axis, split_axis=0, concat_axis=0, tiled=True)  12.1 us
    transpose x1, local copies, waits for them, and re-layouts, backproject(): jnp.einsum('gkic,krc->gkir', grouped, tiles, preferred_element_type=jnp.f...  7.7 us
    all_to_all x1, waiting for transfers between devices, sent_to_all(): return lax.all_to_all(copies, axis, split_axis=0, concat_axis=0, tiled=True)  7.09 us
  transfers between devices with their start and end apart: 5, of which 3 were waited for; matrix products, arithmetic and copies ran while one was open for 2% of the time, Pallas kernels for 0%

commit v1 on v0

v1 whole, which is shorter than its diff:
```python
import jax
import jax.numpy as jnp
from jax import lax
from jax.experimental import pallas as pl
from jax.experimental.pallas import tpu as pltpu
from jax.sharding import PartitionSpec as P

ANGLES = 4
LANES = 128
F32 = jnp.float32
BF16 = jnp.bfloat16
MIB = 1 << 20


def first_plane(offsets, v, slab_rows):
    return offsets[v] - lax.axis_index("slab") * slab_rows + slab_rows


def pair_is_above():
    return lax.rem(lax.axis_index("slab"), 2) == 0


def split(x):
    high = x.astype(BF16)
    return high, (x - high.astype(F32)).astype(BF16)


def lane_sums(x):
    total = x[:, :LANES]
    for j in range(1, x.shape[1] // LANES):
        total = total + x[:, j * LANES : (j + 1) * LANES]
    return jnp.sum(total, axis=0, keepdims=True)


def backproject_residual(offsets, residual_hbm, tiles_hbm, tiles, own, to_pair, to_cross,
                         residual, rows, acc, residual_sem, tiles_sem):
    views, detector_rows, columns = residual.shape
    slab_rows, cells = own.shape[0], tiles.shape[1]
    near = 3 * slab_rows
    blocks = columns // LANES
    parts = 2
    part_cells = cells // parts

    def residual_copy(v):
        return pltpu.make_async_copy(residual_hbm.at[v], residual.at[v], residual_sem.at[v])

    def tile_copy(a, h):
        cut = pl.ds(h * part_cells, part_cells)
        return pltpu.make_async_copy(
            tiles_hbm.at[a, cut], tiles.at[a, cut], tiles_sem.at[a * parts + h]
        )

    order = [g * ANGLES + a for a in range(ANGLES) for g in range(views // ANGLES)]
    for v in order:
        residual_copy(v).start()
    for a in range(ANGLES):
        for h in range(parts):
            tile_copy(a, h).start()

    rows[...] = jnp.zeros_like(rows)
    plane = lax.broadcasted_iota(jnp.int32, (near, LANES), 0)
    lane = lax.broadcasted_iota(jnp.int32, (near, LANES), 1)
    counts = jnp.zeros((near, LANES), F32)
    for v in range(views):
        first = first_plane(offsets, v, slab_rows)
        seen = (plane >= first) & (plane < first + detector_rows) & (lane == v % ANGLES)
        counts = counts + seen.astype(F32)
    acc[:, cells:] = counts

    for a in range(ANGLES):
        for g in range(views // ANGLES):
            v = g * ANGLES + a
            first = first_plane(offsets, v, slab_rows)
            residual_copy(v).wait()
            for j in range(blocks):
                rows[j, pl.ds(first, detector_rows), :] += residual[
                    v, :, j * LANES : (j + 1) * LANES
                ]
        summed = jnp.concatenate([rows[j] for j in range(blocks)], axis=1)
        if a + 1 < ANGLES:
            rows[...] = jnp.zeros_like(rows)
        both = jnp.concatenate(split(summed), axis=0)
        for h in range(parts):
            tile_copy(a, h).wait()
            for b in range(h * part_cells, (h + 1) * part_cells, 512):
                part = lax.dot_general(
                    both, tiles[a, b : b + 512, :], (((1,), (1,)), ((), ())),
                    preferred_element_type=F32,
                )
                part = part[:near] + part[near:]
                if a == 0:
                    acc[:, b : b + 512] = part
                else:
                    acc[:, b : b + 512] += part

    own[...] = acc[slab_rows : 2 * slab_rows, :]
    above = pair_is_above()
    pair_row = pl.multiple_of(jnp.where(above, 2 * slab_rows, 0), 16)
    cross_row = pl.multiple_of(jnp.where(above, 0, 2 * slab_rows), 16)
    to_pair[...] = acc[pl.ds(pair_row, slab_rows), :].astype(BF16)
    to_cross[...] = acc[pl.ds(cross_row, slab_rows), :].astype(BF16)


def project_planes(direction, from_pair, from_cross, gradient, tiles, planes, back, squares,
                   grad_sums, near):
    slab_rows = direction.shape[0]
    columns = tiles.shape[2]
    above = pair_is_above()
    pair_row = pl.multiple_of(jnp.where(above, 2 * slab_rows, 0), 16)
    cross_row = pl.multiple_of(jnp.where(above, 0, 2 * slab_rows), 16)
    near[pl.ds(slab_rows, slab_rows), :] = direction[...].astype(BF16)
    near[pl.ds(pair_row, slab_rows), :] = from_pair[...].astype(BF16)
    near[pl.ds(cross_row, slab_rows), :] = from_cross[...].astype(BF16)
    grad_sums[...] = lane_sums(gradient[...] * gradient[...])
    for a in range(ANGLES):
        image = jnp.dot(near[...], tiles[a], preferred_element_type=F32)
        total = None
        for j in range(columns // LANES):
            block = image[:, j * LANES : (j + 1) * LANES]
            planes[a, j] = block
            mine = block[slab_rows : 2 * slab_rows]
            total = mine * mine if total is None else total + mine * mine
        squares[a] = total
        both = jnp.concatenate(split(image[slab_rows : 2 * slab_rows]), axis=0)
        for b in range(0, tiles.shape[1], 512):
            part = lax.dot_general(
                both, tiles[a, b : b + 512, :], (((1,), (1,)), ((), ())),
                preferred_element_type=F32,
            )
            back[a, :, b : b + 512] = part[:slab_rows] + part[slab_rows:]


def combine(own, from_pair, from_cross, back, squares, grad_sums, residual_part, image_part, sums):
    cells = residual_part.shape[1]
    counts = own[:, cells:] + from_pair[:, cells:].astype(F32) + from_cross[:, cells:].astype(F32)
    zero = jnp.zeros((1, LANES), F32)
    rr, ri, ii = zero, zero, zero
    weights = [counts[:, a : a + 1] for a in range(ANGLES)]
    for b in range(0, cells, 512):
        cut = slice(b, b + 512)
        r = own[:, cut] + from_pair[:, cut].astype(F32) + from_cross[:, cut].astype(F32)
        i = weights[0] * back[0, :, cut]
        for a in range(1, ANGLES):
            i = i + weights[a] * back[a, :, cut]
        residual_part[:, cut] = r
        image_part[:, cut] = i
        rr, ri, ii = rr + lane_sums(r * r), ri + lane_sums(r * i), ii + lane_sums(i * i)
    image_norm = weights[0] * squares[0]
    for a in range(1, ANGLES):
        image_norm = image_norm + weights[a] * squares[a]
    sums[...] = jnp.concatenate(
        [grad_sums[...], lane_sums(image_norm), rr, ri, ii, zero, zero, zero], axis=0
    )


def finish(offsets, sums, solution, direction, residual_part, image_part, planes, residual,
           solution_next, residual_hbm, gradient_next, direction_next, updated, sem):
    views, detector_rows, columns = residual.shape
    slab_rows = solution.shape[0]
    total = jnp.sum(sums[...], axis=1, keepdims=True)
    grad_norm, image_norm = total[0:1], total[1:2]
    step = grad_norm / image_norm
    new_norm = total[2:3] - 2.0 * step * total[3:4] + step * step * total[4:5]
    beta = new_norm / grad_norm

    def out_copy(v):
        return pltpu.make_async_copy(updated.at[v], residual_hbm.at[v], sem.at[v])

    for v in range(views):
        first = first_plane(offsets, v, slab_rows)
        for j in range(columns // LANES):
            cut = slice(j * LANES, (j + 1) * LANES)
            updated[v, :, cut] = (
                residual[v, :, cut] - step * planes[v % ANGLES, j, pl.ds(first, detector_rows), :]
            )
        out_copy(v).start()
    gradient = residual_part[...] - step * image_part[...]
    gradient_next[...] = gradient
    solution_next[...] = solution[...] + step * direction[...]
    direction_next[...] = gradient + beta * direction[...]
    for v in range(views):
        out_copy(v).wait()


def summed_over_slabs(x):
    count = lax.axis_size("slab")
    for mask in (1, 2, 4, 8, 16):
        x = x + lax.ppermute(x, "slab", [(i, i ^ mask) for i in range(count)])
    return x


def local(solution, direction, gradient, residual, tiles, offsets):
    slab_rows, cells = solution.shape
    views, detector_rows, columns = residual.shape
    near = 3 * slab_rows
    blocks = columns // LANES
    count = lax.axis_size("slab")
    pair = [(i, i ^ 1) for i in range(count)]
    cross = [(i, i + 1) for i in range(1, count - 1, 2)]
    cross = cross + [(i, j) for j, i in cross]

    vmem = pl.BlockSpec(memory_space=pltpu.VMEM)
    smem = pl.BlockSpec(memory_space=pltpu.SMEM)
    anywhere = pl.BlockSpec(memory_space=pl.ANY)
    sds = jax.ShapeDtypeStruct

    direction_pair = lax.ppermute(direction, "slab", pair)
    direction_cross = lax.ppermute(direction, "slab", cross)

    wide = cells + LANES
    tiles_here, own, to_pair, to_cross, residual_here = pl.pallas_call(
        backproject_residual,
        name="backproject_residual",
        in_specs=[smem, anywhere, anywhere],
        out_specs=[vmem] * 5,
        out_shape=[
            pltpu.VMEM(tiles.shape, BF16),
            sds((slab_rows, wide), F32),
            sds((slab_rows, wide), BF16),
            sds((slab_rows, wide), BF16),
            pltpu.VMEM(residual.shape, F32),
        ],
        scratch_shapes=[
            pltpu.VMEM((blocks, near, LANES), F32),
            pltpu.VMEM((near, wide), F32),
            pltpu.SemaphoreType.DMA((views,)),
            pltpu.SemaphoreType.DMA((ANGLES * 2,)),
        ],
        compiler_params=pltpu.CompilerParams(vmem_limit_bytes=40 * MIB),
        cost_estimate=pl.CostEstimate(
            flops=4 * near * cells * columns * ANGLES, bytes_accessed=20 * MIB, transcendentals=0
        ),
    )(offsets, residual, tiles)

    from_pair = lax.ppermute(to_pair, "slab", pair)
    from_cross = lax.ppermute(to_cross, "slab", cross)

    planes, back, squares, grad_sums = pl.pallas_call(
        project_planes,
        name="project_planes",
        in_specs=[vmem] * 5,
        out_specs=[vmem] * 4,
        out_shape=[
            sds((ANGLES, blocks, near, LANES), F32),
            sds((ANGLES, slab_rows, cells), F32),
            sds((ANGLES, slab_rows, LANES), F32),
            sds((1, LANES), F32),
        ],
        scratch_shapes=[pltpu.VMEM((near, cells), BF16)],
        compiler_params=pltpu.CompilerParams(vmem_limit_bytes=40 * MIB),
        cost_estimate=pl.CostEstimate(
            flops=5 * near * cells * columns * ANGLES, bytes_accessed=4 * MIB, transcendentals=0
        ),
    )(direction, direction_pair, direction_cross, gradient, tiles_here)

    residual_part, image_part, sums = pl.pallas_call(
        combine,
        name="combine",
        in_specs=[vmem] * 6,
        out_specs=[vmem] * 3,
        out_shape=[
            sds((slab_rows, cells), F32),
            sds((slab_rows, cells), F32),
            sds((8, LANES), F32),
        ],
        compiler_params=pltpu.CompilerParams(vmem_limit_bytes=24 * MIB),
    )(own, from_pair, from_cross, back, squares, grad_sums)

    sums = summed_over_slabs(sums)

    return pl.pallas_call(
        finish,
        name="finish",
        in_specs=[smem] + [vmem] * 7,
        out_specs=[vmem, anywhere, vmem, vmem],
        out_shape=[
            sds(solution.shape, F32),
            sds(residual.shape, F32),
            sds(solution.shape, F32),
            sds(solution.shape, F32),
        ],
        scratch_shapes=[
            pltpu.VMEM(residual.shape, F32),
            pltpu.SemaphoreType.DMA((views,)),
        ],
        compiler_params=pltpu.CompilerParams(vmem_limit_bytes=32 * MIB),
    )(offsets, sums, solution, direction, residual_part, image_part, planes, residual_here)


def solution(mesh):
    placed = (
        P(("scan", "slab"), None),
        P(("scan", "slab"), None),
        P(("scan", "slab"), None),
        P(("scan", "slab"), None, None),
        P(),
        P(("scan", "slab")),
    )
    return jax.shard_map(
        local,
        mesh=mesh,
        in_specs=placed,
        out_specs=(
            P(("scan", "slab"), None),
            P(("scan", "slab"), None, None),
            P(("scan", "slab"), None),
            P(("scan", "slab"), None),
        ),
        check_vma=False,
    )
```

time: 154 us -> 60.3 us (0.39)
  local copies, waits for them, and re-layouts: 43.9 us -> 5.22 us
  matrix products: 30.1 us -> 0 us
  other arithmetic: 27.2 us -> 0.02 us
  Pallas kernels: 0 us -> 26.9 us
  blocking collectives: 19.1 us -> 0 us
  between operations: 3.46 us -> 0.78 us
  waiting for transfers between devices: 10.1 us -> 7.57 us
    gather x48 -> x0, local copies, waits for them, and re-layouts: 32.2 us -> none
    dot_general x2 -> x0, matrix products: 30.1 us -> none  [the longest x1 16.7 us: backproject(): jnp.einsum('gkic,krc->gkir', grouped, tiles, preferred_element_type=jnp.f...]
    pallas_call x0 -> x4, Pallas kernels: none -> 26.9 us  [the longest x1 12.4 us: local(): pl.pallas_call(project_planes, name='project_planes', in_specs=[vmem] * 5...]
    all_to_all x1 -> x0, blocking collectives: 19.1 us -> none  [sent_to_all(): return lax.all_to_all(copies, axis, split_axis=0, concat_axis=0, tiled=True)]
    scatter-add x1 -> x0, other arithmetic: 15 us -> none  [backproject(): return accumulated.at[target_rows].add(contribution)]
    all_to_all x1 -> x0, starting transfers between devices: 12.1 us -> none  [sent_to_all(): return lax.all_to_all(copies, axis, split_axis=0, concat_axis=0, tiled=True)]
    ppermute x4 -> x9, starting transfers between devices: 6.94 us -> 19 us  [the longest x5 14.1 us: summed_over_slabs(): x = x + lax.ppermute(x, 'slab', [(i, i ^ mask) for i in range(count)])]
    transpose x1 -> x0, local copies, waits for them, and re-layouts: 7.7 us -> none  [backproject(): jnp.einsum('gkic,krc->gkir', grouped, tiles, preferred_element_type=jnp.f...]
  transfers between devices with their start and end apart: 5 -> 9, of which waited for: 3 -> 5; matrix products, arithmetic and copies ran while one was open for 2% -> 0% of each run, Pallas kernels for 0% -> 39%
where the time goes in v1:
time: 60.3 us; the launch traced here: 59.6 us
  Pallas kernels  26.9 us (45%)
  starting transfers between devices  19 us (32%)
  waiting for transfers between devices  7.57 us (13%)
  local copies, waits for them, and re-layouts  5.22 us (9%)
  between operations  0.78 us (1%)
    ppermute x5, starting transfers between devices, summed_over_slabs(): x = x + lax.ppermute(x, 'slab', [(i, i ^ mask) for i in range(count)])  14.1 us
    pallas_call x1, Pallas kernels, local(): pl.pallas_call(project_planes, name='project_planes', in_specs=[vmem] * 5...  12.4 us
    pallas_call x1, Pallas kernels, local(): pl.pallas_call(backproject_residual, name='backproject_residual', in_spec...  10.6 us
    ppermute x5, waiting for transfers between devices, summed_over_slabs(): x = x + lax.ppermute(x, 'slab', [(i, i ^ mask) for i in range(count)])  7.56 us
    unnamed x12, local copies, waits for them, and re-layouts  5.22 us
    pallas_call x1, Pallas kernels, local(): pl.pallas_call(finish, name='finish', in_specs=[smem] + [vmem] * 7, out_s...  3.67 us
    ppermute x1, starting transfers between devices, local(): direction_pair = lax.ppermute(direction, 'slab', pair)  3.42 us
  transfers between devices with their start and end apart: 9, of which 5 were waited for; matrix products, arithmetic and copies ran while one was open for 0% of the time, Pallas kernels for 39%

profile of v1, /device:TPU:0, one launch (start us, length us, event | category | flops | bytes accessed | tf_op | source)
XLA Modules:
  0.0 59.6 jit_solution(8963115111440469961)
XLA Ops:
  0.6 0.0 copy-start.1
  0.6 0.0 copy-start.5
  0.7 0.8 %collective-permute-start.3 = (f32[48,2048]{1,0:T(8,128)}, f32[48,2048]{1,0:T(8,128)S(1)}, u32[]{:S(2)}, u32[]{:S(2)}) collective-permute-start(f32[48,2048]{1,0:T(8,128)} %direction.3), channel_id=1, source_target_pairs={{1,2},{3,4},{5,6},{7,8},{9,10},{11,12},{13,14},{15,16},{17,18},{19... | collective-permute-start | bytes 1179656 | tf_op jit(solution)/shard_map/ppermute | solution.py:208
  1.5 3.4 %collective-permute-start.2 = (f32[48,2048]{1,0:T(8,128)}, f32[48,2048]{1,0:T(8,128)S(1)}, u32[]{:S(2)}, u32[]{:S(2)}) collective-permute-start(f32[48,2048]{1,0:T(8,128)} %direction.3), channel_id=1, source_target_pairs={{0,1},{1,0},{2,3},{3,2},{4,5},{5,4},{6,7},{7,6},{8,9},{9,8},{10,11... | collective-permute-start | bytes 1179656 | tf_op jit(solution)/shard_map/ppermute | solution.py:207
  4.9 10.6 %backproject_residual.1 = (bf16[4,2048,896]{2,1,0:T(8,128)(2,1)S(1)}, f32[48,2176]{1,0:T(8,128)}, bf16[48,2176]{1,0:T(8,128)(2,1)}, bf16[48,2176]{1,0:T(8,128)(2,1)}, f32[16,64,896]{2,1,0:T(8,128)S(1)}) custom-call(s32[16]{0:T(128)} %offsets.3, f32[16,64,896]{2,1,0:T(8,128)} %residual_hbm.1, bf16[4,2048,896]{2,1,0:T(8,128)(2,1)} %tiles_hbm.1), custom_call_target="tpu_custom_call" | custom-call | flops 4227858432 | bytes 20971520 | tf_op jit(solution)/shard_map/backproject_residual/pallas_call | solution.py:211
  15.5 0.0 copy-start.4
  15.5 5.2 %copy-done.4 = bf16[4,2048,896]{2,1,0:T(8,128)(2,1)} copy-done((bf16[4,2048,896]{2,1,0:T(8,128)(2,1)}, bf16[4,2048,896]{2,1,0:T(8,128)(2,1)S(1)}, u32[]{:S(2)}) %copy-start.4) | copy-done | bytes 14680088
  20.7 0.0 collective-permute-start
  20.7 0.7 %collective-permute-start.1 = (bf16[48,2176]{1,0:T(8,128)(2,1)}, bf16[48,2176]{1,0:T(8,128)(2,1)S(1)}, u32[]{:S(2)}, u32[]{:S(2)}) collective-permute-start(bf16[48,2176]{1,0:T(8,128)(2,1)} %get-tuple-element.18), channel_id=1, source_target_pairs={{1,2},{3,4},{5,6},{7,8},{9,10},{11,12},{13,14},{15,16},{17,18},{19... | collective-permute-start | bytes 626696 | tf_op jit(solution)/shard_map/ppermute | solution.py:236
  21.4 0.0 collective-permute-done.3.from_cross
  21.4 0.0 collective-permute-done.2.from_pair
  21.4 0.0 copy-done.1
  21.4 0.0 copy-done.5
  21.4 0.0 copy-start
  21.4 0.0 copy-start.2
  21.4 0.0 copy-start.3
  21.4 12.4 %project_planes.1 = (f32[4,7,144,128]{3,2,1,0:T(8,128)S(1)}, f32[4,48,2048]{2,1,0:T(8,128)S(1)}, f32[4,48,128]{2,1,0:T(8,128)S(1)}, f32[1,128]{1,0:T(1,128)S(1)}) custom-call(f32[48,2048]{1,0:T(8,128)S(1)} %copy-done.1, f32[48,2048]{1,0:T(8,128)S(1)} %collective-permute-done.2.from_pair, f32[48,2048]{1,0:T(8,128)S(1)} %collective-permute-done.3.from_cross, ...), custom_call_target="tpu_custom_call" | custom-call | flops 5284823040 | bytes 4194304 | tf_op jit(solution)/shard_map/project_planes/pallas_call | solution.py:238
  33.8 0.0 collective-permute-done.from_pair
  33.8 0.0 collective-permute-done.1.from_cross
  33.8 0.0 copy-done
  33.9 0.3 combine.1
  34.2 3.3 %collective-permute-start.4 = (f32[8,128]{1,0:T(8,128)S(1)}, f32[8,128]{1,0:T(8,128)S(1)}, u32[]{:S(2)}, u32[]{:S(2)}) collective-permute-start(f32[8,128]{1,0:T(8,128)S(1)} %get-tuple-element.23), channel_id=1, source_target_pairs={{0,1},{1,0},{2,3},{3,2},{4,5},{5,4},{6,7},{7,6},{8,9},{9,8},{10,11... | collective-permute-start | bytes 12296 | tf_op jit(solution)/shard_map/ppermute | solution.py:188
  37.5 0.8 %collective-permute-done.4 = f32[8,128]{1,0:T(8,128)S(1)} collective-permute-done((f32[8,128]{1,0:T(8,128)S(1)}, f32[8,128]{1,0:T(8,128)S(1)}, u32[]{:S(2)}, u32[]{:S(2)}) %collective-permute-start.4) | collective-permute-done | bytes 4128 | tf_op jit(solution)/shard_map/ppermute | solution.py:188
  38.3 1.6 %collective-permute-start.5 = (f32[8,128]{1,0:T(8,128)S(1)}, f32[8,128]{1,0:T(8,128)S(1)}, u32[]{:S(2)}, u32[]{:S(2)}) collective-permute-start(f32[8,128]{1,0:T(8,128)S(1)} %add.15), channel_id=1, source_target_pairs={{0,2},{1,3},{2,0},{3,1},{4,6},{5,7},{6,4},{7,5},{8,10},{9,11},{10,... | collective-permute-start | bytes 12296 | tf_op jit(solution)/shard_map/ppermute | solution.py:188
  40.0 2.0 %collective-permute-done.5 = f32[8,128]{1,0:T(8,128)S(1)} collective-permute-done((f32[8,128]{1,0:T(8,128)S(1)}, f32[8,128]{1,0:T(8,128)S(1)}, u32[]{:S(2)}, u32[]{:S(2)}) %collective-permute-start.5) | collective-permute-done | bytes 4128 | tf_op jit(solution)/shard_map/ppermute | solution.py:188
  42.0 3.6 %collective-permute-start.6 = (f32[8,128]{1,0:T(8,128)S(1)}, f32[8,128]{1,0:T(8,128)S(1)}, u32[]{:S(2)}, u32[]{:S(2)}) collective-permute-start(f32[8,128]{1,0:T(8,128)S(1)} %add.16), channel_id=1, source_target_pairs={{0,4},{1,5},{2,6},{3,7},{4,0},{5,1},{6,2},{7,3},{8,12},{9,13},{10,... | collective-permute-start | bytes 12296 | tf_op jit(solution)/shard_map/ppermute | solution.py:188
  45.6 1.6 %collective-permute-done.6 = f32[8,128]{1,0:T(8,128)S(1)} collective-permute-done((f32[8,128]{1,0:T(8,128)S(1)}, f32[8,128]{1,0:T(8,128)S(1)}, u32[]{:S(2)}, u32[]{:S(2)}) %collective-permute-start.6) | collective-permute-done | bytes 4128 | tf_op jit(solution)/shard_map/ppermute | solution.py:188
  47.2 2.0 %collective-permute-start.7 = (f32[8,128]{1,0:T(8,128)S(1)}, f32[8,128]{1,0:T(8,128)S(1)}, u32[]{:S(2)}, u32[]{:S(2)}) collective-permute-start(f32[8,128]{1,0:T(8,128)S(1)} %add.17), channel_id=1, source_target_pairs={{0,8},{1,9},{2,10},{3,11},{4,12},{5,13},{6,14},{7,15},{8,0},{9,1},... | collective-permute-start | bytes 12296 | tf_op jit(solution)/shard_map/ppermute | solution.py:188
  49.2 1.6 %collective-permute-done.7 = f32[8,128]{1,0:T(8,128)S(1)} collective-permute-done((f32[8,128]{1,0:T(8,128)S(1)}, f32[8,128]{1,0:T(8,128)S(1)}, u32[]{:S(2)}, u32[]{:S(2)}) %collective-permute-start.7) | collective-permute-done | bytes 4128 | tf_op jit(solution)/shard_map/ppermute | solution.py:188
  50.8 3.5 %collective-permute-start.8 = (f32[8,128]{1,0:T(8,128)S(1)}, f32[8,128]{1,0:T(8,128)S(1)}, u32[]{:S(2)}, u32[]{:S(2)}) collective-permute-start(f32[8,128]{1,0:T(8,128)S(1)} %add.18), channel_id=1, source_target_pairs={{0,16},{1,17},{2,18},{3,19},{4,20},{5,21},{6,22},{7,23},{8,24},{9,... | collective-permute-start | bytes 12296 | tf_op jit(solution)/shard_map/ppermute | solution.py:188
  54.3 1.6 %collective-permute-done.8 = f32[8,128]{1,0:T(8,128)S(1)} collective-permute-done((f32[8,128]{1,0:T(8,128)S(1)}, f32[8,128]{1,0:T(8,128)S(1)}, u32[]{:S(2)}, u32[]{:S(2)}) %collective-permute-start.8) | collective-permute-done | bytes 4128 | tf_op jit(solution)/shard_map/ppermute | solution.py:188
  55.9 0.0 copy-done.2
  55.9 0.0 copy-done.3
  55.9 3.7 %finish.1 = (f32[48,2048]{1,0:T(8,128)}, f32[16,64,896]{2,1,0:T(8,128)}, f32[48,2048]{1,0:T(8,128)}, f32[48,2048]{1,0:T(8,128)}) custom-call(s32[16]{0:T(128)S(1)} %copy-done.3, f32[8,128]{1,0:T(8,128)S(1)} %add.19.sums, f32[48,2048]{1,0:T(8,128)S(1)} %copy-done.2, f32[48,2048]{1,0:T(8,128)S(1)} %copy-done.1, ...), custom_call_target="tpu_custom_call" | custom-call | tf_op jit(solution)/shard_map/finish/pallas_call | solution.py:271
  (5 shorter events, 0.0 us)
Async XLA Ops:
  0.6 20.8 %copy-start.1 = (f32[48,2048]{1,0:T(8,128)S(1)}, f32[48,2048]{1,0:T(8,128)}, u32[]{:S(2)}) copy-start(f32[48,2048]{1,0:T(8,128)} %direction.3) | copy-start | bytes 1179652
  0.6 20.8 %copy-start.5 = (f32[48,2048]{1,0:T(8,128)S(1)}, f32[48,2048]{1,0:T(8,128)}, u32[]{:S(2)}) copy-start(f32[48,2048]{1,0:T(8,128)} %gradient.1) | copy-start | bytes 1179652
  0.7 20.7 %collective-permute-start.3 = (f32[48,2048]{1,0:T(8,128)}, f32[48,2048]{1,0:T(8,128)S(1)}, u32[]{:S(2)}, u32[]{:S(2)}) collective-permute-start(f32[48,2048]{1,0:T(8,128)} %direction.3), channel_id=1, source_target_pairs={{1,2},{3,4},{5,6},{7,8},{9,10},{11,12},{13,14},{15,16},{17,18},{19... | collective-permute-start | bytes 1179656 | tf_op jit(solution)/shard_map/ppermute | solution.py:208
  1.5 19.9 %collective-permute-start.2 = (f32[48,2048]{1,0:T(8,128)}, f32[48,2048]{1,0:T(8,128)S(1)}, u32[]{:S(2)}, u32[]{:S(2)}) collective-permute-start(f32[48,2048]{1,0:T(8,128)} %direction.3), channel_id=1, source_target_pairs={{0,1},{1,0},{2,3},{3,2},{4,5},{5,4},{6,7},{7,6},{8,9},{9,8},{10,11... | collective-permute-start | bytes 1179656 | tf_op jit(solution)/shard_map/ppermute | solution.py:207
  15.5 5.2 %copy-start.4 = (bf16[4,2048,896]{2,1,0:T(8,128)(2,1)}, bf16[4,2048,896]{2,1,0:T(8,128)(2,1)S(1)}, u32[]{:S(2)}) copy-start(bf16[4,2048,896]{2,1,0:T(8,128)(2,1)S(1)} %get-tuple-element.19.tiles) | copy-start | bytes 44040196
  20.7 13.1 %collective-permute-start = (bf16[48,2176]{1,0:T(8,128)(2,1)}, bf16[48,2176]{1,0:T(8,128)(2,1)S(1)}, u32[]{:S(2)}, u32[]{:S(2)}) collective-permute-start(bf16[48,2176]{1,0:T(8,128)(2,1)} %get-tuple-element.17), channel_id=1, source_target_pairs={{0,1},{1,0},{2,3},{3,2},{4,5},{5,4},{6,7},{7,6},{8,9},{9,8},{10,11... | collective-permute-start | bytes 626696 | tf_op jit(solution)/shard_map/ppermute | solution.py:235
  20.7 13.1 %collective-permute-start.1 = (bf16[48,2176]{1,0:T(8,128)(2,1)}, bf16[48,2176]{1,0:T(8,128)(2,1)S(1)}, u32[]{:S(2)}, u32[]{:S(2)}) collective-permute-start(bf16[48,2176]{1,0:T(8,128)(2,1)} %get-tuple-element.18), channel_id=1, source_target_pairs={{1,2},{3,4},{5,6},{7,8},{9,10},{11,12},{13,14},{15,16},{17,18},{19... | collective-permute-start | bytes 626696 | tf_op jit(solution)/shard_map/ppermute | solution.py:236
  21.4 12.4 %copy-start = (f32[48,2176]{1,0:T(8,128)S(1)}, f32[48,2176]{1,0:T(8,128)}, u32[]{:S(2)}) copy-start(f32[48,2176]{1,0:T(8,128)} %get-tuple-element.16.own) | copy-start | bytes 1253380
  21.4 34.5 %copy-start.2 = (f32[48,2048]{1,0:T(8,128)S(1)}, f32[48,2048]{1,0:T(8,128)}, u32[]{:S(2)}) copy-start(f32[48,2048]{1,0:T(8,128)} %solution.1) | copy-start | bytes 1179652
  21.4 34.5 %copy-start.3 = (s32[16]{0:T(128)S(1)}, s32[16]{0:T(128)}, u32[]{:S(2)}) copy-start(s32[16]{0:T(128)} %offsets.3) | copy-start | bytes 196
  34.2 4.2 %collective-permute-start.4 = (f32[8,128]{1,0:T(8,128)S(1)}, f32[8,128]{1,0:T(8,128)S(1)}, u32[]{:S(2)}, u32[]{:S(2)}) collective-permute-start(f32[8,128]{1,0:T(8,128)S(1)} %get-tuple-element.23), channel_id=1, source_target_pairs={{0,1},{1,0},{2,3},{3,2},{4,5},{5,4},{6,7},{7,6},{8,9},{9,8},{10,11... | collective-permute-start | bytes 12296 | tf_op jit(solution)/shard_map/ppermute | solution.py:188
  38.3 3.6 %collective-permute-start.5 = (f32[8,128]{1,0:T(8,128)S(1)}, f32[8,128]{1,0:T(8,128)S(1)}, u32[]{:S(2)}, u32[]{:S(2)}) collective-permute-start(f32[8,128]{1,0:T(8,128)S(1)} %add.15), channel_id=1, source_target_pairs={{0,2},{1,3},{2,0},{3,1},{4,6},{5,7},{6,4},{7,5},{8,10},{9,11},{10,... | collective-permute-start | bytes 12296 | tf_op jit(solution)/shard_map/ppermute | solution.py:188
  42.0 5.2 %collective-permute-start.6 = (f32[8,128]{1,0:T(8,128)S(1)}, f32[8,128]{1,0:T(8,128)S(1)}, u32[]{:S(2)}, u32[]{:S(2)}) collective-permute-start(f32[8,128]{1,0:T(8,128)S(1)} %add.16), channel_id=1, source_target_pairs={{0,4},{1,5},{2,6},{3,7},{4,0},{5,1},{6,2},{7,3},{8,12},{9,13},{10,... | collective-permute-start | bytes 12296 | tf_op jit(solution)/shard_map/ppermute | solution.py:188
  47.2 3.6 %collective-permute-start.7 = (f32[8,128]{1,0:T(8,128)S(1)}, f32[8,128]{1,0:T(8,128)S(1)}, u32[]{:S(2)}, u32[]{:S(2)}) collective-permute-start(f32[8,128]{1,0:T(8,128)S(1)} %add.17), channel_id=1, source_target_pairs={{0,8},{1,9},{2,10},{3,11},{4,12},{5,13},{6,14},{7,15},{8,0},{9,1},... | collective-permute-start | bytes 12296 | tf_op jit(solution)/shard_map/ppermute | solution.py:188
  50.8 5.1 %collective-permute-start.8 = (f32[8,128]{1,0:T(8,128)S(1)}, f32[8,128]{1,0:T(8,128)S(1)}, u32[]{:S(2)}, u32[]{:S(2)}) collective-permute-start(f32[8,128]{1,0:T(8,128)S(1)} %add.18), channel_id=1, source_target_pairs={{0,16},{1,17},{2,18},{3,19},{4,20},{5,21},{6,22},{7,23},{8,24},{9,... | collective-permute-start | bytes 12296 | tf_op jit(solution)/shard_map/ppermute | solution.py:188

commit v2 on v1

--- a/solution.py
+++ b/solution.py
@@ -201,7 +201,7 @@
 
     vmem = pl.BlockSpec(memory_space=pltpu.VMEM)
     smem = pl.BlockSpec(memory_space=pltpu.SMEM)
-    anywhere = pl.BlockSpec(memory_space=pl.ANY)
+    hbm = pl.BlockSpec(memory_space=pltpu.HBM)
     sds = jax.ShapeDtypeStruct
 
     direction_pair = lax.ppermute(direction, "slab", pair)
@@ -211,7 +211,7 @@
     tiles_here, own, to_pair, to_cross, residual_here = pl.pallas_call(
         backproject_residual,
         name="backproject_residual",
-        in_specs=[smem, anywhere, anywhere],
+        in_specs=[smem, hbm, hbm],
         out_specs=[vmem] * 5,
         out_shape=[
             pltpu.VMEM(tiles.shape, BF16),
@@ -226,7 +226,7 @@
             pltpu.SemaphoreType.DMA((views,)),
             pltpu.SemaphoreType.DMA((ANGLES * 2,)),
         ],
-        compiler_params=pltpu.CompilerParams(vmem_limit_bytes=40 * MIB),
+        compiler_params=pltpu.CompilerParams(vmem_limit_bytes=20 * MIB),
         cost_estimate=pl.CostEstimate(
             flops=4 * near * cells * columns * ANGLES, bytes_accessed=20 * MIB, transcendentals=0
         ),
@@ -247,7 +247,7 @@
             sds((1, LANES), F32),
         ],
         scratch_shapes=[pltpu.VMEM((near, cells), BF16)],
-        compiler_params=pltpu.CompilerParams(vmem_limit_bytes=40 * MIB),
+        compiler_params=pltpu.CompilerParams(vmem_limit_bytes=12 * MIB),
         cost_estimate=pl.CostEstimate(
             flops=5 * near * cells * columns * ANGLES, bytes_accessed=4 * MIB, transcendentals=0
         ),
@@ -263,7 +263,7 @@
             sds((slab_rows, cells), F32),
             sds((8, LANES), F32),
         ],
-        compiler_params=pltpu.CompilerParams(vmem_limit_bytes=24 * MIB),
+        compiler_params=pltpu.CompilerParams(vmem_limit_bytes=8 * MIB),
     )(own, from_pair, from_cross, back, squares, grad_sums)
 
     sums = summed_over_slabs(sums)
@@ -272,7 +272,7 @@
         finish,
         name="finish",
         in_specs=[smem] + [vmem] * 7,
-        out_specs=[vmem, anywhere, vmem, vmem],
+        out_specs=[vmem, hbm, vmem, vmem],
         out_shape=[
             sds(solution.shape, F32),
             sds(residual.shape, F32),
@@ -283,7 +283,7 @@
             pltpu.VMEM(residual.shape, F32),
             pltpu.SemaphoreType.DMA((views,)),
         ],
-        compiler_params=pltpu.CompilerParams(vmem_limit_bytes=32 * MIB),
+        compiler_params=pltpu.CompilerParams(vmem_limit_bytes=12 * MIB),
     )(offsets, sums, solution, direction, residual_part, image_part, planes, residual_here)
 
 

time: 60.3 us -> 55.5 us (0.920)
  local copies, waits for them, and re-layouts: 5.22 us -> 2.71 us
  Pallas kernels: 26.9 us -> 24.8 us
    pallas_call x1, Pallas kernels: 12.4 us -> 7.18 us  [local(): pl.pallas_call(project_planes, name='project_planes', in_specs=[vmem] * 5...]
    pallas_call x1, Pallas kernels: 10.6 us -> 13.6 us  [local(): pl.pallas_call(backproject_residual, name='backproject_residual', in_spec...]
    unnamed x12, local copies, waits for them, and re-layouts: 5.22 us -> 2.71 us
  transfers between devices with their start and end apart: 9 -> 9, of which waited for: 5 -> 5; matrix products, arithmetic and copies ran while one was open for 0% -> 0% of each run, Pallas kernels for 39% -> 38%
where the time goes in v2:
time: 55.5 us; the launch traced here: 54.8 us
  Pallas kernels  24.8 us (45%)
  starting transfers between devices  19 us (34%)
  waiting for transfers between devices  7.6 us (14%)
  local copies, waits for them, and re-layouts  2.71 us (5%)
  between operations  0.75 us (1%)
    ppermute x5, starting transfers between devices, summed_over_slabs(): x = x + lax.ppermute(x, 'slab', [(i, i ^ mask) for i in range(count)])  14.1 us
    pallas_call x1, Pallas kernels, local(): pl.pallas_call(backproject_residual, name='backproject_residual', in_spec...  13.6 us
    ppermute x5, waiting for transfers between devices, summed_over_slabs(): x = x + lax.ppermute(x, 'slab', [(i, i ^ mask) for i in range(count)])  7.59 us
    pallas_call x1, Pallas kernels, local(): pl.pallas_call(project_planes, name='project_planes', in_specs=[vmem] * 5...  7.18 us
    pallas_call x1, Pallas kernels, local(): pl.pallas_call(finish, name='finish', in_specs=[smem] + [vmem] * 7, out_s...  3.67 us
    ppermute x1, starting transfers between devices, local(): direction_pair = lax.ppermute(direction, 'slab', pair)  3.42 us
    unnamed x12, local copies, waits for them, and re-layouts  2.71 us
  transfers between devices with their start and end apart: 9, of which 5 were waited for; matrix products, arithmetic and copies ran while one was open for 0% of the time, Pallas kernels for 38%

profile of v2, /device:TPU:0, one launch (start us, length us, event | category | flops | bytes accessed | tf_op | source)
XLA Modules:
  0.0 54.8 jit_solution(5074926046985984248)
XLA Ops:
  0.6 0.7 %collective-permute-start.3 = (f32[48,2048]{1,0:T(8,128)}, f32[48,2048]{1,0:T(8,128)S(1)}, u32[]{:S(2)}, u32[]{:S(2)}) collective-permute-start(f32[48,2048]{1,0:T(8,128)} %direction.3), channel_id=1, source_target_pairs={{1,2},{3,4},{5,6},{7,8},{9,10},{11,12},{13,14},{15,16},{17,18},{19... | collective-permute-start | bytes 1179656 | tf_op jit(solution)/shard_map/ppermute | solution.py:208
  1.3 3.4 %collective-permute-start.2 = (f32[48,2048]{1,0:T(8,128)}, f32[48,2048]{1,0:T(8,128)S(1)}, u32[]{:S(2)}, u32[]{:S(2)}) collective-permute-start(f32[48,2048]{1,0:T(8,128)} %direction.3), channel_id=1, source_target_pairs={{0,1},{1,0},{2,3},{3,2},{4,5},{5,4},{6,7},{7,6},{8,9},{9,8},{10,11... | collective-permute-start | bytes 1179656 | tf_op jit(solution)/shard_map/ppermute | solution.py:207
  4.7 0.0 copy-start
  4.7 2.0 %copy-done = f32[16,64,896]{2,1,0:T(8,128)S(1)} copy-done((f32[16,64,896]{2,1,0:T(8,128)S(1)}, f32[16,64,896]{2,1,0:T(8,128)}, u32[]{:S(2)}) %copy-start) | copy-done | bytes 3670040
  6.8 0.0 copy-start.3
  6.8 0.7 %copy-done.3 = s32[16]{0:T(128)S(1)} copy-done((s32[16]{0:T(128)S(1)}, s32[16]{0:T(128)}, u32[]{:S(2)}) %copy-start.3) | copy-done | bytes 88
  7.4 0.0 copy-start.1
  7.4 0.0 copy-start.5
  7.4 13.6 %backproject_residual.1 = (bf16[4,2048,896]{2,1,0:T(8,128)(2,1)S(1)}, f32[48,2176]{1,0:T(8,128)S(1)}, bf16[48,2176]{1,0:T(8,128)(2,1)S(1)}, bf16[48,2176]{1,0:T(8,128)(2,1)S(1)}, f32[16,64,896]{2,1,0:T(8,128)S(1)}) custom-call(s32[16]{0:T(128)S(1)} %copy-done.3, f32[16,64,896]{2,1,0:T(8,128)S(1)} %copy-done, bf16[4,2048,896]{2,1,0:T(8,128)(2,1)} %tiles_hbm.1), custom_call_target="tpu_custom_call" | custom-call | flops 4227858432 | bytes 20971520 | tf_op jit(solution)/shard_map/backproject_residual/pallas_call | solution.py:211
  21.0 0.1 collective-permute-start
  21.2 0.7 %collective-permute-start.1 = (bf16[48,2176]{1,0:T(8,128)(2,1)S(1)}, bf16[48,2176]{1,0:T(8,128)(2,1)S(1)}, u32[]{:S(2)}, u32[]{:S(2)}) collective-permute-start(bf16[48,2176]{1,0:T(8,128)(2,1)S(1)} %get-tuple-element.18), channel_id=1, source_target_pairs={{1,2},{3,4},{5,6},{7,8},{9,10},{11,12},{13,14},{15,16},{17,18},{19... | collective-permute-start | bytes 626696 | tf_op jit(solution)/shard_map/ppermute | solution.py:236
  21.8 0.0 collective-permute-done.3.from_cross
  21.8 0.0 collective-permute-done.2.from_pair
  21.8 0.0 copy-done.1
  21.9 0.0 copy-done.5
  21.9 0.0 copy-start.2
  21.9 0.0 copy-start.4
  21.9 7.2 %project_planes.1 = (f32[4,7,144,128]{3,2,1,0:T(8,128)S(1)}, f32[4,48,2048]{2,1,0:T(8,128)S(1)}, f32[4,48,128]{2,1,0:T(8,128)S(1)}, f32[1,128]{1,0:T(1,128)S(1)}) custom-call(f32[48,2048]{1,0:T(8,128)S(1)} %copy-done.1, f32[48,2048]{1,0:T(8,128)S(1)} %collective-permute-done.2.from_pair, f32[48,2048]{1,0:T(8,128)S(1)} %collective-permute-done.3.from_cross, ...), custom_call_target="tpu_custom_call" | custom-call | flops 5284823040 | bytes 4194304 | tf_op jit(solution)/shard_map/project_planes/pallas_call | solution.py:238
  29.1 0.0 collective-permute-done.from_pair
  29.1 0.0 collective-permute-done.1.from_cross
  29.1 0.3 combine.1
  29.4 3.4 %collective-permute-start.4 = (f32[8,128]{1,0:T(8,128)S(1)}, f32[8,128]{1,0:T(8,128)S(1)}, u32[]{:S(2)}, u32[]{:S(2)}) collective-permute-start(f32[8,128]{1,0:T(8,128)S(1)} %get-tuple-element.23), channel_id=1, source_target_pairs={{0,1},{1,0},{2,3},{3,2},{4,5},{5,4},{6,7},{7,6},{8,9},{9,8},{10,11... | collective-permute-start | bytes 12296 | tf_op jit(solution)/shard_map/ppermute | solution.py:188
  32.8 0.8 %collective-permute-done.4 = f32[8,128]{1,0:T(8,128)S(1)} collective-permute-done((f32[8,128]{1,0:T(8,128)S(1)}, f32[8,128]{1,0:T(8,128)S(1)}, u32[]{:S(2)}, u32[]{:S(2)}) %collective-permute-start.4) | collective-permute-done | bytes 4128 | tf_op jit(solution)/shard_map/ppermute | solution.py:188
  33.6 1.6 %collective-permute-start.5 = (f32[8,128]{1,0:T(8,128)S(1)}, f32[8,128]{1,0:T(8,128)S(1)}, u32[]{:S(2)}, u32[]{:S(2)}) collective-permute-start(f32[8,128]{1,0:T(8,128)S(1)} %add.15), channel_id=1, source_target_pairs={{0,2},{1,3},{2,0},{3,1},{4,6},{5,7},{6,4},{7,5},{8,10},{9,11},{10,... | collective-permute-start | bytes 12296 | tf_op jit(solution)/shard_map/ppermute | solution.py:188
  35.2 2.0 %collective-permute-done.5 = f32[8,128]{1,0:T(8,128)S(1)} collective-permute-done((f32[8,128]{1,0:T(8,128)S(1)}, f32[8,128]{1,0:T(8,128)S(1)}, u32[]{:S(2)}, u32[]{:S(2)}) %collective-permute-start.5) | collective-permute-done | bytes 4128 | tf_op jit(solution)/shard_map/ppermute | solution.py:188
  37.2 3.6 %collective-permute-start.6 = (f32[8,128]{1,0:T(8,128)S(1)}, f32[8,128]{1,0:T(8,128)S(1)}, u32[]{:S(2)}, u32[]{:S(2)}) collective-permute-start(f32[8,128]{1,0:T(8,128)S(1)} %add.16), channel_id=1, source_target_pairs={{0,4},{1,5},{2,6},{3,7},{4,0},{5,1},{6,2},{7,3},{8,12},{9,13},{10,... | collective-permute-start | bytes 12296 | tf_op jit(solution)/shard_map/ppermute | solution.py:188
  40.8 1.6 %collective-permute-done.6 = f32[8,128]{1,0:T(8,128)S(1)} collective-permute-done((f32[8,128]{1,0:T(8,128)S(1)}, f32[8,128]{1,0:T(8,128)S(1)}, u32[]{:S(2)}, u32[]{:S(2)}) %collective-permute-start.6) | collective-permute-done | bytes 4128 | tf_op jit(solution)/shard_map/ppermute | solution.py:188
  42.4 2.0 %collective-permute-start.7 = (f32[8,128]{1,0:T(8,128)S(1)}, f32[8,128]{1,0:T(8,128)S(1)}, u32[]{:S(2)}, u32[]{:S(2)}) collective-permute-start(f32[8,128]{1,0:T(8,128)S(1)} %add.17), channel_id=1, source_target_pairs={{0,8},{1,9},{2,10},{3,11},{4,12},{5,13},{6,14},{7,15},{8,0},{9,1},... | collective-permute-start | bytes 12296 | tf_op jit(solution)/shard_map/ppermute | solution.py:188
  44.4 1.6 %collective-permute-done.7 = f32[8,128]{1,0:T(8,128)S(1)} collective-permute-done((f32[8,128]{1,0:T(8,128)S(1)}, f32[8,128]{1,0:T(8,128)S(1)}, u32[]{:S(2)}, u32[]{:S(2)}) %collective-permute-start.7) | collective-permute-done | bytes 4128 | tf_op jit(solution)/shard_map/ppermute | solution.py:188
  46.0 3.5 %collective-permute-start.8 = (f32[8,128]{1,0:T(8,128)S(1)}, f32[8,128]{1,0:T(8,128)S(1)}, u32[]{:S(2)}, u32[]{:S(2)}) collective-permute-start(f32[8,128]{1,0:T(8,128)S(1)} %add.18), channel_id=1, source_target_pairs={{0,16},{1,17},{2,18},{3,19},{4,20},{5,21},{6,22},{7,23},{8,24},{9,... | collective-permute-start | bytes 12296 | tf_op jit(solution)/shard_map/ppermute | solution.py:188
  49.6 1.6 %collective-permute-done.8 = f32[8,128]{1,0:T(8,128)S(1)} collective-permute-done((f32[8,128]{1,0:T(8,128)S(1)}, f32[8,128]{1,0:T(8,128)S(1)}, u32[]{:S(2)}, u32[]{:S(2)}) %collective-permute-start.8) | collective-permute-done | bytes 4128 | tf_op jit(solution)/shard_map/ppermute | solution.py:188
  51.2 0.0 copy-done.2
  51.2 0.0 copy-done.4
  51.2 3.7 %finish.1 = (f32[48,2048]{1,0:T(8,128)}, f32[16,64,896]{2,1,0:T(8,128)}, f32[48,2048]{1,0:T(8,128)}, f32[48,2048]{1,0:T(8,128)}) custom-call(s32[16]{0:T(128)S(1)} %copy-done.4, f32[8,128]{1,0:T(8,128)S(1)} %add.19.sums, f32[48,2048]{1,0:T(8,128)S(1)} %copy-done.2, f32[48,2048]{1,0:T(8,128)S(1)} %copy-done.1, ...), custom_call_target="tpu_custom_call" | custom-call | tf_op jit(solution)/shard_map/finish/pallas_call | solution.py:271
  (5 shorter events, 0.0 us)
Async XLA Ops:
  0.6 21.2 %collective-permute-start.3 = (f32[48,2048]{1,0:T(8,128)}, f32[48,2048]{1,0:T(8,128)S(1)}, u32[]{:S(2)}, u32[]{:S(2)}) collective-permute-start(f32[48,2048]{1,0:T(8,128)} %direction.3), channel_id=1, source_target_pairs={{1,2},{3,4},{5,6},{7,8},{9,10},{11,12},{13,14},{15,16},{17,18},{19... | collective-permute-start | bytes 1179656 | tf_op jit(solution)/shard_map/ppermute | solution.py:208
  1.3 20.5 %collective-permute-start.2 = (f32[48,2048]{1,0:T(8,128)}, f32[48,2048]{1,0:T(8,128)S(1)}, u32[]{:S(2)}, u32[]{:S(2)}) collective-permute-start(f32[48,2048]{1,0:T(8,128)} %direction.3), channel_id=1, source_target_pairs={{0,1},{1,0},{2,3},{3,2},{4,5},{5,4},{6,7},{7,6},{8,9},{9,8},{10,11... | collective-permute-start | bytes 1179656 | tf_op jit(solution)/shard_map/ppermute | solution.py:207
  4.7 2.0 %copy-start = (f32[16,64,896]{2,1,0:T(8,128)S(1)}, f32[16,64,896]{2,1,0:T(8,128)}, u32[]{:S(2)}) copy-start(f32[16,64,896]{2,1,0:T(8,128)} %residual_hbm.1) | copy-start | bytes 11010052
  6.8 0.7 %copy-start.3 = (s32[16]{0:T(128)S(1)}, s32[16]{0:T(128)}, u32[]{:S(2)}) copy-start(s32[16]{0:T(128)} %offsets.3) | copy-start | bytes 196
  7.4 14.4 %copy-start.1 = (f32[48,2048]{1,0:T(8,128)S(1)}, f32[48,2048]{1,0:T(8,128)}, u32[]{:S(2)}) copy-start(f32[48,2048]{1,0:T(8,128)} %direction.3) | copy-start | bytes 1179652
  7.4 14.4 %copy-start.5 = (f32[48,2048]{1,0:T(8,128)S(1)}, f32[48,2048]{1,0:T(8,128)}, u32[]{:S(2)}) copy-start(f32[48,2048]{1,0:T(8,128)} %gradient.1) | copy-start | bytes 1179652
  21.0 8.0 %collective-permute-start = (bf16[48,2176]{1,0:T(8,128)(2,1)S(1)}, bf16[48,2176]{1,0:T(8,128)(2,1)S(1)}, u32[]{:S(2)}, u32[]{:S(2)}) collective-permute-start(bf16[48,2176]{1,0:T(8,128)(2,1)S(1)} %get-tuple-element.17), channel_id=1, source_target_pairs={{0,1},{1,0},{2,3},{3,2},{4,5},{5,4},{6,7},{7,6},{8,9},{9,8},{10,11... | collective-permute-start | bytes 626696 | tf_op jit(solution)/shard_map/ppermute | solution.py:235
  21.2 7.9 %collective-permute-start.1 = (bf16[48,2176]{1,0:T(8,128)(2,1)S(1)}, bf16[48,2176]{1,0:T(8,128)(2,1)S(1)}, u32[]{:S(2)}, u32[]{:S(2)}) collective-permute-start(bf16[48,2176]{1,0:T(8,128)(2,1)S(1)} %get-tuple-element.18), channel_id=1, source_target_pairs={{1,2},{3,4},{5,6},{7,8},{9,10},{11,12},{13,14},{15,16},{17,18},{19... | collective-permute-start | bytes 626696 | tf_op jit(solution)/shard_map/ppermute | solution.py:236
  21.9 29.3 %copy-start.2 = (f32[48,2048]{1,0:T(8,128)S(1)}, f32[48,2048]{1,0:T(8,128)}, u32[]{:S(2)}) copy-start(f32[48,2048]{1,0:T(8,128)} %solution.1) | copy-start | bytes 1179652
  21.9 29.3 %copy-start.4 = (s32[16]{0:T(128)S(1)}, s32[16]{0:T(128)}, u32[]{:S(2)}) copy-start(s32[16]{0:T(128)} %offsets.3) | copy-start | bytes 196
  29.4 4.2 %collective-permute-start.4 = (f32[8,128]{1,0:T(8,128)S(1)}, f32[8,128]{1,0:T(8,128)S(1)}, u32[]{:S(2)}, u32[]{:S(2)}) collective-permute-start(f32[8,128]{1,0:T(8,128)S(1)} %get-tuple-element.23), channel_id=1, source_target_pairs={{0,1},{1,0},{2,3},{3,2},{4,5},{5,4},{6,7},{7,6},{8,9},{9,8},{10,11... | collective-permute-start | bytes 12296 | tf_op jit(solution)/shard_map/ppermute | solution.py:188
  33.6 3.6 %collective-permute-start.5 = (f32[8,128]{1,0:T(8,128)S(1)}, f32[8,128]{1,0:T(8,128)S(1)}, u32[]{:S(2)}, u32[]{:S(2)}) collective-permute-start(f32[8,128]{1,0:T(8,128)S(1)} %add.15), channel_id=1, source_target_pairs={{0,2},{1,3},{2,0},{3,1},{4,6},{5,7},{6,4},{7,5},{8,10},{9,11},{10,... | collective-permute-start | bytes 12296 | tf_op jit(solution)/shard_map/ppermute | solution.py:188
  37.2 5.2 %collective-permute-start.6 = (f32[8,128]{1,0:T(8,128)S(1)}, f32[8,128]{1,0:T(8,128)S(1)}, u32[]{:S(2)}, u32[]{:S(2)}) collective-permute-start(f32[8,128]{1,0:T(8,128)S(1)} %add.16), channel_id=1, source_target_pairs={{0,4},{1,5},{2,6},{3,7},{4,0},{5,1},{6,2},{7,3},{8,12},{9,13},{10,... | collective-permute-start | bytes 12296 | tf_op jit(solution)/shard_map/ppermute | solution.py:188
  42.4 3.6 %collective-permute-start.7 = (f32[8,128]{1,0:T(8,128)S(1)}, f32[8,128]{1,0:T(8,128)S(1)}, u32[]{:S(2)}, u32[]{:S(2)}) collective-permute-start(f32[8,128]{1,0:T(8,128)S(1)} %add.17), channel_id=1, source_target_pairs={{0,8},{1,9},{2,10},{3,11},{4,12},{5,13},{6,14},{7,15},{8,0},{9,1},... | collective-permute-start | bytes 12296 | tf_op jit(solution)/shard_map/ppermute | solution.py:188
  46.0 5.1 %collective-permute-start.8 = (f32[8,128]{1,0:T(8,128)S(1)}, f32[8,128]{1,0:T(8,128)S(1)}, u32[]{:S(2)}, u32[]{:S(2)}) collective-permute-start(f32[8,128]{1,0:T(8,128)S(1)} %add.18), channel_id=1, source_target_pairs={{0,16},{1,17},{2,18},{3,19},{4,20},{5,21},{6,22},{7,23},{8,24},{9,... | collective-permute-start | bytes 12296 | tf_op jit(solution)/shard_map/ppermute | solution.py:188

commit v3 on v2

v3 whole, which is shorter than its diff:
```python
import jax
import jax.numpy as jnp
from jax import lax
from jax.experimental import pallas as pl
from jax.experimental.pallas import tpu as pltpu
from jax.sharding import PartitionSpec as P

ANGLES = 4
LANES = 128
F32 = jnp.float32
BF16 = jnp.bfloat16
MIB = 1 << 20


def first_plane(offsets, v, slab_rows):
    return offsets[v] - lax.axis_index("slab") * slab_rows + slab_rows


def pair_is_above():
    return lax.rem(lax.axis_index("slab"), 2) == 0


def split(x):
    high = x.astype(BF16)
    return high, (x - high.astype(F32)).astype(BF16)


def lane_sums(x):
    total = x[:, :LANES]
    for j in range(1, x.shape[1] // LANES):
        total = total + x[:, j * LANES : (j + 1) * LANES]
    return jnp.sum(total, axis=0, keepdims=True)


def sum_residuals(offsets_hbm, residual_hbm, tiles_hbm, own, to_pair, to_cross, residual, tile,
                  rows, offsets, sem, offsets_sem, tile_sem):
    views, detector_rows, columns = residual.shape
    slab_rows = own.shape[0]
    near = 3 * slab_rows
    blocks = columns // LANES

    def copy(v):
        return pltpu.make_async_copy(residual_hbm.at[v], residual.at[v], sem.at[v])

    offsets_copy = pltpu.make_async_copy(offsets_hbm, offsets, offsets_sem)
    offsets_copy.start()
    for v in range(views):
        copy(v).start()
    tile_copy = pltpu.make_async_copy(tiles_hbm.at[0], tile, tile_sem)
    tile_copy.start()
    above = pair_is_above()
    pair_row = pl.multiple_of(jnp.where(above, 2 * slab_rows, 0), 16)
    cross_row = pl.multiple_of(jnp.where(above, 0, 2 * slab_rows), 16)

    rows[: ANGLES * blocks] = jnp.zeros((ANGLES * blocks, near, LANES), F32)
    plane = lax.broadcasted_iota(jnp.int32, (near, LANES), 0)
    lane = lax.broadcasted_iota(jnp.int32, (near, LANES), 1)
    counts = jnp.zeros((near, LANES), F32)
    offsets_copy.wait()
    for v in range(views):
        first = first_plane(offsets, v, slab_rows)
        seen = (plane >= first) & (plane < first + detector_rows) & (lane == v % ANGLES)
        counts = counts + seen.astype(F32)
    rows[ANGLES * blocks] = counts

    for v in range(views):
        first = first_plane(offsets, v, slab_rows)
        copy(v).wait()
        for j in range(blocks):
            rows[v % ANGLES * blocks + j, pl.ds(first, detector_rows), :] += residual[
                v, :, j * LANES : (j + 1) * LANES
            ]
    for k in range(ANGLES * blocks + 1):
        cut = slice(k * LANES, (k + 1) * LANES)
        to_pair[:, cut] = rows[k, pl.ds(pair_row, slab_rows), :].astype(BF16)
        to_cross[:, cut] = rows[k, pl.ds(cross_row, slab_rows), :].astype(BF16)
        own[:, cut] = rows[k, slab_rows : 2 * slab_rows, :]
    tile_copy.wait()


def project_planes(direction, from_pair, from_cross, gradient, tile, tiles_hbm, planes, back,
                   squares, grad_sums, tiles, near, sem):
    slab_rows = direction.shape[0]
    cells, columns = tile.shape
    copies = [
        pltpu.make_async_copy(tiles_hbm.at[a], tiles.at[a - 1], sem.at[a - 1])
        for a in range(1, ANGLES)
    ]
    for c in copies:
        c.start()
    above = pair_is_above()
    pair_row = pl.multiple_of(jnp.where(above, 2 * slab_rows, 0), 16)
    cross_row = pl.multiple_of(jnp.where(above, 0, 2 * slab_rows), 16)
    near[pl.ds(slab_rows, slab_rows), :] = direction[...].astype(BF16)
    near[pl.ds(pair_row, slab_rows), :] = from_pair[...].astype(BF16)
    near[pl.ds(cross_row, slab_rows), :] = from_cross[...].astype(BF16)
    grad_sums[...] = lane_sums(gradient[...] * gradient[...])
    for a in range(ANGLES):
        weights = tile if a == 0 else tiles.at[a - 1]
        if a > 0:
            copies[a - 1].wait()
        image = jnp.dot(near[...], weights[...], preferred_element_type=F32)
        total = None
        for j in range(columns // LANES):
            block = image[:, j * LANES : (j + 1) * LANES]
            planes[a, j] = block
            mine = block[slab_rows : 2 * slab_rows]
            total = mine * mine if total is None else total + mine * mine
        squares[a] = total
        both = jnp.concatenate(split(image[slab_rows : 2 * slab_rows]), axis=0)
        for b in range(0, cells, 512):
            part = lax.dot_general(
                both, weights[b : b + 512, :], (((1,), (1,)), ((), ())),
                preferred_element_type=F32,
            )
            back[a, :, b : b + 512] = part[:slab_rows] + part[slab_rows:]


def combine(own, from_pair, from_cross, tile, tiles, back, squares, grad_sums, residual_part,
            image_part, sums):
    slab_rows = own.shape[0]
    cells, columns = tile.shape

    def gathered(cut):
        return own[:, cut] + from_pair[:, cut].astype(F32) + from_cross[:, cut].astype(F32)

    for a in range(ANGLES):
        rows = gathered(slice(a * columns, (a + 1) * columns))
        both = jnp.concatenate(split(rows), axis=0)
        weights = tile if a == 0 else tiles.at[a - 1]
        for b in range(0, cells, 512):
            part = lax.dot_general(
                both, weights[b : b + 512, :], (((1,), (1,)), ((), ())),
                preferred_element_type=F32,
            )
            part = part[:slab_rows] + part[slab_rows:]
            if a == 0:
                residual_part[:, b : b + 512] = part
            else:
                residual_part[:, b : b + 512] += part

    counts = gathered(slice(ANGLES * columns, ANGLES * columns + LANES))
    zero = jnp.zeros((1, LANES), F32)
    rr, ri, ii = zero, zero, zero
    weights = [counts[:, a : a + 1] for a in range(ANGLES)]
    for b in range(0, cells, 512):
        cut = slice(b, b + 512)
        r = residual_part[:, cut]
        i = weights[0] * back[0, :, cut]
        for a in range(1, ANGLES):
            i = i + weights[a] * back[a, :, cut]
        image_part[:, cut] = i
        rr, ri, ii = rr + lane_sums(r * r), ri + lane_sums(r * i), ii + lane_sums(i * i)
    image_norm = weights[0] * squares[0]
    for a in range(1, ANGLES):
        image_norm = image_norm + weights[a] * squares[a]
    sums[...] = jnp.concatenate(
        [grad_sums[...], lane_sums(image_norm), rr, ri, ii, zero, zero, zero], axis=0
    )


def finish(offsets, sums, solution, direction, residual_part, image_part, planes, residual,
           solution_hbm, residual_hbm, gradient_hbm, direction_hbm, updated, small, sem, small_sem):
    views, detector_rows, columns = residual.shape
    slab_rows = solution.shape[0]
    total = jnp.sum(sums[...], axis=1, keepdims=True)
    grad_norm, image_norm = total[0:1], total[1:2]
    step = grad_norm / image_norm
    new_norm = total[2:3] - 2.0 * step * total[3:4] + step * step * total[4:5]
    beta = new_norm / grad_norm

    def out_copy(v):
        return pltpu.make_async_copy(updated.at[v], residual_hbm.at[v], sem.at[v])

    small_copies = [
        pltpu.make_async_copy(small.at[k], target, small_sem.at[k])
        for k, target in enumerate((gradient_hbm, solution_hbm, direction_hbm))
    ]
    gradient = residual_part[...] - step * image_part[...]
    small[0] = gradient
    small_copies[0].start()
    small[1] = solution[...] + step * direction[...]
    small_copies[1].start()
    small[2] = gradient + beta * direction[...]
    small_copies[2].start()
    for v in range(views):
        first = first_plane(offsets, v, slab_rows)
        for j in range(columns // LANES):
            cut = slice(j * LANES, (j + 1) * LANES)
            updated[v, :, cut] = (
                residual[v, :, cut] - step * planes[v % ANGLES, j, pl.ds(first, detector_rows), :]
            )
        out_copy(v).start()
    for c in small_copies:
        c.wait()
    for v in range(views):
        out_copy(v).wait()


def summed_over_slabs(x):
    count = lax.axis_size("slab")
    for masks in ((1, 2, 3), (8, 16, 24), (4,)):
        terms = [lax.ppermute(x, "slab", [(i, i ^ m) for i in range(count)]) for m in masks]
        for term in terms:
            x = x + term
    return x


def local(solution, direction, gradient, residual, tiles, offsets):
    slab_rows, cells = solution.shape
    views, detector_rows, columns = residual.shape
    near = 3 * slab_rows
    blocks = columns // LANES
    count = lax.axis_size("slab")
    pair = [(i, i ^ 1) for i in range(count)]
    cross = [(i, i + 1) for i in range(1, count - 1, 2)]
    cross = cross + [(i, j) for j, i in cross]

    vmem = pl.BlockSpec(memory_space=pltpu.VMEM)
    smem = pl.BlockSpec(memory_space=pltpu.SMEM)
    hbm = pl.BlockSpec(memory_space=pltpu.HBM)
    sds = jax.ShapeDtypeStruct

    direction_cross = lax.ppermute(direction, "slab", cross)
    direction_pair = lax.ppermute(direction, "slab", pair)

    wide = ANGLES * columns + LANES
    tiles = pltpu.with_memory_space_constraint(tiles, pltpu.HBM)
    own, to_pair, to_cross, residual_here, tile = pl.pallas_call(
        sum_residuals,
        name="sum_residuals",
        in_specs=[hbm] * 3,
        out_specs=[vmem] * 5,
        out_shape=[
            sds((slab_rows, wide), F32),
            sds((slab_rows, wide), BF16),
            sds((slab_rows, wide), BF16),
            pltpu.VMEM(residual.shape, F32),
            pltpu.VMEM(tiles.shape[1:], BF16),
        ],
        scratch_shapes=[
            pltpu.VMEM((wide // LANES, near, LANES), F32),
            pltpu.SMEM(offsets.shape, jnp.int32),
            pltpu.SemaphoreType.DMA((views,)),
            pltpu.SemaphoreType.DMA,
            pltpu.SemaphoreType.DMA,
        ],
        compiler_params=pltpu.CompilerParams(vmem_limit_bytes=8 * MIB),
        cost_estimate=pl.CostEstimate(
            flops=residual.size, bytes_accessed=4 * residual.size, transcendentals=0
        ),
    )(
        pltpu.with_memory_space_constraint(offsets, pltpu.HBM),
        pltpu.with_memory_space_constraint(residual, pltpu.HBM),
        tiles,
    )

    from_cross = lax.ppermute(to_cross, "slab", cross)
    from_pair = lax.ppermute(to_pair, "slab", pair)

    planes, back, squares, grad_sums, tiles_here = pl.pallas_call(
        project_planes,
        name="project_planes",
        in_specs=[vmem] * 5 + [hbm],
        out_specs=[vmem] * 5,
        out_shape=[
            sds((ANGLES, blocks, near, LANES), F32),
            sds((ANGLES, slab_rows, cells), F32),
            sds((ANGLES, slab_rows, LANES), F32),
            sds((1, LANES), F32),
            pltpu.VMEM((ANGLES - 1, *tiles.shape[1:]), BF16),
        ],
        scratch_shapes=[
            pltpu.VMEM((near, cells), BF16),
            pltpu.SemaphoreType.DMA((ANGLES - 1,)),
        ],
        compiler_params=pltpu.CompilerParams(vmem_limit_bytes=8 * MIB),
        cost_estimate=pl.CostEstimate(
            flops=5 * near * cells * columns * ANGLES, bytes_accessed=4 * MIB, transcendentals=0
        ),
    )(direction, direction_pair, direction_cross, gradient, tile, tiles)

    residual_part, image_part, sums = pl.pallas_call(
        combine,
        name="combine",
        in_specs=[vmem] * 8,
        out_specs=[vmem] * 3,
        out_shape=[
            sds((slab_rows, cells), F32),
            sds((slab_rows, cells), F32),
            sds((8, LANES), F32),
        ],
        compiler_params=pltpu.CompilerParams(vmem_limit_bytes=8 * MIB),
    )(own, from_pair, from_cross, tile, tiles_here, back, squares, grad_sums)

    sums = summed_over_slabs(sums)

    return pl.pallas_call(
        finish,
        name="finish",
        in_specs=[smem] + [vmem] * 7,
        out_specs=[hbm] * 4,
        out_shape=[
            sds(solution.shape, F32),
            sds(residual.shape, F32),
            sds(solution.shape, F32),
            sds(solution.shape, F32),
        ],
        scratch_shapes=[
            pltpu.VMEM(residual.shape, F32),
            pltpu.VMEM((3, slab_rows, cells), F32),
            pltpu.SemaphoreType.DMA((views,)),
            pltpu.SemaphoreType.DMA((3,)),
        ],
        compiler_params=pltpu.CompilerParams(vmem_limit_bytes=12 * MIB),
    )(offsets, sums, solution, direction, residual_part, image_part, planes, residual_here)


def solution(mesh):
    placed = (
        P(("scan", "slab"), None),
        P(("scan", "slab"), None),
        P(("scan", "slab"), None),
        P(("scan", "slab"), None, None),
        P(),
        P(("scan", "slab")),
    )
    return jax.shard_map(
        local,
        mesh=mesh,
        in_specs=placed,
        out_specs=(
            P(("scan", "slab"), None),
            P(("scan", "slab"), None, None),
            P(("scan", "slab"), None),
            P(("scan", "slab"), None),
        ),
        check_vma=False,
    )
```

time: 55.5 us -> 46.3 us (0.83)
  Pallas kernels: 24.8 us -> 19 us
  local copies, waits for them, and re-layouts: 2.71 us -> 0.02 us
  starting transfers between devices: 19 us -> 17.4 us
  waiting for transfers between devices: 7.6 us -> 8.99 us
    pallas_call x2, Pallas kernels: 13.9 us -> 8.09 us  [the longest x1 4.62 us: local(): pl.pallas_call(combine, name='combine', in_specs=[vmem] * 8, out_specs=[v...]
    unnamed x12 -> x8, local copies, waits for them, and re-layouts: 2.71 us -> 0.02 us
    ppermute x5 -> x7, starting transfers between devices: 14.1 us -> 12.4 us  [summed_over_slabs(): lax.ppermute(x, 'slab', [(i, i ^ m) for i in range(count)])]
    ppermute x5 -> x7, waiting for transfers between devices: 7.59 us -> 8.98 us  [summed_over_slabs(): lax.ppermute(x, 'slab', [(i, i ^ m) for i in range(count)])]
    pallas_call x1, Pallas kernels: 7.18 us -> 7.78 us  [local(): pl.pallas_call(project_planes, name='project_planes', in_specs=[vmem] * 5...]
    pallas_call x1, Pallas kernels: 3.67 us -> 3.1 us  [local(): pl.pallas_call(finish, name='finish', in_specs=[smem] + [vmem] * 7, out_s...]
  transfers between devices with their start and end apart: 9 -> 11, of which waited for: 5 -> 5; matrix products, arithmetic and copies ran while one was open for 0% -> 0% of each run, Pallas kernels for 38% -> 24%
where the time goes in v3:
time: 46.3 us; the launch traced here: 46.2 us
  Pallas kernels  19 us (41%)
  starting transfers between devices  17.4 us (38%)
  waiting for transfers between devices  8.99 us (19%)
  between operations  0.77 us (2%)
    ppermute x7, starting transfers between devices, summed_over_slabs(): lax.ppermute(x, 'slab', [(i, i ^ m) for i in range(count)])  12.4 us
    ppermute x7, waiting for transfers between devices, summed_over_slabs(): lax.ppermute(x, 'slab', [(i, i ^ m) for i in range(count)])  8.98 us
    pallas_call x1, Pallas kernels, local(): pl.pallas_call(project_planes, name='project_planes', in_specs=[vmem] * 5...  7.78 us
    pallas_call x1, Pallas kernels, local(): pl.pallas_call(combine, name='combine', in_specs=[vmem] * 8, out_specs=[v...  4.62 us
    pallas_call x1, Pallas kernels, local(): pl.pallas_call(sum_residuals, name='sum_residuals', in_specs=[hbm] * 3, o...  3.47 us
    ppermute x1, starting transfers between devices, local(): direction_pair = lax.ppermute(direction, 'slab', pair)  3.42 us
    pallas_call x1, Pallas kernels, local(): pl.pallas_call(finish, name='finish', in_specs=[smem] + [vmem] * 7, out_s...  3.1 us
  transfers between devices with their start and end apart: 11, of which 5 were waited for; matrix products, arithmetic and copies ran while one was open for 0% of the time, Pallas kernels for 24%

profile of v3, /device:TPU:0, one launch (start us, length us, event | category | flops | bytes accessed | tf_op | source)
XLA Modules:
  0.0 46.2 jit_solution(1577243582693714428)
XLA Ops:
  0.6 0.0 copy-start
  0.6 0.0 copy-start.2
  0.7 0.8 %collective-permute-start.3 = (f32[48,2048]{1,0:T(8,128)}, f32[48,2048]{1,0:T(8,128)S(1)}, u32[]{:S(2)}, u32[]{:S(2)}) collective-permute-start(f32[48,2048]{1,0:T(8,128)} %direction.3), channel_id=1, source_target_pairs={{1,2},{3,4},{5,6},{7,8},{9,10},{11,12},{13,14},{15,16},{17,18},{19... | collective-permute-start | bytes 1179656 | tf_op jit(solution)/shard_map/ppermute | solution.py:224
  1.5 3.4 %collective-permute-start.2 = (f32[48,2048]{1,0:T(8,128)}, f32[48,2048]{1,0:T(8,128)S(1)}, u32[]{:S(2)}, u32[]{:S(2)}) collective-permute-start(f32[48,2048]{1,0:T(8,128)} %direction.3), channel_id=1, source_target_pairs={{0,1},{1,0},{2,3},{3,2},{4,5},{5,4},{6,7},{7,6},{8,9},{9,8},{10,11... | collective-permute-start | bytes 1179656 | tf_op jit(solution)/shard_map/ppermute | solution.py:225
  4.9 3.5 %sum_residuals.1 = (f32[48,3712]{1,0:T(8,128)S(1)}, bf16[48,3712]{1,0:T(8,128)(2,1)S(1)}, bf16[48,3712]{1,0:T(8,128)(2,1)S(1)}, f32[16,64,896]{2,1,0:T(8,128)S(1)}, bf16[2048,896]{1,0:T(8,128)(2,1)S(1)}) custom-call(s32[16]{0:T(128)} %offsets.1, f32[16,64,896]{2,1,0:T(8,128)} %residual_hbm.1, bf16[4,2048,896]{2,1,0:T(8,128)(2,1)} %tiles_hbm.3), custom_call_target="tpu_custom_call" | custom-call | flops 917504 | bytes 3670016 | tf_op jit(solution)/shard_map/sum_residuals/pallas_call | solution.py:229
  8.4 0.1 collective-permute-start
  8.5 0.7 %collective-permute-start.1 = (bf16[48,3712]{1,0:T(8,128)(2,1)S(1)}, bf16[48,3712]{1,0:T(8,128)(2,1)S(1)}, u32[]{:S(2)}, u32[]{:S(2)}) collective-permute-start(bf16[48,3712]{1,0:T(8,128)(2,1)S(1)} %get-tuple-element.19), channel_id=1, source_target_pairs={{1,2},{3,4},{5,6},{7,8},{9,10},{11,12},{13,14},{15,16},{17,18},{19... | collective-permute-start | bytes 1069064 | tf_op jit(solution)/shard_map/ppermute | solution.py:258
  9.2 0.0 collective-permute-done.3.from_cross
  9.2 0.0 collective-permute-done.2.from_pair
  9.2 0.0 copy-done
  9.2 0.0 copy-done.2
  9.2 7.8 %project_planes.1 = (f32[4,7,144,128]{3,2,1,0:T(8,128)S(1)}, f32[4,48,2048]{2,1,0:T(8,128)S(1)}, f32[4,48,128]{2,1,0:T(8,128)S(1)}, f32[1,128]{1,0:T(1,128)S(1)}, bf16[3,2048,896]{2,1,0:T(8,128)(2,1)S(1)}) custom-call(f32[48,2048]{1,0:T(8,128)S(1)} %copy-done, f32[48,2048]{1,0:T(8,128)S(1)} %collective-permute-done.2.from_pair, ...), custom_call_target="tpu_custom_call" | custom-call | flops 5284823040 | bytes 4194304 | tf_op jit(solution)/shard_map/project_planes/pallas_call | solution.py:261
  17.0 0.0 collective-permute-done.from_pair
  17.0 0.0 collective-permute-done.1.from_cross
  17.0 0.0 copy-start.1
  17.0 0.0 copy-start.3
  17.0 4.6 %combine.1 = (f32[48,2048]{1,0:T(8,128)S(1)}, f32[48,2048]{1,0:T(8,128)S(1)}, f32[8,128]{1,0:T(8,128)S(1)}) custom-call(f32[48,3712]{1,0:T(8,128)S(1)} %get-tuple-element.17.own, bf16[48,3712]{1,0:T(8,128)(2,1)S(1)} %collective-permute-done.from_pair, bf16[48,3712]{1,0:T(8,128)(2,1)S(1)} %collective-permute-done.1.from_cross, ...), custom_call_target="tpu_custom_call" | custom-call | tf_op jit(solution)/shard_map/combine/pallas_call | solution.py:283
  21.7 4.6 %collective-permute-start.6 = (f32[8,128]{1,0:T(8,128)S(1)}, f32[8,128]{1,0:T(8,128)S(1)}, u32[]{:S(2)}, u32[]{:S(2)}) collective-permute-start(f32[8,128]{1,0:T(8,128)S(1)} %get-tuple-element.25), channel_id=1, source_target_pairs={{0,3},{1,2},{2,1},{3,0},{4,7},{5,6},{6,5},{7,4},{8,11},{9,10},{10,... | collective-permute-start | bytes 12296 | tf_op jit(solution)/shard_map/ppermute | solution.py:203
  26.2 0.4 collective-permute-start.5
  26.6 0.0 collective-permute-start.4
  26.6 0.9 %collective-permute-done.6 = f32[8,128]{1,0:T(8,128)S(1)} collective-permute-done((f32[8,128]{1,0:T(8,128)S(1)}, f32[8,128]{1,0:T(8,128)S(1)}, u32[]{:S(2)}, u32[]{:S(2)}) %collective-permute-start.6) | collective-permute-done | bytes 4128 | tf_op jit(solution)/shard_map/ppermute | solution.py:203
  27.6 2.3 %collective-permute-done.5 = f32[8,128]{1,0:T(8,128)S(1)} collective-permute-done((f32[8,128]{1,0:T(8,128)S(1)}, f32[8,128]{1,0:T(8,128)S(1)}, u32[]{:S(2)}, u32[]{:S(2)}) %collective-permute-start.5) | collective-permute-done | bytes 4128 | tf_op jit(solution)/shard_map/ppermute | solution.py:203
  29.8 0.0 collective-permute-done.4
  29.8 2.9 %collective-permute-start.9 = (f32[8,128]{1,0:T(8,128)S(1)}, f32[8,128]{1,0:T(8,128)S(1)}, u32[]{:S(2)}, u32[]{:S(2)}) collective-permute-start(f32[8,128]{1,0:T(8,128)S(1)} %add_add_fusion.1), channel_id=1, source_target_pairs={{0,24},{1,25},{2,26},{3,27},{4,28},{5,29},{6,30},{7,31},{8,16},{9,... | collective-permute-start | bytes 12296 | tf_op jit(solution)/shard_map/ppermute | solution.py:203
  32.7 0.8 %collective-permute-start.8 = (f32[8,128]{1,0:T(8,128)S(1)}, f32[8,128]{1,0:T(8,128)S(1)}, u32[]{:S(2)}, u32[]{:S(2)}) collective-permute-start(f32[8,128]{1,0:T(8,128)S(1)} %add_add_fusion.1), channel_id=1, source_target_pairs={{0,16},{1,17},{2,18},{3,19},{4,20},{5,21},{6,22},{7,23},{8,24},{9,... | collective-permute-start | bytes 12296 | tf_op jit(solution)/shard_map/ppermute | solution.py:203
  33.5 0.5 %collective-permute-start.7 = (f32[8,128]{1,0:T(8,128)S(1)}, f32[8,128]{1,0:T(8,128)S(1)}, u32[]{:S(2)}, u32[]{:S(2)}) collective-permute-start(f32[8,128]{1,0:T(8,128)S(1)} %add_add_fusion.1), channel_id=1, source_target_pairs={{0,8},{1,9},{2,10},{3,11},{4,12},{5,13},{6,14},{7,15},{8,0},{9,1},... | collective-permute-start | bytes 12296 | tf_op jit(solution)/shard_map/ppermute | solution.py:203
  34.0 0.7 %collective-permute-done.9 = f32[8,128]{1,0:T(8,128)S(1)} collective-permute-done((f32[8,128]{1,0:T(8,128)S(1)}, f32[8,128]{1,0:T(8,128)S(1)}, u32[]{:S(2)}, u32[]{:S(2)}) %collective-permute-start.9) | collective-permute-done | bytes 4128 | tf_op jit(solution)/shard_map/ppermute | solution.py:203
  34.7 3.1 %collective-permute-done.8 = f32[8,128]{1,0:T(8,128)S(1)} collective-permute-done((f32[8,128]{1,0:T(8,128)S(1)}, f32[8,128]{1,0:T(8,128)S(1)}, u32[]{:S(2)}, u32[]{:S(2)}) %collective-permute-start.8) | collective-permute-done | bytes 4128 | tf_op jit(solution)/shard_map/ppermute | solution.py:203
  37.8 0.0 collective-permute-done.7
  37.9 3.2 %collective-permute-start.10 = (f32[8,128]{1,0:T(8,128)S(1)}, f32[8,128]{1,0:T(8,128)S(1)}, u32[]{:S(2)}, u32[]{:S(2)}) collective-permute-start(f32[8,128]{1,0:T(8,128)S(1)} %add_add_fusion), channel_id=1, source_target_pairs={{0,4},{1,5},{2,6},{3,7},{4,0},{5,1},{6,2},{7,3},{8,12},{9,13},{10,... | collective-permute-start | bytes 12296 | tf_op jit(solution)/shard_map/ppermute | solution.py:203
  41.1 2.0 %collective-permute-done.10 = f32[8,128]{1,0:T(8,128)S(1)} collective-permute-done((f32[8,128]{1,0:T(8,128)S(1)}, f32[8,128]{1,0:T(8,128)S(1)}, u32[]{:S(2)}, u32[]{:S(2)}) %collective-permute-start.10) | collective-permute-done | bytes 4128 | tf_op jit(solution)/shard_map/ppermute | solution.py:203
  43.0 0.0 copy-done.1
  43.1 0.0 copy-done.3
  43.1 3.1 %finish.1 = (f32[48,2048]{1,0:T(8,128)}, f32[16,64,896]{2,1,0:T(8,128)}, f32[48,2048]{1,0:T(8,128)}, f32[48,2048]{1,0:T(8,128)}) custom-call(s32[16]{0:T(128)S(1)} %copy-done.3, f32[8,128]{1,0:T(8,128)S(1)} %add.27.sums, f32[48,2048]{1,0:T(8,128)S(1)} %copy-done.1, f32[48,2048]{1,0:T(8,128)S(1)} %copy-done, f32[48,2048]{1,0:T(8,128)S(1)} %get-tuple-element.26.residual_part, ...), custom_call_target="tpu_custom_call" | custom-call | tf_op jit(solution)/shard_map/finish/pallas_call | solution.py:298
  (3 shorter events, 0.0 us)
Async XLA Ops:
  0.6 8.6 %copy-start = (f32[48,2048]{1,0:T(8,128)S(1)}, f32[48,2048]{1,0:T(8,128)}, u32[]{:S(2)}) copy-start(f32[48,2048]{1,0:T(8,128)} %direction.3) | copy-start | bytes 1179652
  0.6 8.6 %copy-start.2 = (f32[48,2048]{1,0:T(8,128)S(1)}, f32[48,2048]{1,0:T(8,128)}, u32[]{:S(2)}) copy-start(f32[48,2048]{1,0:T(8,128)} %gradient.1) | copy-start | bytes 1179652
  0.7 8.5 %collective-permute-start.3 = (f32[48,2048]{1,0:T(8,128)}, f32[48,2048]{1,0:T(8,128)S(1)}, u32[]{:S(2)}, u32[]{:S(2)}) collective-permute-start(f32[48,2048]{1,0:T(8,128)} %direction.3), channel_id=1, source_target_pairs={{1,2},{3,4},{5,6},{7,8},{9,10},{11,12},{13,14},{15,16},{17,18},{19... | collective-permute-start | bytes 1179656 | tf_op jit(solution)/shard_map/ppermute | solution.py:224
  1.5 7.7 %collective-permute-start.2 = (f32[48,2048]{1,0:T(8,128)}, f32[48,2048]{1,0:T(8,128)S(1)}, u32[]{:S(2)}, u32[]{:S(2)}) collective-permute-start(f32[48,2048]{1,0:T(8,128)} %direction.3), channel_id=1, source_target_pairs={{0,1},{1,0},{2,3},{3,2},{4,5},{5,4},{6,7},{7,6},{8,9},{9,8},{10,11... | collective-permute-start | bytes 1179656 | tf_op jit(solution)/shard_map/ppermute | solution.py:225
  8.4 8.6 %collective-permute-start = (bf16[48,3712]{1,0:T(8,128)(2,1)S(1)}, bf16[48,3712]{1,0:T(8,128)(2,1)S(1)}, u32[]{:S(2)}, u32[]{:S(2)}) collective-permute-start(bf16[48,3712]{1,0:T(8,128)(2,1)S(1)} %get-tuple-element.18), channel_id=1, source_target_pairs={{0,1},{1,0},{2,3},{3,2},{4,5},{5,4},{6,7},{7,6},{8,9},{9,8},{10,11... | collective-permute-start | bytes 1069064 | tf_op jit(solution)/shard_map/ppermute | solution.py:259
  8.5 8.5 %collective-permute-start.1 = (bf16[48,3712]{1,0:T(8,128)(2,1)S(1)}, bf16[48,3712]{1,0:T(8,128)(2,1)S(1)}, u32[]{:S(2)}, u32[]{:S(2)}) collective-permute-start(bf16[48,3712]{1,0:T(8,128)(2,1)S(1)} %get-tuple-element.19), channel_id=1, source_target_pairs={{1,2},{3,4},{5,6},{7,8},{9,10},{11,12},{13,14},{15,16},{17,18},{19... | collective-permute-start | bytes 1069064 | tf_op jit(solution)/shard_map/ppermute | solution.py:258
  17.0 26.0 %copy-start.1 = (f32[48,2048]{1,0:T(8,128)S(1)}, f32[48,2048]{1,0:T(8,128)}, u32[]{:S(2)}) copy-start(f32[48,2048]{1,0:T(8,128)} %solution.1) | copy-start | bytes 1179652
  17.0 26.0 %copy-start.3 = (s32[16]{0:T(128)S(1)}, s32[16]{0:T(128)}, u32[]{:S(2)}) copy-start(s32[16]{0:T(128)} %offsets.1) | copy-start | bytes 196
  21.7 5.9 %collective-permute-start.6 = (f32[8,128]{1,0:T(8,128)S(1)}, f32[8,128]{1,0:T(8,128)S(1)}, u32[]{:S(2)}, u32[]{:S(2)}) collective-permute-start(f32[8,128]{1,0:T(8,128)S(1)} %get-tuple-element.25), channel_id=1, source_target_pairs={{0,3},{1,2},{2,1},{3,0},{4,7},{5,6},{6,5},{7,4},{8,11},{9,10},{10,... | collective-permute-start | bytes 12296 | tf_op jit(solution)/shard_map/ppermute | solution.py:203
  26.2 3.6 %collective-permute-start.5 = (f32[8,128]{1,0:T(8,128)S(1)}, f32[8,128]{1,0:T(8,128)S(1)}, u32[]{:S(2)}, u32[]{:S(2)}) collective-permute-start(f32[8,128]{1,0:T(8,128)S(1)} %get-tuple-element.25), channel_id=1, source_target_pairs={{0,2},{1,3},{2,0},{3,1},{4,6},{5,7},{6,4},{7,5},{8,10},{9,11},{10,... | collective-permute-start | bytes 12296 | tf_op jit(solution)/shard_map/ppermute | solution.py:203
  26.6 3.2 %collective-permute-start.4 = (f32[8,128]{1,0:T(8,128)S(1)}, f32[8,128]{1,0:T(8,128)S(1)}, u32[]{:S(2)}, u32[]{:S(2)}) collective-permute-start(f32[8,128]{1,0:T(8,128)S(1)} %get-tuple-element.25), channel_id=1, source_target_pairs={{0,1},{1,0},{2,3},{3,2},{4,5},{5,4},{6,7},{7,6},{8,9},{9,8},{10,11... | collective-permute-start | bytes 12296 | tf_op jit(solution)/shard_map/ppermute | solution.py:203
  29.8 4.9 %collective-permute-start.9 = (f32[8,128]{1,0:T(8,128)S(1)}, f32[8,128]{1,0:T(8,128)S(1)}, u32[]{:S(2)}, u32[]{:S(2)}) collective-permute-start(f32[8,128]{1,0:T(8,128)S(1)} %add_add_fusion.1), channel_id=1, source_target_pairs={{0,24},{1,25},{2,26},{3,27},{4,28},{5,29},{6,30},{7,31},{8,16},{9,... | collective-permute-start | bytes 12296 | tf_op jit(solution)/shard_map/ppermute | solution.py:203
  32.7 5.1 %collective-permute-start.8 = (f32[8,128]{1,0:T(8,128)S(1)}, f32[8,128]{1,0:T(8,128)S(1)}, u32[]{:S(2)}, u32[]{:S(2)}) collective-permute-start(f32[8,128]{1,0:T(8,128)S(1)} %add_add_fusion.1), channel_id=1, source_target_pairs={{0,16},{1,17},{2,18},{3,19},{4,20},{5,21},{6,22},{7,23},{8,24},{9,... | collective-permute-start | bytes 12296 | tf_op jit(solution)/shard_map/ppermute | solution.py:203
  33.5 4.4 %collective-permute-start.7 = (f32[8,128]{1,0:T(8,128)S(1)}, f32[8,128]{1,0:T(8,128)S(1)}, u32[]{:S(2)}, u32[]{:S(2)}) collective-permute-start(f32[8,128]{1,0:T(8,128)S(1)} %add_add_fusion.1), channel_id=1, source_target_pairs={{0,8},{1,9},{2,10},{3,11},{4,12},{5,13},{6,14},{7,15},{8,0},{9,1},... | collective-permute-start | bytes 12296 | tf_op jit(solution)/shard_map/ppermute | solution.py:203
  37.9 5.2 %collective-permute-start.10 = (f32[8,128]{1,0:T(8,128)S(1)}, f32[8,128]{1,0:T(8,128)S(1)}, u32[]{:S(2)}, u32[]{:S(2)}) collective-permute-start(f32[8,128]{1,0:T(8,128)S(1)} %add_add_fusion), channel_id=1, source_target_pairs={{0,4},{1,5},{2,6},{3,7},{4,0},{5,1},{6,2},{7,3},{8,12},{9,13},{10,... | collective-permute-start | bytes 12296 | tf_op jit(solution)/shard_map/ppermute | solution.py:203

commit v4 on v3

--- a/solution.py
+++ b/solution.py
@@ -7,6 +7,7 @@
 
 ANGLES = 4
 LANES = 128
+CHUNK = 512
 F32 = jnp.float32
 BF16 = jnp.bfloat16
 MIB = 1 << 20
@@ -78,10 +79,10 @@
     tile_copy.wait()
 
 
-def project_planes(direction, from_pair, from_cross, gradient, tile, tiles_hbm, planes, back,
-                   squares, grad_sums, tiles, near, sem):
+def project_planes(direction, from_pair, from_cross, gradient, tile, tiles_hbm, planes, grad_sums,
+                   tiles, near, sem):
     slab_rows = direction.shape[0]
-    cells, columns = tile.shape
+    columns = tile.shape[1]
     copies = [
         pltpu.make_async_copy(tiles_hbm.at[a], tiles.at[a - 1], sem.at[a - 1])
         for a in range(1, ANGLES)
@@ -100,62 +101,50 @@
         if a > 0:
             copies[a - 1].wait()
         image = jnp.dot(near[...], weights[...], preferred_element_type=F32)
-        total = None
         for j in range(columns // LANES):
-            block = image[:, j * LANES : (j + 1) * LANES]
-            planes[a, j] = block
-            mine = block[slab_rows : 2 * slab_rows]
-            total = mine * mine if total is None else total + mine * mine
-        squares[a] = total
-        both = jnp.concatenate(split(image[slab_rows : 2 * slab_rows]), axis=0)
-        for b in range(0, cells, 512):
-            part = lax.dot_general(
-                both, weights[b : b + 512, :], (((1,), (1,)), ((), ())),
-                preferred_element_type=F32,
-            )
-            back[a, :, b : b + 512] = part[:slab_rows] + part[slab_rows:]
-
-
-def combine(own, from_pair, from_cross, tile, tiles, back, squares, grad_sums, residual_part,
-            image_part, sums):
+            planes[a, j] = image[:, j * LANES : (j + 1) * LANES]
+
+
+def combine(own, from_pair, from_cross, tile, tiles, planes, grad_sums, residual_part, image_part,
+            sums):
     slab_rows = own.shape[0]
     cells, columns = tile.shape
+    zero = jnp.zeros((1, LANES), F32)
 
     def gathered(cut):
         return own[:, cut] + from_pair[:, cut].astype(F32) + from_cross[:, cut].astype(F32)
 
+    counts = gathered(slice(ANGLES * columns, ANGLES * columns + LANES))
+    image_norm = zero
     for a in range(ANGLES):
         rows = gathered(slice(a * columns, (a + 1) * columns))
-        both = jnp.concatenate(split(rows), axis=0)
+        image = jnp.concatenate(
+            [planes[a, j, slab_rows : 2 * slab_rows, :] for j in range(columns // LANES)], axis=1
+        )
+        weighted = counts[:, a : a + 1] * image
+        image_norm = image_norm + lane_sums(weighted * image)
+        both = jnp.concatenate([*split(rows), *split(weighted)], axis=0)
         weights = tile if a == 0 else tiles.at[a - 1]
-        for b in range(0, cells, 512):
+        for b in range(0, cells, CHUNK):
+            cut = slice(b, b + CHUNK)
             part = lax.dot_general(
-                both, weights[b : b + 512, :], (((1,), (1,)), ((), ())),
-                preferred_element_type=F32,
+                both, weights[cut, :], (((1,), (1,)), ((), ())), preferred_element_type=F32
             )
-            part = part[:slab_rows] + part[slab_rows:]
+            r = part[:slab_rows] + part[slab_rows : 2 * slab_rows]
+            i = part[2 * slab_rows : 3 * slab_rows] + part[3 * slab_rows :]
             if a == 0:
-                residual_part[:, b : b + 512] = part
+                residual_part[:, cut] = r
+                image_part[:, cut] = i
             else:
-                residual_part[:, b : b + 512] += part
-
-    counts = gathered(slice(ANGLES * columns, ANGLES * columns + LANES))
-    zero = jnp.zeros((1, LANES), F32)
+                residual_part[:, cut] += r
+                image_part[:, cut] += i
+
     rr, ri, ii = zero, zero, zero
-    weights = [counts[:, a : a + 1] for a in range(ANGLES)]
-    for b in range(0, cells, 512):
-        cut = slice(b, b + 512)
-        r = residual_part[:, cut]
-        i = weights[0] * back[0, :, cut]
-        for a in range(1, ANGLES):
-            i = i + weights[a] * back[a, :, cut]
-        image_part[:, cut] = i
+    for b in range(0, cells, CHUNK):
+        r, i = residual_part[:, b : b + CHUNK], image_part[:, b : b + CHUNK]
         rr, ri, ii = rr + lane_sums(r * r), ri + lane_sums(r * i), ii + lane_sums(i * i)
-    image_norm = weights[0] * squares[0]
-    for a in range(1, ANGLES):
-        image_norm = image_norm + weights[a] * squares[a]
     sums[...] = jnp.concatenate(
-        [grad_sums[...], lane_sums(image_norm), rr, ri, ii, zero, zero, zero], axis=0
+        [grad_sums[...], image_norm, rr, ri, ii, zero, zero, zero], axis=0
     )
 
 
@@ -258,15 +247,13 @@
     from_cross = lax.ppermute(to_cross, "slab", cross)
     from_pair = lax.ppermute(to_pair, "slab", pair)
 
-    planes, back, squares, grad_sums, tiles_here = pl.pallas_call(
+    planes, grad_sums, tiles_here = pl.pallas_call(
         project_planes,
         name="project_planes",
         in_specs=[vmem] * 5 + [hbm],
-        out_specs=[vmem] * 5,
+        out_specs=[vmem] * 3,
         out_shape=[
             sds((ANGLES, blocks, near, LANES), F32),
-            sds((ANGLES, slab_rows, cells), F32),
-            sds((ANGLES, slab_rows, LANES), F32),
             sds((1, LANES), F32),
             pltpu.VMEM((ANGLES - 1, *tiles.shape[1:]), BF16),
         ],
@@ -276,14 +263,14 @@
         ],
         compiler_params=pltpu.CompilerParams(vmem_limit_bytes=8 * MIB),
         cost_estimate=pl.CostEstimate(
-            flops=5 * near * cells * columns * ANGLES, bytes_accessed=4 * MIB, transcendentals=0
+            flops=2 * near * cells * columns * ANGLES, bytes_accessed=16 * MIB, transcendentals=0
         ),
     )(direction, direction_pair, direction_cross, gradient, tile, tiles)
 
     residual_part, image_part, sums = pl.pallas_call(
         combine,
         name="combine",
-        in_specs=[vmem] * 8,
+        in_specs=[vmem] * 7,
         out_specs=[vmem] * 3,
         out_shape=[
             sds((slab_rows, cells), F32),
@@ -291,7 +278,7 @@
             sds((8, LANES), F32),
         ],
         compiler_params=pltpu.CompilerParams(vmem_limit_bytes=8 * MIB),
-    )(own, from_pair, from_cross, tile, tiles_here, back, squares, grad_sums)
+    )(own, from_pair, from_cross, tile, tiles_here, planes, grad_sums)
 
     sums = summed_over_slabs(sums)
 

time: 46.3 us -> 46.8 us (1.011)
  waiting for transfers between devices: 8.99 us -> 12 us
  Pallas kernels: 19 us -> 16.9 us
    ppermute x7, waiting for transfers between devices: 8.98 us -> 12 us  [summed_over_slabs(): lax.ppermute(x, 'slab', [(i, i ^ m) for i in range(count)])]
    pallas_call x1, Pallas kernels: 7.78 us -> 5.13 us  [local(): pl.pallas_call(project_planes, name='project_planes', in_specs=[vmem] * 5...]
    pallas_call x1, Pallas kernels: 4.62 us -> 5.17 us  [local(): pl.pallas_call(combine, name='combine', in_specs=[vmem] * 7, out_specs=[v...]
  transfers between devices with their start and end apart: 11 -> 11, of which waited for: 5 -> 5; matrix products, arithmetic and copies ran while one was open for 0% -> 0% of each run, Pallas kernels for 24% -> 18%
where the time goes in v4:
time: 46.8 us; the launch traced here: 46.7 us
  starting transfers between devices  17.1 us (37%)
  Pallas kernels  16.9 us (36%)
  waiting for transfers between devices  12 us (26%)
  between operations  0.76 us (2%)
    ppermute x7, starting transfers between devices, summed_over_slabs(): lax.ppermute(x, 'slab', [(i, i ^ m) for i in range(count)])  12.1 us
    ppermute x7, waiting for transfers between devices, summed_over_slabs(): lax.ppermute(x, 'slab', [(i, i ^ m) for i in range(count)])  12 us
    pallas_call x1, Pallas kernels, local(): pl.pallas_call(combine, name='combine', in_specs=[vmem] * 7, out_specs=[v...  5.17 us
    pallas_call x1, Pallas kernels, local(): pl.pallas_call(project_planes, name='project_planes', in_specs=[vmem] * 5...  5.13 us
    pallas_call x1, Pallas kernels, local(): pl.pallas_call(sum_residuals, name='sum_residuals', in_specs=[hbm] * 3, o...  3.47 us
    ppermute x1, starting transfers between devices, local(): direction_pair = lax.ppermute(direction, 'slab', pair)  3.42 us
    pallas_call x1, Pallas kernels, local(): pl.pallas_call(finish, name='finish', in_specs=[smem] + [vmem] * 7, out_s...  3.1 us
  transfers between devices with their start and end apart: 11, of which 5 were waited for; matrix products, arithmetic and copies ran while one was open for 0% of the time, Pallas kernels for 18%

profile of v4, /device:TPU:0, one launch (start us, length us, event | category | flops | bytes accessed | tf_op | source)
XLA Modules:
  0.0 46.7 jit_solution(1943513824121935217)
XLA Ops:
  0.6 0.0 copy-start
  0.6 0.0 copy-start.2
  0.7 0.8 %collective-permute-start.3 = (f32[48,2048]{1,0:T(8,128)}, f32[48,2048]{1,0:T(8,128)S(1)}, u32[]{:S(2)}, u32[]{:S(2)}) collective-permute-start(f32[48,2048]{1,0:T(8,128)} %direction.3), channel_id=1, source_target_pairs={{1,2},{3,4},{5,6},{7,8},{9,10},{11,12},{13,14},{15,16},{17,18},{19... | collective-permute-start | bytes 1179656 | tf_op jit(solution)/shard_map/ppermute | solution.py:213
  1.5 3.4 %collective-permute-start.2 = (f32[48,2048]{1,0:T(8,128)}, f32[48,2048]{1,0:T(8,128)S(1)}, u32[]{:S(2)}, u32[]{:S(2)}) collective-permute-start(f32[48,2048]{1,0:T(8,128)} %direction.3), channel_id=1, source_target_pairs={{0,1},{1,0},{2,3},{3,2},{4,5},{5,4},{6,7},{7,6},{8,9},{9,8},{10,11... | collective-permute-start | bytes 1179656 | tf_op jit(solution)/shard_map/ppermute | solution.py:214
  4.9 3.5 %sum_residuals.1 = (f32[48,3712]{1,0:T(8,128)S(1)}, bf16[48,3712]{1,0:T(8,128)(2,1)S(1)}, bf16[48,3712]{1,0:T(8,128)(2,1)S(1)}, f32[16,64,896]{2,1,0:T(8,128)S(1)}, bf16[2048,896]{1,0:T(8,128)(2,1)S(1)}) custom-call(s32[16]{0:T(128)} %offsets.1, f32[16,64,896]{2,1,0:T(8,128)} %residual_hbm.1, bf16[4,2048,896]{2,1,0:T(8,128)(2,1)} %tiles_hbm.3), custom_call_target="tpu_custom_call" | custom-call | flops 917504 | bytes 3670016 | tf_op jit(solution)/shard_map/sum_residuals/pallas_call | solution.py:218
  8.4 0.1 collective-permute-start
  8.5 0.7 %collective-permute-start.1 = (bf16[48,3712]{1,0:T(8,128)(2,1)S(1)}, bf16[48,3712]{1,0:T(8,128)(2,1)S(1)}, u32[]{:S(2)}, u32[]{:S(2)}) collective-permute-start(bf16[48,3712]{1,0:T(8,128)(2,1)S(1)} %get-tuple-element.17), channel_id=1, source_target_pairs={{1,2},{3,4},{5,6},{7,8},{9,10},{11,12},{13,14},{15,16},{17,18},{19... | collective-permute-start | bytes 1069064 | tf_op jit(solution)/shard_map/ppermute | solution.py:247
  9.2 0.0 collective-permute-done.3.from_cross
  9.2 0.0 collective-permute-done.2.from_pair
  9.2 0.0 copy-done
  9.2 0.0 copy-done.2
  9.2 5.1 %project_planes.1 = (f32[4,7,144,128]{3,2,1,0:T(8,128)S(1)}, f32[1,128]{1,0:T(1,128)S(1)}, bf16[3,2048,896]{2,1,0:T(8,128)(2,1)S(1)}) custom-call(f32[48,2048]{1,0:T(8,128)S(1)} %copy-done, f32[48,2048]{1,0:T(8,128)S(1)} %collective-permute-done.2.from_pair, f32[48,2048]{1,0:T(8,128)S(1)} %collective-permute-done.3.from_cross, f32[48,2048]{1,0:T(8,128)S(1)} %copy-done.2, ...), custom_call_target="tpu_custom_call" | custom-call | flops 2113929216 | bytes 16777216 | tf_op jit(solution)/shard_map/project_planes/pallas_call | solution.py:250
  14.3 0.0 collective-permute-done.from_pair
  14.3 0.0 collective-permute-done.1.from_cross
  14.4 0.0 copy-start.1
  14.4 0.0 copy-start.3
  14.4 5.2 %combine.1 = (f32[48,2048]{1,0:T(8,128)S(1)}, f32[48,2048]{1,0:T(8,128)S(1)}, f32[8,128]{1,0:T(8,128)S(1)}) custom-call(f32[48,3712]{1,0:T(8,128)S(1)} %get-tuple-element.15.own, bf16[48,3712]{1,0:T(8,128)(2,1)S(1)} %collective-permute-done.from_pair, bf16[48,3712]{1,0:T(8,128)(2,1)S(1)} %collective-permute-done.1.from_cross, ...), custom_call_target="tpu_custom_call" | custom-call | tf_op jit(solution)/shard_map/combine/pallas_call | solution.py:270
  19.6 4.9 %collective-permute-start.6 = (f32[8,128]{1,0:T(8,128)S(1)}, f32[8,128]{1,0:T(8,128)S(1)}, u32[]{:S(2)}, u32[]{:S(2)}) collective-permute-start(f32[8,128]{1,0:T(8,128)S(1)} %get-tuple-element.22), channel_id=1, source_target_pairs={{0,3},{1,2},{2,1},{3,0},{4,7},{5,6},{6,5},{7,4},{8,11},{9,10},{10,... | collective-permute-start | bytes 12296 | tf_op jit(solution)/shard_map/ppermute | solution.py:192
  24.4 0.1 collective-permute-start.5
  24.6 0.1 collective-permute-start.4
  24.6 1.1 %collective-permute-done.6 = f32[8,128]{1,0:T(8,128)S(1)} collective-permute-done((f32[8,128]{1,0:T(8,128)S(1)}, f32[8,128]{1,0:T(8,128)S(1)}, u32[]{:S(2)}, u32[]{:S(2)}) %collective-permute-start.6) | collective-permute-done | bytes 4128 | tf_op jit(solution)/shard_map/ppermute | solution.py:192
  25.8 2.3 %collective-permute-done.5 = f32[8,128]{1,0:T(8,128)S(1)} collective-permute-done((f32[8,128]{1,0:T(8,128)S(1)}, f32[8,128]{1,0:T(8,128)S(1)}, u32[]{:S(2)}, u32[]{:S(2)}) %collective-permute-start.5) | collective-permute-done | bytes 4128 | tf_op jit(solution)/shard_map/ppermute | solution.py:192
  28.0 0.0 collective-permute-done.4
  28.0 5.2 %collective-permute-start.9 = (f32[8,128]{1,0:T(8,128)S(1)}, f32[8,128]{1,0:T(8,128)S(1)}, u32[]{:S(2)}, u32[]{:S(2)}) collective-permute-start(f32[8,128]{1,0:T(8,128)S(1)} %add_add_fusion.1), channel_id=1, source_target_pairs={{0,24},{1,25},{2,26},{3,27},{4,28},{5,29},{6,30},{7,31},{8,16},{9,... | collective-permute-start | bytes 12296 | tf_op jit(solution)/shard_map/ppermute | solution.py:192
  33.3 0.5 %collective-permute-start.8 = (f32[8,128]{1,0:T(8,128)S(1)}, f32[8,128]{1,0:T(8,128)S(1)}, u32[]{:S(2)}, u32[]{:S(2)}) collective-permute-start(f32[8,128]{1,0:T(8,128)S(1)} %add_add_fusion.1), channel_id=1, source_target_pairs={{0,16},{1,17},{2,18},{3,19},{4,20},{5,21},{6,22},{7,23},{8,24},{9,... | collective-permute-start | bytes 12296 | tf_op jit(solution)/shard_map/ppermute | solution.py:192
  33.8 0.4 collective-permute-start.7
  34.2 0.6 %collective-permute-done.9 = f32[8,128]{1,0:T(8,128)S(1)} collective-permute-done((f32[8,128]{1,0:T(8,128)S(1)}, f32[8,128]{1,0:T(8,128)S(1)}, u32[]{:S(2)}, u32[]{:S(2)}) %collective-permute-start.9) | collective-permute-done | bytes 4128 | tf_op jit(solution)/shard_map/ppermute | solution.py:192
  34.9 3.5 %collective-permute-done.8 = f32[8,128]{1,0:T(8,128)S(1)} collective-permute-done((f32[8,128]{1,0:T(8,128)S(1)}, f32[8,128]{1,0:T(8,128)S(1)}, u32[]{:S(2)}, u32[]{:S(2)}) %collective-permute-start.8) | collective-permute-done | bytes 4128 | tf_op jit(solution)/shard_map/ppermute | solution.py:192
  38.4 0.0 collective-permute-done.7
  38.4 0.8 %collective-permute-start.10 = (f32[8,128]{1,0:T(8,128)S(1)}, f32[8,128]{1,0:T(8,128)S(1)}, u32[]{:S(2)}, u32[]{:S(2)}) collective-permute-start(f32[8,128]{1,0:T(8,128)S(1)} %add_add_fusion), channel_id=1, source_target_pairs={{0,4},{1,5},{2,6},{3,7},{4,0},{5,1},{6,2},{7,3},{8,12},{9,13},{10,... | collective-permute-start | bytes 12296 | tf_op jit(solution)/shard_map/ppermute | solution.py:192
  39.2 4.4 %collective-permute-done.10 = f32[8,128]{1,0:T(8,128)S(1)} collective-permute-done((f32[8,128]{1,0:T(8,128)S(1)}, f32[8,128]{1,0:T(8,128)S(1)}, u32[]{:S(2)}, u32[]{:S(2)}) %collective-permute-start.10) | collective-permute-done | bytes 4128 | tf_op jit(solution)/shard_map/ppermute | solution.py:192
  43.6 0.0 copy-done.1
  43.6 0.0 copy-done.3
  43.6 3.1 %finish.1 = (f32[48,2048]{1,0:T(8,128)}, f32[16,64,896]{2,1,0:T(8,128)}, f32[48,2048]{1,0:T(8,128)}, f32[48,2048]{1,0:T(8,128)}) custom-call(s32[16]{0:T(128)S(1)} %copy-done.3, f32[8,128]{1,0:T(8,128)S(1)} %add.27.sums, f32[48,2048]{1,0:T(8,128)S(1)} %copy-done.1, f32[48,2048]{1,0:T(8,128)S(1)} %copy-done, f32[48,2048]{1,0:T(8,128)S(1)} %get-tuple-element.23.residual_part, ...), custom_call_target="tpu_custom_call" | custom-call | tf_op jit(solution)/shard_map/finish/pallas_call | solution.py:285
  (3 shorter events, 0.0 us)
Async XLA Ops:
  0.6 8.6 %copy-start = (f32[48,2048]{1,0:T(8,128)S(1)}, f32[48,2048]{1,0:T(8,128)}, u32[]{:S(2)}) copy-start(f32[48,2048]{1,0:T(8,128)} %direction.3) | copy-start | bytes 1179652
  0.6 8.6 %copy-start.2 = (f32[48,2048]{1,0:T(8,128)S(1)}, f32[48,2048]{1,0:T(8,128)}, u32[]{:S(2)}) copy-start(f32[48,2048]{1,0:T(8,128)} %gradient.1) | copy-start | bytes 1179652
  0.7 8.5 %collective-permute-start.3 = (f32[48,2048]{1,0:T(8,128)}, f32[48,2048]{1,0:T(8,128)S(1)}, u32[]{:S(2)}, u32[]{:S(2)}) collective-permute-start(f32[48,2048]{1,0:T(8,128)} %direction.3), channel_id=1, source_target_pairs={{1,2},{3,4},{5,6},{7,8},{9,10},{11,12},{13,14},{15,16},{17,18},{19... | collective-permute-start | bytes 1179656 | tf_op jit(solution)/shard_map/ppermute | solution.py:213
  1.5 7.7 %collective-permute-start.2 = (f32[48,2048]{1,0:T(8,128)}, f32[48,2048]{1,0:T(8,128)S(1)}, u32[]{:S(2)}, u32[]{:S(2)}) collective-permute-start(f32[48,2048]{1,0:T(8,128)} %direction.3), channel_id=1, source_target_pairs={{0,1},{1,0},{2,3},{3,2},{4,5},{5,4},{6,7},{7,6},{8,9},{9,8},{10,11... | collective-permute-start | bytes 1179656 | tf_op jit(solution)/shard_map/ppermute | solution.py:214
  8.4 6.0 %collective-permute-start = (bf16[48,3712]{1,0:T(8,128)(2,1)S(1)}, bf16[48,3712]{1,0:T(8,128)(2,1)S(1)}, u32[]{:S(2)}, u32[]{:S(2)}) collective-permute-start(bf16[48,3712]{1,0:T(8,128)(2,1)S(1)} %get-tuple-element.16), channel_id=1, source_target_pairs={{0,1},{1,0},{2,3},{3,2},{4,5},{5,4},{6,7},{7,6},{8,9},{9,8},{10,11... | collective-permute-start | bytes 1069064 | tf_op jit(solution)/shard_map/ppermute | solution.py:248
  8.5 5.9 %collective-permute-start.1 = (bf16[48,3712]{1,0:T(8,128)(2,1)S(1)}, bf16[48,3712]{1,0:T(8,128)(2,1)S(1)}, u32[]{:S(2)}, u32[]{:S(2)}) collective-permute-start(bf16[48,3712]{1,0:T(8,128)(2,1)S(1)} %get-tuple-element.17), channel_id=1, source_target_pairs={{1,2},{3,4},{5,6},{7,8},{9,10},{11,12},{13,14},{15,16},{17,18},{19... | collective-permute-start | bytes 1069064 | tf_op jit(solution)/shard_map/ppermute | solution.py:247
  14.4 29.2 %copy-start.1 = (f32[48,2048]{1,0:T(8,128)S(1)}, f32[48,2048]{1,0:T(8,128)}, u32[]{:S(2)}) copy-start(f32[48,2048]{1,0:T(8,128)} %solution.1) | copy-start | bytes 1179652
  14.4 29.2 %copy-start.3 = (s32[16]{0:T(128)S(1)}, s32[16]{0:T(128)}, u32[]{:S(2)}) copy-start(s32[16]{0:T(128)} %offsets.1) | copy-start | bytes 196
  19.6 6.2 %collective-permute-start.6 = (f32[8,128]{1,0:T(8,128)S(1)}, f32[8,128]{1,0:T(8,128)S(1)}, u32[]{:S(2)}, u32[]{:S(2)}) collective-permute-start(f32[8,128]{1,0:T(8,128)S(1)} %get-tuple-element.22), channel_id=1, source_target_pairs={{0,3},{1,2},{2,1},{3,0},{4,7},{5,6},{6,5},{7,4},{8,11},{9,10},{10,... | collective-permute-start | bytes 12296 | tf_op jit(solution)/shard_map/ppermute | solution.py:192
  24.4 3.6 %collective-permute-start.5 = (f32[8,128]{1,0:T(8,128)S(1)}, f32[8,128]{1,0:T(8,128)S(1)}, u32[]{:S(2)}, u32[]{:S(2)}) collective-permute-start(f32[8,128]{1,0:T(8,128)S(1)} %get-tuple-element.22), channel_id=1, source_target_pairs={{0,2},{1,3},{2,0},{3,1},{4,6},{5,7},{6,4},{7,5},{8,10},{9,11},{10,... | collective-permute-start | bytes 12296 | tf_op jit(solution)/shard_map/ppermute | solution.py:192
  24.6 3.5 %collective-permute-start.4 = (f32[8,128]{1,0:T(8,128)S(1)}, f32[8,128]{1,0:T(8,128)S(1)}, u32[]{:S(2)}, u32[]{:S(2)}) collective-permute-start(f32[8,128]{1,0:T(8,128)S(1)} %get-tuple-element.22), channel_id=1, source_target_pairs={{0,1},{1,0},{2,3},{3,2},{4,5},{5,4},{6,7},{7,6},{8,9},{9,8},{10,11... | collective-permute-start | bytes 12296 | tf_op jit(solution)/shard_map/ppermute | solution.py:192
  28.0 6.8 %collective-permute-start.9 = (f32[8,128]{1,0:T(8,128)S(1)}, f32[8,128]{1,0:T(8,128)S(1)}, u32[]{:S(2)}, u32[]{:S(2)}) collective-permute-start(f32[8,128]{1,0:T(8,128)S(1)} %add_add_fusion.1), channel_id=1, source_target_pairs={{0,24},{1,25},{2,26},{3,27},{4,28},{5,29},{6,30},{7,31},{8,16},{9,... | collective-permute-start | bytes 12296 | tf_op jit(solution)/shard_map/ppermute | solution.py:192
  33.3 5.1 %collective-permute-start.8 = (f32[8,128]{1,0:T(8,128)S(1)}, f32[8,128]{1,0:T(8,128)S(1)}, u32[]{:S(2)}, u32[]{:S(2)}) collective-permute-start(f32[8,128]{1,0:T(8,128)S(1)} %add_add_fusion.1), channel_id=1, source_target_pairs={{0,16},{1,17},{2,18},{3,19},{4,20},{5,21},{6,22},{7,23},{8,24},{9,... | collective-permute-start | bytes 12296 | tf_op jit(solution)/shard_map/ppermute | solution.py:192
  33.8 4.6 %collective-permute-start.7 = (f32[8,128]{1,0:T(8,128)S(1)}, f32[8,128]{1,0:T(8,128)S(1)}, u32[]{:S(2)}, u32[]{:S(2)}) collective-permute-start(f32[8,128]{1,0:T(8,128)S(1)} %add_add_fusion.1), channel_id=1, source_target_pairs={{0,8},{1,9},{2,10},{3,11},{4,12},{5,13},{6,14},{7,15},{8,0},{9,1},... | collective-permute-start | bytes 12296 | tf_op jit(solution)/shard_map/ppermute | solution.py:192
  38.4 5.2 %collective-permute-start.10 = (f32[8,128]{1,0:T(8,128)S(1)}, f32[8,128]{1,0:T(8,128)S(1)}, u32[]{:S(2)}, u32[]{:S(2)}) collective-permute-start(f32[8,128]{1,0:T(8,128)S(1)} %add_add_fusion), channel_id=1, source_target_pairs={{0,4},{1,5},{2,6},{3,7},{4,0},{5,1},{6,2},{7,3},{8,12},{9,13},{10,... | collective-permute-start | bytes 12296 | tf_op jit(solution)/shard_map/ppermute | solution.py:192

commit v5 on v4

--- a/solution.py
+++ b/solution.py
@@ -1,3 +1,5 @@
+import functools
+
 import jax
 import jax.numpy as jnp
 from jax import lax
@@ -8,6 +10,8 @@
 ANGLES = 4
 LANES = 128
 CHUNK = 512
+ROUNDS = ((1, 2, 3), (8, 16, 24), (4,))
+GROUPS = ((0,), (1,), (2, 3))
 F32 = jnp.float32
 BF16 = jnp.bfloat16
 MIB = 1 << 20
@@ -33,8 +37,9 @@
     return jnp.sum(total, axis=0, keepdims=True)
 
 
-def sum_residuals(offsets_hbm, residual_hbm, tiles_hbm, own, to_pair, to_cross, residual, tile,
-                  rows, offsets, sem, offsets_sem, tile_sem):
+def sum_residuals(offsets_hbm, residual_hbm, tiles_hbm, direction_hbm, own, to_pair, to_cross,
+                  residual, tile, half, rows, offsets, direction, sem, offsets_sem, tile_sem,
+                  direction_sem):
     views, detector_rows, columns = residual.shape
     slab_rows = own.shape[0]
     near = 3 * slab_rows
@@ -47,6 +52,8 @@
     offsets_copy.start()
     for v in range(views):
         copy(v).start()
+    direction_copy = pltpu.make_async_copy(direction_hbm, direction, direction_sem)
+    direction_copy.start()
     tile_copy = pltpu.make_async_copy(tiles_hbm.at[0], tile, tile_sem)
     tile_copy.start()
     above = pair_is_above()
@@ -76,36 +83,42 @@
         to_pair[:, cut] = rows[k, pl.ds(pair_row, slab_rows), :].astype(BF16)
         to_cross[:, cut] = rows[k, pl.ds(cross_row, slab_rows), :].astype(BF16)
         own[:, cut] = rows[k, slab_rows : 2 * slab_rows, :]
+    direction_copy.wait()
+    half[...] = direction[...].astype(BF16)
     tile_copy.wait()
 
 
-def project_planes(direction, from_pair, from_cross, gradient, tile, tiles_hbm, planes, grad_sums,
-                   tiles, near, sem):
-    slab_rows = direction.shape[0]
-    columns = tile.shape[1]
+def project_own(half, gradient, tile, tiles_hbm, images, grad_sums, tiles, sem):
     copies = [
         pltpu.make_async_copy(tiles_hbm.at[a], tiles.at[a - 1], sem.at[a - 1])
         for a in range(1, ANGLES)
     ]
     for c in copies:
         c.start()
+    grad_sums[...] = lane_sums(gradient[...] * gradient[...])
+    images[0] = jnp.dot(half[...], tile[...], preferred_element_type=F32)
+    for a in range(1, ANGLES):
+        copies[a - 1].wait()
+        images[a] = jnp.dot(half[...], tiles[a - 1], preferred_element_type=F32)
+
+
+def project_near(angles, after, half, from_pair, from_cross, tile, tiles, planes, near):
+    del after
+    slab_rows = half.shape[0]
     above = pair_is_above()
     pair_row = pl.multiple_of(jnp.where(above, 2 * slab_rows, 0), 16)
     cross_row = pl.multiple_of(jnp.where(above, 0, 2 * slab_rows), 16)
-    near[pl.ds(slab_rows, slab_rows), :] = direction[...].astype(BF16)
-    near[pl.ds(pair_row, slab_rows), :] = from_pair[...].astype(BF16)
-    near[pl.ds(cross_row, slab_rows), :] = from_cross[...].astype(BF16)
-    grad_sums[...] = lane_sums(gradient[...] * gradient[...])
-    for a in range(ANGLES):
-        weights = tile if a == 0 else tiles.at[a - 1]
-        if a > 0:
-            copies[a - 1].wait()
-        image = jnp.dot(near[...], weights[...], preferred_element_type=F32)
-        for j in range(columns // LANES):
-            planes[a, j] = image[:, j * LANES : (j + 1) * LANES]
-
-
-def combine(own, from_pair, from_cross, tile, tiles, planes, grad_sums, residual_part, image_part,
+    near[pl.ds(slab_rows, slab_rows), :] = half[...]
+    near[pl.ds(pair_row, slab_rows), :] = from_pair[...]
+    near[pl.ds(cross_row, slab_rows), :] = from_cross[...]
+    for k, a in enumerate(angles):
+        weights = tile[...] if a == 0 else tiles[a - 1]
+        image = jnp.dot(near[...], weights, preferred_element_type=F32)
+        for j in range(image.shape[1] // LANES):
+            planes[k, j] = image[:, j * LANES : (j + 1) * LANES]
+
+
+def combine(own, from_pair, from_cross, tile, tiles, images, grad_sums, residual_part, image_part,
             sums):
     slab_rows = own.shape[0]
     cells, columns = tile.shape
@@ -118,9 +131,7 @@
     image_norm = zero
     for a in range(ANGLES):
         rows = gathered(slice(a * columns, (a + 1) * columns))
-        image = jnp.concatenate(
-            [planes[a, j, slab_rows : 2 * slab_rows, :] for j in range(columns // LANES)], axis=1
-        )
+        image = images[a]
         weighted = counts[:, a : a + 1] * image
         image_norm = image_norm + lane_sums(weighted * image)
         both = jnp.concatenate([*split(rows), *split(weighted)], axis=0)
@@ -148,7 +159,15 @@
     )
 
 
-def finish(offsets, sums, solution, direction, residual_part, image_part, planes, residual,
+def finish(offsets, sums, solution, direction, residual_part, image_part, *refs):
+    finish_planes(
+        offsets, sums, solution, direction, residual_part, image_part,
+        [refs[g].at[k] for g, angles in enumerate(GROUPS) for k in range(len(angles))],
+        *refs[len(GROUPS) :],
+    )
+
+
+def finish_planes(offsets, sums, solution, direction, residual_part, image_part, planes, residual,
            solution_hbm, residual_hbm, gradient_hbm, direction_hbm, updated, small, sem, small_sem):
     views, detector_rows, columns = residual.shape
     slab_rows = solution.shape[0]
@@ -177,7 +196,7 @@
         for j in range(columns // LANES):
             cut = slice(j * LANES, (j + 1) * LANES)
             updated[v, :, cut] = (
-                residual[v, :, cut] - step * planes[v % ANGLES, j, pl.ds(first, detector_rows), :]
+                residual[v, :, cut] - step * planes[v % ANGLES][j, pl.ds(first, detector_rows), :]
             )
         out_copy(v).start()
     for c in small_copies:
@@ -186,12 +205,11 @@
         out_copy(v).wait()
 
 
-def summed_over_slabs(x):
+def exchanged_sum(x, masks):
     count = lax.axis_size("slab")
-    for masks in ((1, 2, 3), (8, 16, 24), (4,)):
-        terms = [lax.ppermute(x, "slab", [(i, i ^ m) for i in range(count)]) for m in masks]
-        for term in terms:
-            x = x + term
+    terms = [lax.ppermute(x, "slab", [(i, i ^ m) for i in range(count)]) for m in masks]
+    for term in terms:
+        x = x + term
     return x
 
 
@@ -210,27 +228,27 @@
     hbm = pl.BlockSpec(memory_space=pltpu.HBM)
     sds = jax.ShapeDtypeStruct
 
-    direction_cross = lax.ppermute(direction, "slab", cross)
-    direction_pair = lax.ppermute(direction, "slab", pair)
-
     wide = ANGLES * columns + LANES
     tiles = pltpu.with_memory_space_constraint(tiles, pltpu.HBM)
-    own, to_pair, to_cross, residual_here, tile = pl.pallas_call(
+    own, to_pair, to_cross, residual_here, tile, half = pl.pallas_call(
         sum_residuals,
         name="sum_residuals",
-        in_specs=[hbm] * 3,
-        out_specs=[vmem] * 5,
+        in_specs=[hbm] * 4,
+        out_specs=[vmem] * 6,
         out_shape=[
             sds((slab_rows, wide), F32),
             sds((slab_rows, wide), BF16),
             sds((slab_rows, wide), BF16),
             pltpu.VMEM(residual.shape, F32),
             pltpu.VMEM(tiles.shape[1:], BF16),
+            sds((slab_rows, cells), BF16),
         ],
         scratch_shapes=[
             pltpu.VMEM((wide // LANES, near, LANES), F32),
             pltpu.SMEM(offsets.shape, jnp.int32),
+            pltpu.VMEM((slab_rows, cells), F32),
             pltpu.SemaphoreType.DMA((views,)),
+            pltpu.SemaphoreType.DMA,
             pltpu.SemaphoreType.DMA,
             pltpu.SemaphoreType.DMA,
         ],
@@ -242,30 +260,30 @@
         pltpu.with_memory_space_constraint(offsets, pltpu.HBM),
         pltpu.with_memory_space_constraint(residual, pltpu.HBM),
         tiles,
+        pltpu.with_memory_space_constraint(direction, pltpu.HBM),
     )
 
     from_cross = lax.ppermute(to_cross, "slab", cross)
     from_pair = lax.ppermute(to_pair, "slab", pair)
-
-    planes, grad_sums, tiles_here = pl.pallas_call(
-        project_planes,
-        name="project_planes",
-        in_specs=[vmem] * 5 + [hbm],
+    half_cross = lax.ppermute(half, "slab", cross)
+    half_pair = lax.ppermute(half, "slab", pair)
+
+    images, grad_sums, tiles_here = pl.pallas_call(
+        project_own,
+        name="project_own",
+        in_specs=[vmem] * 3 + [hbm],
         out_specs=[vmem] * 3,
         out_shape=[
-            sds((ANGLES, blocks, near, LANES), F32),
+            sds((ANGLES, slab_rows, columns), F32),
             sds((1, LANES), F32),
             pltpu.VMEM((ANGLES - 1, *tiles.shape[1:]), BF16),
         ],
-        scratch_shapes=[
-            pltpu.VMEM((near, cells), BF16),
-            pltpu.SemaphoreType.DMA((ANGLES - 1,)),
-        ],
+        scratch_shapes=[pltpu.SemaphoreType.DMA((ANGLES - 1,))],
         compiler_params=pltpu.CompilerParams(vmem_limit_bytes=8 * MIB),
         cost_estimate=pl.CostEstimate(
             flops=2 * near * cells * columns * ANGLES, bytes_accessed=16 * MIB, transcendentals=0
         ),
-    )(direction, direction_pair, direction_cross, gradient, tile, tiles)
+    )(half, gradient, tile, tiles)
 
     residual_part, image_part, sums = pl.pallas_call(
         combine,
@@ -278,14 +296,32 @@
             sds((8, LANES), F32),
         ],
         compiler_params=pltpu.CompilerParams(vmem_limit_bytes=8 * MIB),
-    )(own, from_pair, from_cross, tile, tiles_here, planes, grad_sums)
-
-    sums = summed_over_slabs(sums)
+    )(own, from_pair, from_cross, tile, tiles_here, images, grad_sums)
+
+    planes = []
+    for masks, angles in zip(ROUNDS, GROUPS):
+        planes.append(
+            pl.pallas_call(
+                functools.partial(project_near, angles),
+                name="project_near",
+                in_specs=[vmem] * 6,
+                out_specs=vmem,
+                out_shape=sds((len(angles), blocks, near, LANES), F32),
+                scratch_shapes=[pltpu.VMEM((near, cells), BF16)],
+                compiler_params=pltpu.CompilerParams(vmem_limit_bytes=6 * MIB),
+                cost_estimate=pl.CostEstimate(
+                    flops=2 * near * cells * columns * len(angles),
+                    bytes_accessed=MIB,
+                    transcendentals=0,
+                ),
+            )(sums, half, half_pair, half_cross, tile, tiles_here)
+        )
+        sums = exchanged_sum(sums, masks)
 
     return pl.pallas_call(
         finish,
         name="finish",
-        in_specs=[smem] + [vmem] * 7,
+        in_specs=[smem] + [vmem] * 9,
         out_specs=[hbm] * 4,
         out_shape=[
             sds(solution.shape, F32),
@@ -300,7 +336,7 @@
             pltpu.SemaphoreType.DMA((3,)),
         ],
         compiler_params=pltpu.CompilerParams(vmem_limit_bytes=12 * MIB),
-    )(offsets, sums, solution, direction, residual_part, image_part, planes, residual_here)
+    )(offsets, sums, solution, direction, residual_part, image_part, *planes, residual_here)
 
 
 def solution(mesh):

time: 46.8 us -> 44.7 us (0.955)
  waiting for transfers between devices: 12 us -> 5.54 us
  Pallas kernels: 16.9 us -> 20.6 us
    ppermute x9, waiting for transfers between devices: 12 us -> 5.53 us  [the longest x7 5.53 us: exchanged_sum(): lax.ppermute(x, 'slab', [(i, i ^ m) for i in range(count)])]
    pallas_call x3 -> x6, Pallas kernels: 11.7 us -> 15.5 us  [the longest x1 5.65 us: local(): pl.pallas_call(project_own, name='project_own', in_specs=[vmem] * 3 + [hb...]
    ppermute x9, starting transfers between devices: 16.3 us -> 16.8 us  [the longest x7 12.7 us: exchanged_sum(): lax.ppermute(x, 'slab', [(i, i ^ m) for i in range(count)])]
  transfers between devices with their start and end apart: 11 -> 11, of which waited for: 5 -> 4; matrix products, arithmetic and copies ran while one was open for 0% -> 0% of each run, Pallas kernels for 18% -> 31%
where the time goes in v5:
time: 44.7 us; the launch traced here: 44.5 us
  Pallas kernels  20.6 us (46%)
  starting transfers between devices  17.5 us (39%)
  waiting for transfers between devices  5.54 us (12%)
  between operations  0.78 us (2%)
    ppermute x7, starting transfers between devices, exchanged_sum(): lax.ppermute(x, 'slab', [(i, i ^ m) for i in range(count)])  12.7 us
    pallas_call x1, Pallas kernels, local(): pl.pallas_call(project_own, name='project_own', in_specs=[vmem] * 3 + [hb...  5.65 us
    ppermute x7, waiting for transfers between devices, exchanged_sum(): lax.ppermute(x, 'slab', [(i, i ^ m) for i in range(count)])  5.53 us
    pallas_call x1, Pallas kernels, local(): pl.pallas_call(combine, name='combine', in_specs=[vmem] * 7, out_specs=[v...  5.17 us
    pallas_call x1, Pallas kernels, local(): pl.pallas_call(sum_residuals, name='sum_residuals', in_specs=[hbm] * 4, o...  3.64 us
    ppermute x1, starting transfers between devices, local(): half_pair = lax.ppermute(half, 'slab', pair)  3.42 us
    pallas_call x1, Pallas kernels, local(): pl.pallas_call(finish, name='finish', in_specs=[smem] + [vmem] * 9, out_s...  3.1 us
    pallas_call x3, Pallas kernels, local(): pl.pallas_call(functools.partial(project_near, angles), name='project_nea...  3.07 us
  transfers between devices with their start and end apart: 11, of which 4 were waited for; matrix products, arithmetic and copies ran while one was open for 0% of the time, Pallas kernels for 31%

profile of v5, /device:TPU:0, one launch (start us, length us, event | category | flops | bytes accessed | tf_op | source)
XLA Modules:
  0.0 44.5 jit_solution(11950942139502112811)
XLA Ops:
  0.6 0.0 copy-start.2
  0.6 3.6 %sum_residuals.1 = (f32[48,3712]{1,0:T(8,128)S(1)}, bf16[48,3712]{1,0:T(8,128)(2,1)S(1)}, bf16[48,3712]{1,0:T(8,128)(2,1)S(1)}, f32[16,64,896]{2,1,0:T(8,128)S(1...) custom-call(s32[16]{0:T(128)} %offsets.1, f32[16,64,896]{2,1,0:T(8,128)} %residual_hbm.1, ...), custom_call_target="tpu_custom_call" | custom-call | flops 917504 | bytes 3670016 | tf_op jit(solution)/shard_map/sum_residuals/pallas_call | solution.py:233
  4.3 0.1 collective-permute-start
  4.4 0.7 %collective-permute-start.1 = (bf16[48,3712]{1,0:T(8,128)(2,1)S(1)}, bf16[48,3712]{1,0:T(8,128)(2,1)S(1)}, u32[]{:S(2)}, u32[]{:S(2)}) collective-permute-start(bf16[48,3712]{1,0:T(8,128)(2,1)S(1)} %get-tuple-element.18), channel_id=1, source_target_pairs={{1,2},{3,4},{5,6},{7,8},{9,10},{11,12},{13,14},{15,16},{17,18},{19... | collective-permute-start | bytes 1069064 | tf_op jit(solution)/shard_map/ppermute | solution.py:266
  5.1 3.4 %collective-permute-start.9 = (bf16[48,2048]{1,0:T(8,128)(2,1)S(1)}, bf16[48,2048]{1,0:T(8,128)(2,1)S(1)}, u32[]{:S(2)}, u32[]{:S(2)}) collective-permute-start(bf16[48,2048]{1,0:T(8,128)(2,1)S(1)} %get-tuple-element.20.half), channel_id=1, source_target_pairs={{0,1},{1,0},{2,3},{3,2},{4,5},{5,4},{6,7},{7,6},{8,9},{9,8},{10,11... | collective-permute-start | bytes 589832 | tf_op jit(solution)/shard_map/ppermute | solution.py:269
  8.5 0.7 %collective-permute-start.10 = (bf16[48,2048]{1,0:T(8,128)(2,1)S(1)}, bf16[48,2048]{1,0:T(8,128)(2,1)S(1)}, u32[]{:S(2)}, u32[]{:S(2)}) collective-permute-start(bf16[48,2048]{1,0:T(8,128)(2,1)S(1)} %get-tuple-element.20.half), channel_id=1, source_target_pairs={{1,2},{3,4},{5,6},{7,8},{9,10},{11,12},{13,14},{15,16},{17,18},{19... | collective-permute-start | bytes 589832 | tf_op jit(solution)/shard_map/ppermute | solution.py:268
  9.2 0.0 copy-done.2
  9.2 5.6 %project_own.1 = (f32[4,48,896]{2,1,0:T(8,128)S(1)}, f32[1,128]{1,0:T(1,128)S(1)}, bf16[3,2048,896]{2,1,0:T(8,128)(2,1)S(1)}) custom-call(bf16[48,2048]{1,0:T(8,128)(2,1)S(1)} %get-tuple-element.20.half, f32[48,2048]{1,0:T(8,128)S(1)} %copy-done.2, bf16[2048,896]{1,0:T(8,128)(2,1)S(1)} %get-tuple-element.19.tile, bf16[4,2048,896]{2,1,0:T(8,128)(2,1)} %tiles_hbm.3), custom_call_target="tpu_custom_call" | custom-call | flops 2113929216 | bytes 16777216 | tf_op jit(solution)/shard_map/project_own/pallas_call | solution.py:271
  14.8 0.0 collective-permute-done.from_pair
  14.8 0.0 collective-permute-done.1.from_cross
  14.8 5.2 %combine.1 = (f32[48,2048]{1,0:T(8,128)S(1)}, f32[48,2048]{1,0:T(8,128)S(1)}, f32[8,128]{1,0:T(8,128)S(1)}) custom-call(f32[48,3712]{1,0:T(8,128)S(1)} %get-tuple-element.16.own, bf16[48,3712]{1,0:T(8,128)(2,1)S(1)} %collective-permute-done.from_pair, bf16[48,3712]{1,0:T(8,128)(2,1)S(1)} %collective-permute-done.1.from_cross, ...), custom_call_target="tpu_custom_call" | custom-call | tf_op jit(solution)/shard_map/combine/pallas_call | solution.py:288
  20.0 4.6 %collective-permute-start.4 = (f32[8,128]{1,0:T(8,128)S(1)}, f32[8,128]{1,0:T(8,128)S(1)}, u32[]{:S(2)}, u32[]{:S(2)}) collective-permute-start(f32[8,128]{1,0:T(8,128)S(1)} %get-tuple-element.24.after), channel_id=1, source_target_pairs={{0,3},{1,2},{2,1},{3,0},{4,7},{5,6},{6,5},{7,4},{8,11},{9,10},{10,... | collective-permute-start | bytes 12296 | tf_op jit(solution)/shard_map/ppermute | solution.py:210
  24.6 0.4 collective-permute-start.3
  25.0 0.0 collective-permute-start.2
  25.0 0.0 collective-permute-done.9.from_pair
  25.0 0.0 collective-permute-done.10.from_cross
  25.0 0.8 %project_near.3.refs_0_ = f32[1,7,144,128]{3,2,1,0:T(8,128)S(1)} custom-call(f32[8,128]{1,0:T(8,128)S(1)} %get-tuple-element.24.after, bf16[48,2048]{1,0:T(8,128)(2,1)S(1)} %get-tuple-element.20.half, bf16[48,2048]{1,0:T(8,128)(2,1)S(1)} %collective-permute-done.9.from_pair, bf16[48,2048]{1,0:T(8,128)(2,1)S(1)} %collective-permute-done.10.from_cross, ...), custom_call_target="tpu_custom_call" | custom-call | flops 528482304 | bytes 1048576 | tf_op jit(solution)/shard_map/project_near/pallas_call | solution.py:304
  25.8 0.1 collective-permute-done.4
  25.9 2.3 %collective-permute-done.3 = f32[8,128]{1,0:T(8,128)S(1)} collective-permute-done((f32[8,128]{1,0:T(8,128)S(1)}, f32[8,128]{1,0:T(8,128)S(1)}, u32[]{:S(2)}, u32[]{:S(2)}) %collective-permute-start.3) | collective-permute-done | bytes 4128 | tf_op jit(solution)/shard_map/ppermute | solution.py:210
  28.2 0.0 collective-permute-done.2
  28.2 2.8 %collective-permute-start.7 = (f32[8,128]{1,0:T(8,128)S(1)}, f32[8,128]{1,0:T(8,128)S(1)}, u32[]{:S(2)}, u32[]{:S(2)}) collective-permute-start(f32[8,128]{1,0:T(8,128)S(1)} %add_add_fusion.1.after), channel_id=1, source_target_pairs={{0,24},{1,25},{2,26},{3,27},{4,28},{5,29},{6,30},{7,31},{8,16},{9,... | collective-permute-start | bytes 12296 | tf_op jit(solution)/shard_map/ppermute | solution.py:210
  31.1 0.8 %collective-permute-start.6 = (f32[8,128]{1,0:T(8,128)S(1)}, f32[8,128]{1,0:T(8,128)S(1)}, u32[]{:S(2)}, u32[]{:S(2)}) collective-permute-start(f32[8,128]{1,0:T(8,128)S(1)} %add_add_fusion.1.after), channel_id=1, source_target_pairs={{0,16},{1,17},{2,18},{3,19},{4,20},{5,21},{6,22},{7,23},{8,24},{9,... | collective-permute-start | bytes 12296 | tf_op jit(solution)/shard_map/ppermute | solution.py:210
  31.8 0.5 %collective-permute-start.5 = (f32[8,128]{1,0:T(8,128)S(1)}, f32[8,128]{1,0:T(8,128)S(1)}, u32[]{:S(2)}, u32[]{:S(2)}) collective-permute-start(f32[8,128]{1,0:T(8,128)S(1)} %add_add_fusion.1.after), channel_id=1, source_target_pairs={{0,8},{1,9},{2,10},{3,11},{4,12},{5,13},{6,14},{7,15},{8,0},{9,1},... | collective-permute-start | bytes 12296 | tf_op jit(solution)/shard_map/ppermute | solution.py:210
  32.4 0.8 %project_near.4.refs_1_ = f32[1,7,144,128]{3,2,1,0:T(8,128)S(1)} custom-call(f32[8,128]{1,0:T(8,128)S(1)} %add_add_fusion.1.after, bf16[48,2048]{1,0:T(8,128)(2,1)S(1)} %get-tuple-element.20.half, bf16[48,2048]{1,0:T(8,128)(2,1)S(1)} %collective-permute-done.9.from_pair, bf16[48,2048]{1,0:T(8,128)(2,1)S(1)} %collective-permute-done.10.from_cross, ...), custom_call_target="tpu_custom_call" | custom-call | flops 528482304 | bytes 1048576 | tf_op jit(solution)/shard_map/project_near/pallas_call | solution.py:304
  33.2 0.0 collective-permute-done.7
  33.2 2.9 %collective-permute-done.6 = f32[8,128]{1,0:T(8,128)S(1)} collective-permute-done((f32[8,128]{1,0:T(8,128)S(1)}, f32[8,128]{1,0:T(8,128)S(1)}, u32[]{:S(2)}, u32[]{:S(2)}) %collective-permute-start.6) | collective-permute-done | bytes 4128 | tf_op jit(solution)/shard_map/ppermute | solution.py:210
  36.2 0.0 collective-permute-done.5
  36.2 0.0 copy-start
  36.2 0.0 copy-start.1
  36.2 0.0 copy-start.3
  36.2 3.5 %collective-permute-start.8 = (f32[8,128]{1,0:T(8,128)S(1)}, f32[8,128]{1,0:T(8,128)S(1)}, u32[]{:S(2)}, u32[]{:S(2)}) collective-permute-start(f32[8,128]{1,0:T(8,128)S(1)} %add_add_fusion.after), channel_id=1, source_target_pairs={{0,4},{1,5},{2,6},{3,7},{4,0},{5,1},{6,2},{7,3},{8,12},{9,13},{10,... | collective-permute-start | bytes 12296 | tf_op jit(solution)/shard_map/ppermute | solution.py:210
  39.7 1.5 %project_near.5.refs_2_ = f32[2,7,144,128]{3,2,1,0:T(8,128)S(1)} custom-call(f32[8,128]{1,0:T(8,128)S(1)} %add_add_fusion.after, bf16[48,2048]{1,0:T(8,128)(2,1)S(1)} %get-tuple-element.20.half, bf16[48,2048]{1,0:T(8,128)(2,1)S(1)} %collective-permute-done.9.from_pair, bf16[48,2048]{1,0:T(8,128)(2,1)S(1)} %collective-permute-done.10.from_cross, ...), custom_call_target="tpu_custom_call" | custom-call | flops 1056964608 | bytes 1048576 | tf_op jit(solution)/shard_map/project_near/pallas_call | solution.py:304
  41.2 0.2 collective-permute-done.8
  41.4 0.0 copy-done
  41.4 0.0 copy-done.1
  41.4 0.0 copy-done.3
  41.4 3.1 %finish.1 = (f32[48,2048]{1,0:T(8,128)}, f32[16,64,896]{2,1,0:T(8,128)}, f32[48,2048]{1,0:T(8,128)}, f32[48,2048]{1,0:T(8,128)}) custom-call(s32[16]{0:T(128)S(1)} %copy-done.3, f32[8,128]{1,0:T(8,128)S(1)} %add.27.sums, f32[48,2048]{1,0:T(8,128)S(1)} %copy-done.1, f32[48,2048]{1,0:T(8,128)S(1)} %copy-done, f32[48,2048]{1,0:T(8,128)S(1)} %get-tuple-element.25.residual_part, ...), custom_call_target="tpu_custom_call" | custom-call | tf_op jit(solution)/shard_map/finish/pallas_call | solution.py:321
  (3 shorter events, 0.0 us)
Async XLA Ops:
  0.6 8.5 %copy-start.2 = (f32[48,2048]{1,0:T(8,128)S(1)}, f32[48,2048]{1,0:T(8,128)}, u32[]{:S(2)}) copy-start(f32[48,2048]{1,0:T(8,128)} %gradient.1) | copy-start | bytes 1179652
  4.3 10.5 %collective-permute-start = (bf16[48,3712]{1,0:T(8,128)(2,1)S(1)}, bf16[48,3712]{1,0:T(8,128)(2,1)S(1)}, u32[]{:S(2)}, u32[]{:S(2)}) collective-permute-start(bf16[48,3712]{1,0:T(8,128)(2,1)S(1)} %get-tuple-element.17), channel_id=1, source_target_pairs={{0,1},{1,0},{2,3},{3,2},{4,5},{5,4},{6,7},{7,6},{8,9},{9,8},{10,11... | collective-permute-start | bytes 1069064 | tf_op jit(solution)/shard_map/ppermute | solution.py:267
  4.4 10.5 %collective-permute-start.1 = (bf16[48,3712]{1,0:T(8,128)(2,1)S(1)}, bf16[48,3712]{1,0:T(8,128)(2,1)S(1)}, u32[]{:S(2)}, u32[]{:S(2)}) collective-permute-start(bf16[48,3712]{1,0:T(8,128)(2,1)S(1)} %get-tuple-element.18), channel_id=1, source_target_pairs={{1,2},{3,4},{5,6},{7,8},{9,10},{11,12},{13,14},{15,16},{17,18},{19... | collective-permute-start | bytes 1069064 | tf_op jit(solution)/shard_map/ppermute | solution.py:266
  5.1 19.9 %collective-permute-start.9 = (bf16[48,2048]{1,0:T(8,128)(2,1)S(1)}, bf16[48,2048]{1,0:T(8,128)(2,1)S(1)}, u32[]{:S(2)}, u32[]{:S(2)}) collective-permute-start(bf16[48,2048]{1,0:T(8,128)(2,1)S(1)} %get-tuple-element.20.half), channel_id=1, source_target_pairs={{0,1},{1,0},{2,3},{3,2},{4,5},{5,4},{6,7},{7,6},{8,9},{9,8},{10,11... | collective-permute-start | bytes 589832 | tf_op jit(solution)/shard_map/ppermute | solution.py:269
  8.5 16.5 %collective-permute-start.10 = (bf16[48,2048]{1,0:T(8,128)(2,1)S(1)}, bf16[48,2048]{1,0:T(8,128)(2,1)S(1)}, u32[]{:S(2)}, u32[]{:S(2)}) collective-permute-start(bf16[48,2048]{1,0:T(8,128)(2,1)S(1)} %get-tuple-element.20.half), channel_id=1, source_target_pairs={{1,2},{3,4},{5,6},{7,8},{9,10},{11,12},{13,14},{15,16},{17,18},{19... | collective-permute-start | bytes 589832 | tf_op jit(solution)/shard_map/ppermute | solution.py:268
  20.0 5.9 %collective-permute-start.4 = (f32[8,128]{1,0:T(8,128)S(1)}, f32[8,128]{1,0:T(8,128)S(1)}, u32[]{:S(2)}, u32[]{:S(2)}) collective-permute-start(f32[8,128]{1,0:T(8,128)S(1)} %get-tuple-element.24.after), channel_id=1, source_target_pairs={{0,3},{1,2},{2,1},{3,0},{4,7},{5,6},{6,5},{7,4},{8,11},{9,10},{10,... | collective-permute-start | bytes 12296 | tf_op jit(solution)/shard_map/ppermute | solution.py:210
  24.6 3.6 %collective-permute-start.3 = (f32[8,128]{1,0:T(8,128)S(1)}, f32[8,128]{1,0:T(8,128)S(1)}, u32[]{:S(2)}, u32[]{:S(2)}) collective-permute-start(f32[8,128]{1,0:T(8,128)S(1)} %get-tuple-element.24.after), channel_id=1, source_target_pairs={{0,2},{1,3},{2,0},{3,1},{4,6},{5,7},{6,4},{7,5},{8,10},{9,11},{10,... | collective-permute-start | bytes 12296 | tf_op jit(solution)/shard_map/ppermute | solution.py:210
  25.0 3.2 %collective-permute-start.2 = (f32[8,128]{1,0:T(8,128)S(1)}, f32[8,128]{1,0:T(8,128)S(1)}, u32[]{:S(2)}, u32[]{:S(2)}) collective-permute-start(f32[8,128]{1,0:T(8,128)S(1)} %get-tuple-element.24.after), channel_id=1, source_target_pairs={{0,1},{1,0},{2,3},{3,2},{4,5},{5,4},{6,7},{7,6},{8,9},{9,8},{10,11... | collective-permute-start | bytes 12296 | tf_op jit(solution)/shard_map/ppermute | solution.py:210
  28.2 5.0 %collective-permute-start.7 = (f32[8,128]{1,0:T(8,128)S(1)}, f32[8,128]{1,0:T(8,128)S(1)}, u32[]{:S(2)}, u32[]{:S(2)}) collective-permute-start(f32[8,128]{1,0:T(8,128)S(1)} %add_add_fusion.1.after), channel_id=1, source_target_pairs={{0,24},{1,25},{2,26},{3,27},{4,28},{5,29},{6,30},{7,31},{8,16},{9,... | collective-permute-start | bytes 12296 | tf_op jit(solution)/shard_map/ppermute | solution.py:210
  31.1 5.1 %collective-permute-start.6 = (f32[8,128]{1,0:T(8,128)S(1)}, f32[8,128]{1,0:T(8,128)S(1)}, u32[]{:S(2)}, u32[]{:S(2)}) collective-permute-start(f32[8,128]{1,0:T(8,128)S(1)} %add_add_fusion.1.after), channel_id=1, source_target_pairs={{0,16},{1,17},{2,18},{3,19},{4,20},{5,21},{6,22},{7,23},{8,24},{9,... | collective-permute-start | bytes 12296 | tf_op jit(solution)/shard_map/ppermute | solution.py:210
  31.8 4.3 %collective-permute-start.5 = (f32[8,128]{1,0:T(8,128)S(1)}, f32[8,128]{1,0:T(8,128)S(1)}, u32[]{:S(2)}, u32[]{:S(2)}) collective-permute-start(f32[8,128]{1,0:T(8,128)S(1)} %add_add_fusion.1.after), channel_id=1, source_target_pairs={{0,8},{1,9},{2,10},{3,11},{4,12},{5,13},{6,14},{7,15},{8,0},{9,1},... | collective-permute-start | bytes 12296 | tf_op jit(solution)/shard_map/ppermute | solution.py:210
  36.2 5.2 %copy-start = (f32[48,2048]{1,0:T(8,128)S(1)}, f32[48,2048]{1,0:T(8,128)}, u32[]{:S(2)}) copy-start(f32[48,2048]{1,0:T(8,128)} %direction.1) | copy-start | bytes 1179652
  36.2 5.2 %copy-start.1 = (f32[48,2048]{1,0:T(8,128)S(1)}, f32[48,2048]{1,0:T(8,128)}, u32[]{:S(2)}) copy-start(f32[48,2048]{1,0:T(8,128)} %solution.1) | copy-start | bytes 1179652
  36.2 5.2 %copy-start.3 = (s32[16]{0:T(128)S(1)}, s32[16]{0:T(128)}, u32[]{:S(2)}) copy-start(s32[16]{0:T(128)} %offsets.1) | copy-start | bytes 196
  36.2 5.2 %collective-permute-start.8 = (f32[8,128]{1,0:T(8,128)S(1)}, f32[8,128]{1,0:T(8,128)S(1)}, u32[]{:S(2)}, u32[]{:S(2)}) collective-permute-start(f32[8,128]{1,0:T(8,128)S(1)} %add_add_fusion.after), channel_id=1, source_target_pairs={{0,4},{1,5},{2,6},{3,7},{4,0},{5,1},{6,2},{7,3},{8,12},{9,13},{10,... | collective-permute-start | bytes 12296 | tf_op jit(solution)/shard_map/ppermute | solution.py:210

commit v6 on v5

--- a/solution.py
+++ b/solution.py
@@ -85,10 +85,11 @@
         own[:, cut] = rows[k, slab_rows : 2 * slab_rows, :]
     direction_copy.wait()
     half[...] = direction[...].astype(BF16)
+    to_pair[:, to_cross.shape[1] :] = half[...]
     tile_copy.wait()
 
 
-def project_own(half, gradient, tile, tiles_hbm, images, grad_sums, tiles, sem):
+def project_own(half, gradient, tile, tiles_hbm, images, grad_sums, tiles, to_cross, sem):
     copies = [
         pltpu.make_async_copy(tiles_hbm.at[a], tiles.at[a - 1], sem.at[a - 1])
         for a in range(1, ANGLES)
@@ -96,6 +97,7 @@
     for c in copies:
         c.start()
     grad_sums[...] = lane_sums(gradient[...] * gradient[...])
+    to_cross[...] = half[...]
     images[0] = jnp.dot(half[...], tile[...], preferred_element_type=F32)
     for a in range(1, ANGLES):
         copies[a - 1].wait()
@@ -109,7 +111,7 @@
     pair_row = pl.multiple_of(jnp.where(above, 2 * slab_rows, 0), 16)
     cross_row = pl.multiple_of(jnp.where(above, 0, 2 * slab_rows), 16)
     near[pl.ds(slab_rows, slab_rows), :] = half[...]
-    near[pl.ds(pair_row, slab_rows), :] = from_pair[...]
+    near[pl.ds(pair_row, slab_rows), :] = from_pair[:, from_pair.shape[1] - half.shape[1] :]
     near[pl.ds(cross_row, slab_rows), :] = from_cross[...]
     for k, a in enumerate(angles):
         weights = tile[...] if a == 0 else tiles[a - 1]
@@ -119,7 +121,7 @@
 
 
 def combine(own, from_pair, from_cross, tile, tiles, images, grad_sums, residual_part, image_part,
-            sums):
+            sums, both):
     slab_rows = own.shape[0]
     cells, columns = tile.shape
     zero = jnp.zeros((1, LANES), F32)
@@ -130,29 +132,26 @@
     counts = gathered(slice(ANGLES * columns, ANGLES * columns + LANES))
     image_norm = zero
     for a in range(ANGLES):
-        rows = gathered(slice(a * columns, (a + 1) * columns))
-        image = images[a]
-        weighted = counts[:, a : a + 1] * image
-        image_norm = image_norm + lane_sums(weighted * image)
-        both = jnp.concatenate([*split(rows), *split(weighted)], axis=0)
-        weights = tile if a == 0 else tiles.at[a - 1]
-        for b in range(0, cells, CHUNK):
-            cut = slice(b, b + CHUNK)
-            part = lax.dot_general(
-                both, weights[cut, :], (((1,), (1,)), ((), ())), preferred_element_type=F32
-            )
-            r = part[:slab_rows] + part[slab_rows : 2 * slab_rows]
-            i = part[2 * slab_rows : 3 * slab_rows] + part[3 * slab_rows :]
-            if a == 0:
-                residual_part[:, cut] = r
-                image_part[:, cut] = i
-            else:
-                residual_part[:, cut] += r
-                image_part[:, cut] += i
+        cut = slice(a * columns, (a + 1) * columns)
+        weighted = counts[:, a : a + 1] * images[a]
+        image_norm = image_norm + lane_sums(weighted * images[a])
+        for k, part in enumerate((*split(gathered(cut)), *split(weighted))):
+            both[k * slab_rows : (k + 1) * slab_rows, cut] = part
+    both[4 * slab_rows :, :] = jnp.zeros_like(both[4 * slab_rows :, :])
 
     rr, ri, ii = zero, zero, zero
     for b in range(0, cells, CHUNK):
-        r, i = residual_part[:, b : b + CHUNK], image_part[:, b : b + CHUNK]
+        cut = slice(b, b + CHUNK)
+        weights = jnp.concatenate(
+            [tile[cut, :], *(tiles[a, cut, :] for a in range(ANGLES - 1))], axis=1
+        )
+        part = lax.dot_general(
+            both[...], weights, (((1,), (1,)), ((), ())), preferred_element_type=F32
+        )
+        r = part[:slab_rows] + part[slab_rows : 2 * slab_rows]
+        i = part[2 * slab_rows : 3 * slab_rows] + part[3 * slab_rows : 4 * slab_rows]
+        residual_part[:, cut] = r
+        image_part[:, cut] = i
         rr, ri, ii = rr + lane_sums(r * r), ri + lane_sums(r * i), ii + lane_sums(i * i)
     sums[...] = jnp.concatenate(
         [grad_sums[...], image_norm, rr, ri, ii, zero, zero, zero], axis=0
@@ -237,7 +236,7 @@
         out_specs=[vmem] * 6,
         out_shape=[
             sds((slab_rows, wide), F32),
-            sds((slab_rows, wide), BF16),
+            sds((slab_rows, wide + cells), BF16),
             sds((slab_rows, wide), BF16),
             pltpu.VMEM(residual.shape, F32),
             pltpu.VMEM(tiles.shape[1:], BF16),
@@ -265,18 +264,17 @@
 
     from_cross = lax.ppermute(to_cross, "slab", cross)
     from_pair = lax.ppermute(to_pair, "slab", pair)
-    half_cross = lax.ppermute(half, "slab", cross)
-    half_pair = lax.ppermute(half, "slab", pair)
-
-    images, grad_sums, tiles_here = pl.pallas_call(
+
+    images, grad_sums, tiles_here, half_to_cross = pl.pallas_call(
         project_own,
         name="project_own",
         in_specs=[vmem] * 3 + [hbm],
-        out_specs=[vmem] * 3,
+        out_specs=[vmem] * 4,
         out_shape=[
             sds((ANGLES, slab_rows, columns), F32),
             sds((1, LANES), F32),
             pltpu.VMEM((ANGLES - 1, *tiles.shape[1:]), BF16),
+            sds((slab_rows, cells), BF16),
         ],
         scratch_shapes=[pltpu.SemaphoreType.DMA((ANGLES - 1,))],
         compiler_params=pltpu.CompilerParams(vmem_limit_bytes=8 * MIB),
@@ -284,6 +282,8 @@
             flops=2 * near * cells * columns * ANGLES, bytes_accessed=16 * MIB, transcendentals=0
         ),
     )(half, gradient, tile, tiles)
+
+    half_cross = lax.ppermute(half_to_cross, "slab", cross)
 
     residual_part, image_part, sums = pl.pallas_call(
         combine,
@@ -295,6 +295,7 @@
             sds((slab_rows, cells), F32),
             sds((8, LANES), F32),
         ],
+        scratch_shapes=[pltpu.VMEM((256, ANGLES * columns), BF16)],
         compiler_params=pltpu.CompilerParams(vmem_limit_bytes=8 * MIB),
     )(own, from_pair, from_cross, tile, tiles_here, images, grad_sums)
 
@@ -314,7 +315,7 @@
                     bytes_accessed=MIB,
                     transcendentals=0,
                 ),
-            )(sums, half, half_pair, half_cross, tile, tiles_here)
+            )(sums, half, from_pair, half_cross, tile, tiles_here)
         )
         sums = exchanged_sum(sums, masks)
 

time: 44.7 us -> 42.9 us (0.960)
  Pallas kernels: 20.6 us -> 19.1 us
  starting transfers between devices: 17.5 us -> 16.9 us
  waiting for transfers between devices: 5.54 us -> 6.03 us
    ppermute x2 -> x1, starting transfers between devices: 4.08 us -> 0.67 us  [local(): half_cross = lax.ppermute(half_to_cross, 'slab', cross)]
    ppermute x7, starting transfers between devices: 12.7 us -> 15.4 us  [exchanged_sum(): lax.ppermute(x, 'slab', [(i, i ^ m) for i in range(count)])]
    pallas_call x1, Pallas kernels: 5.17 us -> 4.21 us  [local(): pl.pallas_call(combine, name='combine', in_specs=[vmem] * 7, out_specs=[v...]
    pallas_call x1, Pallas kernels: 5.65 us -> 5.01 us  [local(): pl.pallas_call(project_own, name='project_own', in_specs=[vmem] * 3 + [hb...]
    ppermute x7, waiting for transfers between devices: 5.53 us -> 6.02 us  [exchanged_sum(): lax.ppermute(x, 'slab', [(i, i ^ m) for i in range(count)])]
  transfers between devices with their start and end apart: 11 -> 10, of which waited for: 4 -> 4; matrix products, arithmetic and copies ran while one was open for 0% -> 0% of each run, Pallas kernels for 31% -> 29%
where the time goes in v6:
time: 42.9 us; the launch traced here: 42.8 us
  Pallas kernels  19.1 us (45%)
  starting transfers between devices  16.9 us (39%)
  waiting for transfers between devices  6.03 us (14%)
  between operations  0.78 us (2%)
    ppermute x7, starting transfers between devices, exchanged_sum(): lax.ppermute(x, 'slab', [(i, i ^ m) for i in range(count)])  15.4 us
    ppermute x7, waiting for transfers between devices, exchanged_sum(): lax.ppermute(x, 'slab', [(i, i ^ m) for i in range(count)])  6.02 us
    pallas_call x1, Pallas kernels, local(): pl.pallas_call(project_own, name='project_own', in_specs=[vmem] * 3 + [hb...  5.01 us
    pallas_call x1, Pallas kernels, local(): pl.pallas_call(combine, name='combine', in_specs=[vmem] * 7, out_specs=[v...  4.21 us
    pallas_call x1, Pallas kernels, local(): pl.pallas_call(sum_residuals, name='sum_residuals', in_specs=[hbm] * 4, o...  3.64 us
    pallas_call x1, Pallas kernels, local(): pl.pallas_call(finish, name='finish', in_specs=[smem] + [vmem] * 9, out_s...  3.1 us
    pallas_call x3, Pallas kernels, local(): pl.pallas_call(functools.partial(project_near, angles), name='project_nea...  3.1 us
  transfers between devices with their start and end apart: 10, of which 4 were waited for; matrix products, arithmetic and copies ran while one was open for 0% of the time, Pallas kernels for 29%

profile of v6, /device:TPU:0, one launch (start us, length us, event | category | flops | bytes accessed | tf_op | source)
XLA Modules:
  0.0 42.8 jit_solution(7884572636250934562)
XLA Ops:
  0.6 0.0 copy-start.2
  0.6 3.6 %sum_residuals.1 = (f32[48,3712]{1,0:T(8,128)S(1)}, bf16[48,5760]{1,0:T(8,128)(2,1)S(1)}, bf16[48,3712]{1,0:T(8,128)(2,1)S(1)}, f32[16,64,896]{2,1,0:T(8,128)S(1...) custom-call(s32[16]{0:T(128)} %offsets.1, f32[16,64,896]{2,1,0:T(8,128)} %residual_hbm.1, ...), custom_call_target="tpu_custom_call" | custom-call | flops 917504 | bytes 3670016 | tf_op jit(solution)/shard_map/sum_residuals/pallas_call | solution.py:232
  4.3 0.1 collective-permute-start
  4.4 0.7 %collective-permute-start.1 = (bf16[48,3712]{1,0:T(8,128)(2,1)S(1)}, bf16[48,3712]{1,0:T(8,128)(2,1)S(1)}, u32[]{:S(2)}, u32[]{:S(2)}) collective-permute-start(bf16[48,3712]{1,0:T(8,128)(2,1)S(1)} %get-tuple-element.19), channel_id=1, source_target_pairs={{1,2},{3,4},{5,6},{7,8},{9,10},{11,12},{13,14},{15,16},{17,18},{19... | collective-permute-start | bytes 1069064 | tf_op jit(solution)/shard_map/ppermute | solution.py:265
  5.1 0.0 copy-done.2
  5.1 5.0 %project_own.1 = (f32[4,48,896]{2,1,0:T(8,128)S(1)}, f32[1,128]{1,0:T(1,128)S(1)}, bf16[3,2048,896]{2,1,0:T(8,128)(2,1)S(1)}, bf16[48,2048]{1,0:T(8,128)(2,1)S(1)}) custom-call(bf16[48,2048]{1,0:T(8,128)(2,1)S(1)} %get-tuple-element.21.half, f32[48,2048]{1,0:T(8,128)S(1)} %copy-done.2, bf16[2048,896]{1,0:T(8,128)(2,1)S(1)} %get-tuple-element.20.tile, ...), custom_call_target="tpu_custom_call" | custom-call | flops 2113929216 | bytes 16777216 | tf_op jit(solution)/shard_map/project_own/pallas_call | solution.py:268
  10.1 0.7 %collective-permute-start.9 = (bf16[48,2048]{1,0:T(8,128)(2,1)S(1)}, bf16[48,2048]{1,0:T(8,128)(2,1)S(1)}, u32[]{:S(2)}, u32[]{:S(2)}) collective-permute-start(bf16[48,2048]{1,0:T(8,128)(2,1)S(1)} %get-tuple-element.28), channel_id=1, source_target_pairs={{1,2},{3,4},{5,6},{7,8},{9,10},{11,12},{13,14},{15,16},{17,18},{19... | collective-permute-start | bytes 589832 | tf_op jit(solution)/shard_map/ppermute | solution.py:286
  10.8 0.0 collective-permute-done.1.from_cross
  10.8 0.0 collective-permute-done.from_pair
  10.8 4.2 %combine.1 = (f32[48,2048]{1,0:T(8,128)S(1)}, f32[48,2048]{1,0:T(8,128)S(1)}, f32[8,128]{1,0:T(8,128)S(1)}) custom-call(f32[48,3712]{1,0:T(8,128)S(1)} %get-tuple-element.17.own, bf16[48,5760]{1,0:T(8,128)(2,1)S(1)} %collective-permute-done.from_pair, bf16[48,3712]{1,0:T(8,128)(2,1)S(1)} %collective-permute-done.1.from_cross, ...), custom_call_target="tpu_custom_call" | custom-call | tf_op jit(solution)/shard_map/combine/pallas_call | solution.py:288
  15.0 6.4 %collective-permute-start.4 = (f32[8,128]{1,0:T(8,128)S(1)}, f32[8,128]{1,0:T(8,128)S(1)}, u32[]{:S(2)}, u32[]{:S(2)}) collective-permute-start(f32[8,128]{1,0:T(8,128)S(1)} %get-tuple-element.25.after), channel_id=1, source_target_pairs={{0,3},{1,2},{2,1},{3,0},{4,7},{5,6},{6,5},{7,4},{8,11},{9,10},{10,... | collective-permute-start | bytes 12296 | tf_op jit(solution)/shard_map/ppermute | solution.py:209
  21.4 0.0 collective-permute-start.3
  21.4 0.2 collective-permute-start.2
  21.6 0.0 collective-permute-done.9.from_cross
  21.6 0.8 %project_near.3.refs_0_ = f32[1,7,144,128]{3,2,1,0:T(8,128)S(1)} custom-call(f32[8,128]{1,0:T(8,128)S(1)} %get-tuple-element.25.after, bf16[48,2048]{1,0:T(8,128)(2,1)S(1)} %get-tuple-element.21.half, bf16[48,5760]{1,0:T(8,128)(2,1)S(1)} %collective-permute-done.from_pair, bf16[48,2048]{1,0:T(8,128)(2,1)S(1)} %collective-permute-done.9.from_cross, ...), custom_call_target="tpu_custom_call" | custom-call | flops 528482304 | bytes 1048576 | tf_op jit(solution)/shard_map/project_near/pallas_call | solution.py:305
  22.4 0.3 collective-permute-done.4
  22.7 2.3 %collective-permute-done.3 = f32[8,128]{1,0:T(8,128)S(1)} collective-permute-done((f32[8,128]{1,0:T(8,128)S(1)}, f32[8,128]{1,0:T(8,128)S(1)}, u32[]{:S(2)}, u32[]{:S(2)}) %collective-permute-start.3) | collective-permute-done | bytes 4128 | tf_op jit(solution)/shard_map/ppermute | solution.py:209
  25.0 0.0 collective-permute-done.2
  25.0 3.6 %collective-permute-start.7 = (f32[8,128]{1,0:T(8,128)S(1)}, f32[8,128]{1,0:T(8,128)S(1)}, u32[]{:S(2)}, u32[]{:S(2)}) collective-permute-start(f32[8,128]{1,0:T(8,128)S(1)} %add_add_fusion.1.after), channel_id=1, source_target_pairs={{0,24},{1,25},{2,26},{3,27},{4,28},{5,29},{6,30},{7,31},{8,16},{9,... | collective-permute-start | bytes 12296 | tf_op jit(solution)/shard_map/ppermute | solution.py:209
  28.6 0.5 %collective-permute-start.6 = (f32[8,128]{1,0:T(8,128)S(1)}, f32[8,128]{1,0:T(8,128)S(1)}, u32[]{:S(2)}, u32[]{:S(2)}) collective-permute-start(f32[8,128]{1,0:T(8,128)S(1)} %add_add_fusion.1.after), channel_id=1, source_target_pairs={{0,16},{1,17},{2,18},{3,19},{4,20},{5,21},{6,22},{7,23},{8,24},{9,... | collective-permute-start | bytes 12296 | tf_op jit(solution)/shard_map/ppermute | solution.py:209
  29.1 0.4 %collective-permute-start.5 = (f32[8,128]{1,0:T(8,128)S(1)}, f32[8,128]{1,0:T(8,128)S(1)}, u32[]{:S(2)}, u32[]{:S(2)}) collective-permute-start(f32[8,128]{1,0:T(8,128)S(1)} %add_add_fusion.1.after), channel_id=1, source_target_pairs={{0,8},{1,9},{2,10},{3,11},{4,12},{5,13},{6,14},{7,15},{8,0},{9,1},... | collective-permute-start | bytes 12296 | tf_op jit(solution)/shard_map/ppermute | solution.py:209
  29.5 0.8 %project_near.4.refs_1_ = f32[1,7,144,128]{3,2,1,0:T(8,128)S(1)} custom-call(f32[8,128]{1,0:T(8,128)S(1)} %add_add_fusion.1.after, bf16[48,2048]{1,0:T(8,128)(2,1)S(1)} %get-tuple-element.21.half, bf16[48,5760]{1,0:T(8,128)(2,1)S(1)} %collective-permute-done.from_pair, bf16[48,2048]{1,0:T(8,128)(2,1)S(1)} %collective-permute-done.9.from_cross, ...), custom_call_target="tpu_custom_call" | custom-call | flops 528482304 | bytes 1048576 | tf_op jit(solution)/shard_map/project_near/pallas_call | solution.py:305
  30.4 0.0 collective-permute-done.7
  30.4 3.3 %collective-permute-done.6 = f32[8,128]{1,0:T(8,128)S(1)} collective-permute-done((f32[8,128]{1,0:T(8,128)S(1)}, f32[8,128]{1,0:T(8,128)S(1)}, u32[]{:S(2)}, u32[]{:S(2)}) %collective-permute-start.6) | collective-permute-done | bytes 4128 | tf_op jit(solution)/shard_map/ppermute | solution.py:209
  33.7 0.0 collective-permute-done.5
  33.7 0.0 copy-start
  33.7 0.0 copy-start.1
  33.7 0.0 copy-start.3
  33.8 4.3 %collective-permute-start.8 = (f32[8,128]{1,0:T(8,128)S(1)}, f32[8,128]{1,0:T(8,128)S(1)}, u32[]{:S(2)}, u32[]{:S(2)}) collective-permute-start(f32[8,128]{1,0:T(8,128)S(1)} %add_add_fusion.after), channel_id=1, source_target_pairs={{0,4},{1,5},{2,6},{3,7},{4,0},{5,1},{6,2},{7,3},{8,12},{9,13},{10,... | collective-permute-start | bytes 12296 | tf_op jit(solution)/shard_map/ppermute | solution.py:209
  38.1 1.5 %project_near.5.refs_2_ = f32[2,7,144,128]{3,2,1,0:T(8,128)S(1)} custom-call(f32[8,128]{1,0:T(8,128)S(1)} %add_add_fusion.after, bf16[48,2048]{1,0:T(8,128)(2,1)S(1)} %get-tuple-element.21.half, bf16[48,5760]{1,0:T(8,128)(2,1)S(1)} %collective-permute-done.from_pair, bf16[48,2048]{1,0:T(8,128)(2,1)S(1)} %collective-permute-done.9.from_cross, ...), custom_call_target="tpu_custom_call" | custom-call | flops 1056964608 | bytes 1048576 | tf_op jit(solution)/shard_map/project_near/pallas_call | solution.py:305
  39.6 0.1 collective-permute-done.8
  39.7 0.0 copy-done
  39.7 0.0 copy-done.1
  39.7 0.0 copy-done.3
  39.7 3.1 %finish.1 = (f32[48,2048]{1,0:T(8,128)}, f32[16,64,896]{2,1,0:T(8,128)}, f32[48,2048]{1,0:T(8,128)}, f32[48,2048]{1,0:T(8,128)}) custom-call(s32[16]{0:T(128)S(1)} %copy-done.3, f32[8,128]{1,0:T(8,128)S(1)} %add.27.sums, f32[48,2048]{1,0:T(8,128)S(1)} %copy-done.1, f32[48,2048]{1,0:T(8,128)S(1)} %copy-done, f32[48,2048]{1,0:T(8,128)S(1)} %get-tuple-element.26.residual_part, ...), custom_call_target="tpu_custom_call" | custom-call | tf_op jit(solution)/shard_map/finish/pallas_call | solution.py:322
  (3 shorter events, 0.0 us)
Async XLA Ops:
  0.6 4.4 %copy-start.2 = (f32[48,2048]{1,0:T(8,128)S(1)}, f32[48,2048]{1,0:T(8,128)}, u32[]{:S(2)}) copy-start(f32[48,2048]{1,0:T(8,128)} %gradient.1) | copy-start | bytes 1179652
  4.3 6.5 %collective-permute-start = (bf16[48,5760]{1,0:T(8,128)(2,1)S(1)}, bf16[48,5760]{1,0:T(8,128)(2,1)S(1)}, u32[]{:S(2)}, u32[]{:S(2)}) collective-permute-start(bf16[48,5760]{1,0:T(8,128)(2,1)S(1)} %get-tuple-element.18), channel_id=1, source_target_pairs={{0,1},{1,0},{2,3},{3,2},{4,5},{5,4},{6,7},{7,6},{8,9},{9,8},{10,11... | collective-permute-start | bytes 1658888 | tf_op jit(solution)/shard_map/ppermute | solution.py:266
  4.4 6.4 %collective-permute-start.1 = (bf16[48,3712]{1,0:T(8,128)(2,1)S(1)}, bf16[48,3712]{1,0:T(8,128)(2,1)S(1)}, u32[]{:S(2)}, u32[]{:S(2)}) collective-permute-start(bf16[48,3712]{1,0:T(8,128)(2,1)S(1)} %get-tuple-element.19), channel_id=1, source_target_pairs={{1,2},{3,4},{5,6},{7,8},{9,10},{11,12},{13,14},{15,16},{17,18},{19... | collective-permute-start | bytes 1069064 | tf_op jit(solution)/shard_map/ppermute | solution.py:265
  10.1 11.5 %collective-permute-start.9 = (bf16[48,2048]{1,0:T(8,128)(2,1)S(1)}, bf16[48,2048]{1,0:T(8,128)(2,1)S(1)}, u32[]{:S(2)}, u32[]{:S(2)}) collective-permute-start(bf16[48,2048]{1,0:T(8,128)(2,1)S(1)} %get-tuple-element.28), channel_id=1, source_target_pairs={{1,2},{3,4},{5,6},{7,8},{9,10},{11,12},{13,14},{15,16},{17,18},{19... | collective-permute-start | bytes 589832 | tf_op jit(solution)/shard_map/ppermute | solution.py:286
  15.0 7.7 %collective-permute-start.4 = (f32[8,128]{1,0:T(8,128)S(1)}, f32[8,128]{1,0:T(8,128)S(1)}, u32[]{:S(2)}, u32[]{:S(2)}) collective-permute-start(f32[8,128]{1,0:T(8,128)S(1)} %get-tuple-element.25.after), channel_id=1, source_target_pairs={{0,3},{1,2},{2,1},{3,0},{4,7},{5,6},{6,5},{7,4},{8,11},{9,10},{10,... | collective-permute-start | bytes 12296 | tf_op jit(solution)/shard_map/ppermute | solution.py:209
  21.4 3.6 %collective-permute-start.3 = (f32[8,128]{1,0:T(8,128)S(1)}, f32[8,128]{1,0:T(8,128)S(1)}, u32[]{:S(2)}, u32[]{:S(2)}) collective-permute-start(f32[8,128]{1,0:T(8,128)S(1)} %get-tuple-element.25.after), channel_id=1, source_target_pairs={{0,2},{1,3},{2,0},{3,1},{4,6},{5,7},{6,4},{7,5},{8,10},{9,11},{10,... | collective-permute-start | bytes 12296 | tf_op jit(solution)/shard_map/ppermute | solution.py:209
  21.4 3.6 %collective-permute-start.2 = (f32[8,128]{1,0:T(8,128)S(1)}, f32[8,128]{1,0:T(8,128)S(1)}, u32[]{:S(2)}, u32[]{:S(2)}) collective-permute-start(f32[8,128]{1,0:T(8,128)S(1)} %get-tuple-element.25.after), channel_id=1, source_target_pairs={{0,1},{1,0},{2,3},{3,2},{4,5},{5,4},{6,7},{7,6},{8,9},{9,8},{10,11... | collective-permute-start | bytes 12296 | tf_op jit(solution)/shard_map/ppermute | solution.py:209
  25.0 5.4 %collective-permute-start.7 = (f32[8,128]{1,0:T(8,128)S(1)}, f32[8,128]{1,0:T(8,128)S(1)}, u32[]{:S(2)}, u32[]{:S(2)}) collective-permute-start(f32[8,128]{1,0:T(8,128)S(1)} %add_add_fusion.1.after), channel_id=1, source_target_pairs={{0,24},{1,25},{2,26},{3,27},{4,28},{5,29},{6,30},{7,31},{8,16},{9,... | collective-permute-start | bytes 12296 | tf_op jit(solution)/shard_map/ppermute | solution.py:209
  28.6 5.1 %collective-permute-start.6 = (f32[8,128]{1,0:T(8,128)S(1)}, f32[8,128]{1,0:T(8,128)S(1)}, u32[]{:S(2)}, u32[]{:S(2)}) collective-permute-start(f32[8,128]{1,0:T(8,128)S(1)} %add_add_fusion.1.after), channel_id=1, source_target_pairs={{0,16},{1,17},{2,18},{3,19},{4,20},{5,21},{6,22},{7,23},{8,24},{9,... | collective-permute-start | bytes 12296 | tf_op jit(solution)/shard_map/ppermute | solution.py:209
  29.1 4.6 %collective-permute-start.5 = (f32[8,128]{1,0:T(8,128)S(1)}, f32[8,128]{1,0:T(8,128)S(1)}, u32[]{:S(2)}, u32[]{:S(2)}) collective-permute-start(f32[8,128]{1,0:T(8,128)S(1)} %add_add_fusion.1.after), channel_id=1, source_target_pairs={{0,8},{1,9},{2,10},{3,11},{4,12},{5,13},{6,14},{7,15},{8,0},{9,1},... | collective-permute-start | bytes 12296 | tf_op jit(solution)/shard_map/ppermute | solution.py:209
  33.7 5.9 %copy-start = (f32[48,2048]{1,0:T(8,128)S(1)}, f32[48,2048]{1,0:T(8,128)}, u32[]{:S(2)}) copy-start(f32[48,2048]{1,0:T(8,128)} %direction.1) | copy-start | bytes 1179652
  33.7 5.9 %copy-start.1 = (f32[48,2048]{1,0:T(8,128)S(1)}, f32[48,2048]{1,0:T(8,128)}, u32[]{:S(2)}) copy-start(f32[48,2048]{1,0:T(8,128)} %solution.1) | copy-start | bytes 1179652
  33.7 5.9 %copy-start.3 = (s32[16]{0:T(128)S(1)}, s32[16]{0:T(128)}, u32[]{:S(2)}) copy-start(s32[16]{0:T(128)} %offsets.1) | copy-start | bytes 196
  33.8 5.9 %collective-permute-start.8 = (f32[8,128]{1,0:T(8,128)S(1)}, f32[8,128]{1,0:T(8,128)S(1)}, u32[]{:S(2)}, u32[]{:S(2)}) collective-permute-start(f32[8,128]{1,0:T(8,128)S(1)} %add_add_fusion.after), channel_id=1, source_target_pairs={{0,4},{1,5},{2,6},{3,7},{4,0},{5,1},{6,2},{7,3},{8,12},{9,13},{10,... | collective-permute-start | bytes 12296 | tf_op jit(solution)/shard_map/ppermute | solution.py:209

commit v7 on v6

--- a/solution.py
+++ b/solution.py
@@ -10,7 +10,7 @@
 ANGLES = 4
 LANES = 128
 CHUNK = 512
-ROUNDS = ((1, 2, 3), (8, 16, 24), (4,))
+ROUNDS = ((1, 2, 3), (8, 24, 16), (6,))
 GROUPS = ((0,), (1,), (2, 3))
 F32 = jnp.float32
 BF16 = jnp.bfloat16

time: 42.9 us -> 42.2 us (0.984)
  waiting for transfers between devices: 6.03 us -> 5.55 us
    ppermute x7, waiting for transfers between devices: 6.02 us -> 5.54 us  [exchanged_sum(): lax.ppermute(x, 'slab', [(i, i ^ m) for i in range(count)])]
where the time goes in v7:
time: 42.2 us; the launch traced here: 42 us
  Pallas kernels  19 us (45%)
  starting transfers between devices  16.6 us (39%)
  waiting for transfers between devices  5.55 us (13%)
  between operations  0.78 us (2%)
    ppermute x7, starting transfers between devices, exchanged_sum(): lax.ppermute(x, 'slab', [(i, i ^ m) for i in range(count)])  15.2 us
    ppermute x7, waiting for transfers between devices, exchanged_sum(): lax.ppermute(x, 'slab', [(i, i ^ m) for i in range(count)])  5.54 us
    pallas_call x1, Pallas kernels, local(): pl.pallas_call(project_own, name='project_own', in_specs=[vmem] * 3 + [hb...  5.01 us
    pallas_call x1, Pallas kernels, local(): pl.pallas_call(combine, name='combine', in_specs=[vmem] * 7, out_specs=[v...  4.21 us
    pallas_call x1, Pallas kernels, local(): pl.pallas_call(sum_residuals, name='sum_residuals', in_specs=[hbm] * 4, o...  3.64 us
    pallas_call x1, Pallas kernels, local(): pl.pallas_call(finish, name='finish', in_specs=[smem] + [vmem] * 9, out_s...  3.1 us
    pallas_call x3, Pallas kernels, local(): pl.pallas_call(functools.partial(project_near, angles), name='project_nea...  3.08 us
  transfers between devices with their start and end apart: 10, of which 4 were waited for; matrix products, arithmetic and copies ran while one was open for 0% of the time, Pallas kernels for 29%

profile of v7, /device:TPU:0, one launch (start us, length us, event | category | flops | bytes accessed | tf_op | source)
XLA Modules:
  0.0 42.0 jit_solution(15194444940343899051)
XLA Ops:
  0.6 0.0 copy-start.2
  0.6 3.6 %sum_residuals.1 = (f32[48,3712]{1,0:T(8,128)S(1)}, bf16[48,5760]{1,0:T(8,128)(2,1)S(1)}, bf16[48,3712]{1,0:T(8,128)(2,1)S(1)}, f32[16,64,896]{2,1,0:T(8,128)S(1...) custom-call(s32[16]{0:T(128)} %offsets.1, f32[16,64,896]{2,1,0:T(8,128)} %residual_hbm.1, ...), custom_call_target="tpu_custom_call" | custom-call | flops 917504 | bytes 3670016 | tf_op jit(solution)/shard_map/sum_residuals/pallas_call | solution.py:232
  4.3 0.1 collective-permute-start
  4.4 0.7 %collective-permute-start.1 = (bf16[48,3712]{1,0:T(8,128)(2,1)S(1)}, bf16[48,3712]{1,0:T(8,128)(2,1)S(1)}, u32[]{:S(2)}, u32[]{:S(2)}) collective-permute-start(bf16[48,3712]{1,0:T(8,128)(2,1)S(1)} %get-tuple-element.19), channel_id=1, source_target_pairs={{1,2},{3,4},{5,6},{7,8},{9,10},{11,12},{13,14},{15,16},{17,18},{19... | collective-permute-start | bytes 1069064 | tf_op jit(solution)/shard_map/ppermute | solution.py:265
  5.1 0.0 copy-done.2
  5.1 5.0 %project_own.1 = (f32[4,48,896]{2,1,0:T(8,128)S(1)}, f32[1,128]{1,0:T(1,128)S(1)}, bf16[3,2048,896]{2,1,0:T(8,128)(2,1)S(1)}, bf16[48,2048]{1,0:T(8,128)(2,1)S(1)}) custom-call(bf16[48,2048]{1,0:T(8,128)(2,1)S(1)} %get-tuple-element.21.half, f32[48,2048]{1,0:T(8,128)S(1)} %copy-done.2, bf16[2048,896]{1,0:T(8,128)(2,1)S(1)} %get-tuple-element.20.tile, ...), custom_call_target="tpu_custom_call" | custom-call | flops 2113929216 | bytes 16777216 | tf_op jit(solution)/shard_map/project_own/pallas_call | solution.py:268
  10.1 0.7 %collective-permute-start.9 = (bf16[48,2048]{1,0:T(8,128)(2,1)S(1)}, bf16[48,2048]{1,0:T(8,128)(2,1)S(1)}, u32[]{:S(2)}, u32[]{:S(2)}) collective-permute-start(bf16[48,2048]{1,0:T(8,128)(2,1)S(1)} %get-tuple-element.28), channel_id=1, source_target_pairs={{1,2},{3,4},{5,6},{7,8},{9,10},{11,12},{13,14},{15,16},{17,18},{19... | collective-permute-start | bytes 589832 | tf_op jit(solution)/shard_map/ppermute | solution.py:286
  10.8 0.0 collective-permute-done.1.from_cross
  10.8 0.0 collective-permute-done.from_pair
  10.8 4.2 %combine.1 = (f32[48,2048]{1,0:T(8,128)S(1)}, f32[48,2048]{1,0:T(8,128)S(1)}, f32[8,128]{1,0:T(8,128)S(1)}) custom-call(f32[48,3712]{1,0:T(8,128)S(1)} %get-tuple-element.17.own, bf16[48,5760]{1,0:T(8,128)(2,1)S(1)} %collective-permute-done.from_pair, bf16[48,3712]{1,0:T(8,128)(2,1)S(1)} %collective-permute-done.1.from_cross, ...), custom_call_target="tpu_custom_call" | custom-call | tf_op jit(solution)/shard_map/combine/pallas_call | solution.py:288
  15.0 6.4 %collective-permute-start.4 = (f32[8,128]{1,0:T(8,128)S(1)}, f32[8,128]{1,0:T(8,128)S(1)}, u32[]{:S(2)}, u32[]{:S(2)}) collective-permute-start(f32[8,128]{1,0:T(8,128)S(1)} %get-tuple-element.25.after), channel_id=1, source_target_pairs={{0,3},{1,2},{2,1},{3,0},{4,7},{5,6},{6,5},{7,4},{8,11},{9,10},{10,... | collective-permute-start | bytes 12296 | tf_op jit(solution)/shard_map/ppermute | solution.py:209
  21.4 0.0 collective-permute-start.3
  21.4 0.2 collective-permute-start.2
  21.6 0.0 collective-permute-done.9.from_cross
  21.6 0.8 %project_near.3.refs_0_ = f32[1,7,144,128]{3,2,1,0:T(8,128)S(1)} custom-call(f32[8,128]{1,0:T(8,128)S(1)} %get-tuple-element.25.after, bf16[48,2048]{1,0:T(8,128)(2,1)S(1)} %get-tuple-element.21.half, bf16[48,5760]{1,0:T(8,128)(2,1)S(1)} %collective-permute-done.from_pair, bf16[48,2048]{1,0:T(8,128)(2,1)S(1)} %collective-permute-done.9.from_cross, ...), custom_call_target="tpu_custom_call" | custom-call | flops 528482304 | bytes 1048576 | tf_op jit(solution)/shard_map/project_near/pallas_call | solution.py:305
  22.4 0.3 collective-permute-done.4
  22.7 2.3 %collective-permute-done.3 = f32[8,128]{1,0:T(8,128)S(1)} collective-permute-done((f32[8,128]{1,0:T(8,128)S(1)}, f32[8,128]{1,0:T(8,128)S(1)}, u32[]{:S(2)}, u32[]{:S(2)}) %collective-permute-start.3) | collective-permute-done | bytes 4128 | tf_op jit(solution)/shard_map/ppermute | solution.py:209
  25.0 0.0 collective-permute-done.2
  25.0 3.6 %collective-permute-start.7 = (f32[8,128]{1,0:T(8,128)S(1)}, f32[8,128]{1,0:T(8,128)S(1)}, u32[]{:S(2)}, u32[]{:S(2)}) collective-permute-start(f32[8,128]{1,0:T(8,128)S(1)} %add_add_fusion.1.after), channel_id=1, source_target_pairs={{0,16},{1,17},{2,18},{3,19},{4,20},{5,21},{6,22},{7,23},{8,24},{9,... | collective-permute-start | bytes 12296 | tf_op jit(solution)/shard_map/ppermute | solution.py:209
  28.6 1.2 %collective-permute-start.6 = (f32[8,128]{1,0:T(8,128)S(1)}, f32[8,128]{1,0:T(8,128)S(1)}, u32[]{:S(2)}, u32[]{:S(2)}) collective-permute-start(f32[8,128]{1,0:T(8,128)S(1)} %add_add_fusion.1.after), channel_id=1, source_target_pairs={{0,24},{1,25},{2,26},{3,27},{4,28},{5,29},{6,30},{7,31},{8,16},{9,... | collective-permute-start | bytes 12296 | tf_op jit(solution)/shard_map/ppermute | solution.py:209
  29.7 0.0 collective-permute-start.5
  29.7 0.8 %project_near.4.refs_1_ = f32[1,7,144,128]{3,2,1,0:T(8,128)S(1)} custom-call(f32[8,128]{1,0:T(8,128)S(1)} %add_add_fusion.1.after, bf16[48,2048]{1,0:T(8,128)(2,1)S(1)} %get-tuple-element.21.half, bf16[48,5760]{1,0:T(8,128)(2,1)S(1)} %collective-permute-done.from_pair, bf16[48,2048]{1,0:T(8,128)(2,1)S(1)} %collective-permute-done.9.from_cross, ...), custom_call_target="tpu_custom_call" | custom-call | flops 528482304 | bytes 1048576 | tf_op jit(solution)/shard_map/project_near/pallas_call | solution.py:305
  30.5 0.0 collective-permute-done.7
  30.6 2.8 %collective-permute-done.6 = f32[8,128]{1,0:T(8,128)S(1)} collective-permute-done((f32[8,128]{1,0:T(8,128)S(1)}, f32[8,128]{1,0:T(8,128)S(1)}, u32[]{:S(2)}, u32[]{:S(2)}) %collective-permute-start.6) | collective-permute-done | bytes 4128 | tf_op jit(solution)/shard_map/ppermute | solution.py:209
  33.4 0.0 collective-permute-done.5
  33.4 0.0 copy-start
  33.4 0.0 copy-start.1
  33.4 0.0 copy-start.3
  33.4 3.9 %collective-permute-start.8 = (f32[8,128]{1,0:T(8,128)S(1)}, f32[8,128]{1,0:T(8,128)S(1)}, u32[]{:S(2)}, u32[]{:S(2)}) collective-permute-start(f32[8,128]{1,0:T(8,128)S(1)} %add_add_fusion.after), channel_id=1, source_target_pairs={{0,6},{1,7},{2,4},{3,5},{4,2},{5,3},{6,0},{7,1},{8,14},{9,15},{10,... | collective-permute-start | bytes 12296 | tf_op jit(solution)/shard_map/ppermute | solution.py:209
  37.3 1.5 %project_near.5.refs_2_ = f32[2,7,144,128]{3,2,1,0:T(8,128)S(1)} custom-call(f32[8,128]{1,0:T(8,128)S(1)} %add_add_fusion.after, bf16[48,2048]{1,0:T(8,128)(2,1)S(1)} %get-tuple-element.21.half, bf16[48,5760]{1,0:T(8,128)(2,1)S(1)} %collective-permute-done.from_pair, bf16[48,2048]{1,0:T(8,128)(2,1)S(1)} %collective-permute-done.9.from_cross, ...), custom_call_target="tpu_custom_call" | custom-call | flops 1056964608 | bytes 1048576 | tf_op jit(solution)/shard_map/project_near/pallas_call | solution.py:305
  38.8 0.1 collective-permute-done.8
  38.9 0.0 copy-done
  38.9 0.0 copy-done.1
  38.9 0.0 copy-done.3
  38.9 3.1 %finish.1 = (f32[48,2048]{1,0:T(8,128)}, f32[16,64,896]{2,1,0:T(8,128)}, f32[48,2048]{1,0:T(8,128)}, f32[48,2048]{1,0:T(8,128)}) custom-call(s32[16]{0:T(128)S(1)} %copy-done.3, f32[8,128]{1,0:T(8,128)S(1)} %add.27.sums, f32[48,2048]{1,0:T(8,128)S(1)} %copy-done.1, f32[48,2048]{1,0:T(8,128)S(1)} %copy-done, f32[48,2048]{1,0:T(8,128)S(1)} %get-tuple-element.26.residual_part, ...), custom_call_target="tpu_custom_call" | custom-call | tf_op jit(solution)/shard_map/finish/pallas_call | solution.py:322
  (3 shorter events, 0.0 us)
Async XLA Ops:
  0.6 4.4 %copy-start.2 = (f32[48,2048]{1,0:T(8,128)S(1)}, f32[48,2048]{1,0:T(8,128)}, u32[]{:S(2)}) copy-start(f32[48,2048]{1,0:T(8,128)} %gradient.1) | copy-start | bytes 1179652
  4.3 6.5 %collective-permute-start = (bf16[48,5760]{1,0:T(8,128)(2,1)S(1)}, bf16[48,5760]{1,0:T(8,128)(2,1)S(1)}, u32[]{:S(2)}, u32[]{:S(2)}) collective-permute-start(bf16[48,5760]{1,0:T(8,128)(2,1)S(1)} %get-tuple-element.18), channel_id=1, source_target_pairs={{0,1},{1,0},{2,3},{3,2},{4,5},{5,4},{6,7},{7,6},{8,9},{9,8},{10,11... | collective-permute-start | bytes 1658888 | tf_op jit(solution)/shard_map/ppermute | solution.py:266
  4.4 6.4 %collective-permute-start.1 = (bf16[48,3712]{1,0:T(8,128)(2,1)S(1)}, bf16[48,3712]{1,0:T(8,128)(2,1)S(1)}, u32[]{:S(2)}, u32[]{:S(2)}) collective-permute-start(bf16[48,3712]{1,0:T(8,128)(2,1)S(1)} %get-tuple-element.19), channel_id=1, source_target_pairs={{1,2},{3,4},{5,6},{7,8},{9,10},{11,12},{13,14},{15,16},{17,18},{19... | collective-permute-start | bytes 1069064 | tf_op jit(solution)/shard_map/ppermute | solution.py:265
  10.1 11.5 %collective-permute-start.9 = (bf16[48,2048]{1,0:T(8,128)(2,1)S(1)}, bf16[48,2048]{1,0:T(8,128)(2,1)S(1)}, u32[]{:S(2)}, u32[]{:S(2)}) collective-permute-start(bf16[48,2048]{1,0:T(8,128)(2,1)S(1)} %get-tuple-element.28), channel_id=1, source_target_pairs={{1,2},{3,4},{5,6},{7,8},{9,10},{11,12},{13,14},{15,16},{17,18},{19... | collective-permute-start | bytes 589832 | tf_op jit(solution)/shard_map/ppermute | solution.py:286
  15.0 7.7 %collective-permute-start.4 = (f32[8,128]{1,0:T(8,128)S(1)}, f32[8,128]{1,0:T(8,128)S(1)}, u32[]{:S(2)}, u32[]{:S(2)}) collective-permute-start(f32[8,128]{1,0:T(8,128)S(1)} %get-tuple-element.25.after), channel_id=1, source_target_pairs={{0,3},{1,2},{2,1},{3,0},{4,7},{5,6},{6,5},{7,4},{8,11},{9,10},{10,... | collective-permute-start | bytes 12296 | tf_op jit(solution)/shard_map/ppermute | solution.py:209
  21.4 3.6 %collective-permute-start.3 = (f32[8,128]{1,0:T(8,128)S(1)}, f32[8,128]{1,0:T(8,128)S(1)}, u32[]{:S(2)}, u32[]{:S(2)}) collective-permute-start(f32[8,128]{1,0:T(8,128)S(1)} %get-tuple-element.25.after), channel_id=1, source_target_pairs={{0,2},{1,3},{2,0},{3,1},{4,6},{5,7},{6,4},{7,5},{8,10},{9,11},{10,... | collective-permute-start | bytes 12296 | tf_op jit(solution)/shard_map/ppermute | solution.py:209
  21.4 3.6 %collective-permute-start.2 = (f32[8,128]{1,0:T(8,128)S(1)}, f32[8,128]{1,0:T(8,128)S(1)}, u32[]{:S(2)}, u32[]{:S(2)}) collective-permute-start(f32[8,128]{1,0:T(8,128)S(1)} %get-tuple-element.25.after), channel_id=1, source_target_pairs={{0,1},{1,0},{2,3},{3,2},{4,5},{5,4},{6,7},{7,6},{8,9},{9,8},{10,11... | collective-permute-start | bytes 12296 | tf_op jit(solution)/shard_map/ppermute | solution.py:209
  25.0 5.5 %collective-permute-start.7 = (f32[8,128]{1,0:T(8,128)S(1)}, f32[8,128]{1,0:T(8,128)S(1)}, u32[]{:S(2)}, u32[]{:S(2)}) collective-permute-start(f32[8,128]{1,0:T(8,128)S(1)} %add_add_fusion.1.after), channel_id=1, source_target_pairs={{0,16},{1,17},{2,18},{3,19},{4,20},{5,21},{6,22},{7,23},{8,24},{9,... | collective-permute-start | bytes 12296 | tf_op jit(solution)/shard_map/ppermute | solution.py:209
  28.6 4.8 %collective-permute-start.6 = (f32[8,128]{1,0:T(8,128)S(1)}, f32[8,128]{1,0:T(8,128)S(1)}, u32[]{:S(2)}, u32[]{:S(2)}) collective-permute-start(f32[8,128]{1,0:T(8,128)S(1)} %add_add_fusion.1.after), channel_id=1, source_target_pairs={{0,24},{1,25},{2,26},{3,27},{4,28},{5,29},{6,30},{7,31},{8,16},{9,... | collective-permute-start | bytes 12296 | tf_op jit(solution)/shard_map/ppermute | solution.py:209
  29.7 3.7 %collective-permute-start.5 = (f32[8,128]{1,0:T(8,128)S(1)}, f32[8,128]{1,0:T(8,128)S(1)}, u32[]{:S(2)}, u32[]{:S(2)}) collective-permute-start(f32[8,128]{1,0:T(8,128)S(1)} %add_add_fusion.1.after), channel_id=1, source_target_pairs={{0,8},{1,9},{2,10},{3,11},{4,12},{5,13},{6,14},{7,15},{8,0},{9,1},... | collective-permute-start | bytes 12296 | tf_op jit(solution)/shard_map/ppermute | solution.py:209
  33.4 5.5 %copy-start = (f32[48,2048]{1,0:T(8,128)S(1)}, f32[48,2048]{1,0:T(8,128)}, u32[]{:S(2)}) copy-start(f32[48,2048]{1,0:T(8,128)} %direction.1) | copy-start | bytes 1179652
  33.4 5.5 %copy-start.1 = (f32[48,2048]{1,0:T(8,128)S(1)}, f32[48,2048]{1,0:T(8,128)}, u32[]{:S(2)}) copy-start(f32[48,2048]{1,0:T(8,128)} %solution.1) | copy-start | bytes 1179652
  33.4 5.5 %copy-start.3 = (s32[16]{0:T(128)S(1)}, s32[16]{0:T(128)}, u32[]{:S(2)}) copy-start(s32[16]{0:T(128)} %offsets.1) | copy-start | bytes 196
  33.4 5.5 %collective-permute-start.8 = (f32[8,128]{1,0:T(8,128)S(1)}, f32[8,128]{1,0:T(8,128)S(1)}, u32[]{:S(2)}, u32[]{:S(2)}) collective-permute-start(f32[8,128]{1,0:T(8,128)S(1)} %add_add_fusion.after), channel_id=1, source_target_pairs={{0,6},{1,7},{2,4},{3,5},{4,2},{5,3},{6,0},{7,1},{8,14},{9,15},{10,... | collective-permute-start | bytes 12296 | tf_op jit(solution)/shard_map/ppermute | solution.py:209

commit v8 on v7

--- a/solution.py
+++ b/solution.py
@@ -37,9 +37,8 @@
     return jnp.sum(total, axis=0, keepdims=True)
 
 
-def sum_residuals(offsets_hbm, residual_hbm, tiles_hbm, direction_hbm, own, to_pair, to_cross,
-                  residual, tile, half, rows, offsets, direction, sem, offsets_sem, tile_sem,
-                  direction_sem):
+def sum_residuals(offsets_hbm, residual_hbm, direction_hbm, own, to_pair, to_cross, residual, half,
+                  rows, offsets, direction, sem, offsets_sem, direction_sem):
     views, detector_rows, columns = residual.shape
     slab_rows = own.shape[0]
     near = 3 * slab_rows
@@ -54,8 +53,6 @@
         copy(v).start()
     direction_copy = pltpu.make_async_copy(direction_hbm, direction, direction_sem)
     direction_copy.start()
-    tile_copy = pltpu.make_async_copy(tiles_hbm.at[0], tile, tile_sem)
-    tile_copy.start()
     above = pair_is_above()
     pair_row = pl.multiple_of(jnp.where(above, 2 * slab_rows, 0), 16)
     cross_row = pl.multiple_of(jnp.where(above, 0, 2 * slab_rows), 16)
@@ -86,22 +83,21 @@
     direction_copy.wait()
     half[...] = direction[...].astype(BF16)
     to_pair[:, to_cross.shape[1] :] = half[...]
-    tile_copy.wait()
-
-
-def project_own(half, gradient, tile, tiles_hbm, images, grad_sums, tiles, to_cross, sem):
+
+
+def project_own(half, gradient, tiles_hbm, images, grad_sums, tile, tiles, to_cross, sem):
     copies = [
-        pltpu.make_async_copy(tiles_hbm.at[a], tiles.at[a - 1], sem.at[a - 1])
-        for a in range(1, ANGLES)
+        pltpu.make_async_copy(tiles_hbm.at[a], tile if a == 0 else tiles.at[a - 1], sem.at[a])
+        for a in range(ANGLES)
     ]
     for c in copies:
         c.start()
     grad_sums[...] = lane_sums(gradient[...] * gradient[...])
     to_cross[...] = half[...]
-    images[0] = jnp.dot(half[...], tile[...], preferred_element_type=F32)
-    for a in range(1, ANGLES):
-        copies[a - 1].wait()
-        images[a] = jnp.dot(half[...], tiles[a - 1], preferred_element_type=F32)
+    for a in range(ANGLES):
+        copies[a].wait()
+        weights = tile[...] if a == 0 else tiles[a - 1]
+        images[a] = jnp.dot(half[...], weights, preferred_element_type=F32)
 
 
 def project_near(angles, after, half, from_pair, from_cross, tile, tiles, planes, near):
@@ -229,17 +225,16 @@
 
     wide = ANGLES * columns + LANES
     tiles = pltpu.with_memory_space_constraint(tiles, pltpu.HBM)
-    own, to_pair, to_cross, residual_here, tile, half = pl.pallas_call(
+    own, to_pair, to_cross, residual_here, half = pl.pallas_call(
         sum_residuals,
         name="sum_residuals",
-        in_specs=[hbm] * 4,
-        out_specs=[vmem] * 6,
+        in_specs=[hbm] * 3,
+        out_specs=[vmem] * 5,
         out_shape=[
             sds((slab_rows, wide), F32),
             sds((slab_rows, wide + cells), BF16),
             sds((slab_rows, wide), BF16),
             pltpu.VMEM(residual.shape, F32),
-            pltpu.VMEM(tiles.shape[1:], BF16),
             sds((slab_rows, cells), BF16),
         ],
         scratch_shapes=[
@@ -249,7 +244,6 @@
             pltpu.SemaphoreType.DMA((views,)),
             pltpu.SemaphoreType.DMA,
             pltpu.SemaphoreType.DMA,
-            pltpu.SemaphoreType.DMA,
         ],
         compiler_params=pltpu.CompilerParams(vmem_limit_bytes=8 * MIB),
         cost_estimate=pl.CostEstimate(
@@ -258,30 +252,30 @@
     )(
         pltpu.with_memory_space_constraint(offsets, pltpu.HBM),
         pltpu.with_memory_space_constraint(residual, pltpu.HBM),
-        tiles,
         pltpu.with_memory_space_constraint(direction, pltpu.HBM),
     )
 
     from_cross = lax.ppermute(to_cross, "slab", cross)
     from_pair = lax.ppermute(to_pair, "slab", pair)
 
-    images, grad_sums, tiles_here, half_to_cross = pl.pallas_call(
+    images, grad_sums, tile, tiles_here, half_to_cross = pl.pallas_call(
         project_own,
         name="project_own",
-        in_specs=[vmem] * 3 + [hbm],
-        out_specs=[vmem] * 4,
+        in_specs=[vmem] * 2 + [hbm],
+        out_specs=[vmem] * 5,
         out_shape=[
             sds((ANGLES, slab_rows, columns), F32),
             sds((1, LANES), F32),
+            pltpu.VMEM(tiles.shape[1:], BF16),
             pltpu.VMEM((ANGLES - 1, *tiles.shape[1:]), BF16),
             sds((slab_rows, cells), BF16),
         ],
-        scratch_shapes=[pltpu.SemaphoreType.DMA((ANGLES - 1,))],
+        scratch_shapes=[pltpu.SemaphoreType.DMA((ANGLES,))],
         compiler_params=pltpu.CompilerParams(vmem_limit_bytes=8 * MIB),
         cost_estimate=pl.CostEstimate(
             flops=2 * near * cells * columns * ANGLES, bytes_accessed=16 * MIB, transcendentals=0
         ),
-    )(half, gradient, tile, tiles)
+    )(half, gradient, tiles)
 
     half_cross = lax.ppermute(half_to_cross, "slab", cross)
 

time: 42.2 us -> 42.1 us (level)
  transfers between devices with their start and end apart: 10 -> 10, of which waited for: 4 -> 4; matrix products, arithmetic and copies ran while one was open for 0% -> 0% of each run, Pallas kernels for 29% -> 32%
where the time goes in v8:
time: 42.1 us; the launch traced here: 42 us
  Pallas kernels  19 us (45%)
  starting transfers between devices  16.6 us (39%)
  waiting for transfers between devices  5.55 us (13%)
  between operations  0.78 us (2%)
    ppermute x7, starting transfers between devices, exchanged_sum(): lax.ppermute(x, 'slab', [(i, i ^ m) for i in range(count)])  15.2 us
    pallas_call x1, Pallas kernels, local(): pl.pallas_call(project_own, name='project_own', in_specs=[vmem] * 2 + [hb...  6.04 us
    ppermute x7, waiting for transfers between devices, exchanged_sum(): lax.ppermute(x, 'slab', [(i, i ^ m) for i in range(count)])  5.55 us
    pallas_call x1, Pallas kernels, local(): pl.pallas_call(combine, name='combine', in_specs=[vmem] * 7, out_specs=[v...  4.27 us
    pallas_call x1, Pallas kernels, local(): pl.pallas_call(finish, name='finish', in_specs=[smem] + [vmem] * 9, out_s...  3.1 us
    pallas_call x3, Pallas kernels, local(): pl.pallas_call(functools.partial(project_near, angles), name='project_nea...  3.08 us
    pallas_call x1, Pallas kernels, local(): pl.pallas_call(sum_residuals, name='sum_residuals', in_specs=[hbm] * 3, o...  2.51 us
  transfers between devices with their start and end apart: 10, of which 4 were waited for; matrix products, arithmetic and copies ran while one was open for 0% of the time, Pallas kernels for 32%

profile of v8, /device:TPU:0, one launch (start us, length us, event | category | flops | bytes accessed | tf_op | source)
XLA Modules:
  0.0 42.0 jit_solution(18027707977090305054)
XLA Ops:
  0.6 0.0 copy-start.2
  0.6 2.5 %sum_residuals.1 = (f32[48,3712]{1,0:T(8,128)S(1)}, bf16[48,5760]{1,0:T(8,128)(2,1)S(1)}, bf16[48,3712]{1,0:T(8,128)(2,1)S(1)}, f32[16,64,896]{2,1,0:T(8,128)S(1)}, bf16[48,2048]{1,0:T(8,128)(2,1)S(1)}) custom-call(s32[16]{0:T(128)} %offsets.1, f32[16,64,896]{2,1,0:T(8,128)} %residual_hbm.1, f32[48,2048]{1,0:T(8,128)} %direction.1), custom_call_target="tpu_custom_call" | custom-call | flops 917504 | bytes 3670016 | tf_op jit(solution)/shard_map/sum_residuals/pallas_call | solution.py:228
  3.2 0.1 collective-permute-start
  3.2 0.7 %collective-permute-start.1 = (bf16[48,3712]{1,0:T(8,128)(2,1)S(1)}, bf16[48,3712]{1,0:T(8,128)(2,1)S(1)}, u32[]{:S(2)}, u32[]{:S(2)}) collective-permute-start(bf16[48,3712]{1,0:T(8,128)(2,1)S(1)} %get-tuple-element.19), channel_id=1, source_target_pairs={{1,2},{3,4},{5,6},{7,8},{9,10},{11,12},{13,14},{15,16},{17,18},{19... | collective-permute-start | bytes 1069064 | tf_op jit(solution)/shard_map/ppermute | solution.py:258
  3.9 0.0 copy-done.2
  3.9 6.0 %project_own.1 = (f32[4,48,896]{2,1,0:T(8,128)S(1)}, f32[1,128]{1,0:T(1,128)S(1)}, bf16[2048,896]{1,0:T(8,128)(2,1)S(1)}, bf16[3,2048,896]{2,1,0:T(8,128)(2,1)S(1)}, bf16[48,2048]{1,0:T(8,128)(2,1)S(1)}) custom-call(bf16[48,2048]{1,0:T(8,128)(2,1)S(1)} %get-tuple-element.20.half, f32[48,2048]{1,0:T(8,128)S(1)} %copy-done.2, bf16[4,2048,896]{2,1,0:T(8,128)(2,1)} %tiles_hbm.1), custom_call_target="tpu_custom_call" | custom-call | flops 2113929216 | bytes 16777216 | tf_op jit(solution)/shard_map/project_own/pallas_call | solution.py:261
  10.0 0.7 %collective-permute-start.9 = (bf16[48,2048]{1,0:T(8,128)(2,1)S(1)}, bf16[48,2048]{1,0:T(8,128)(2,1)S(1)}, u32[]{:S(2)}, u32[]{:S(2)}) collective-permute-start(bf16[48,2048]{1,0:T(8,128)(2,1)S(1)} %get-tuple-element.28), channel_id=1, source_target_pairs={{1,2},{3,4},{5,6},{7,8},{9,10},{11,12},{13,14},{15,16},{17,18},{19... | collective-permute-start | bytes 589832 | tf_op jit(solution)/shard_map/ppermute | solution.py:280
  10.7 0.0 collective-permute-done.1.from_cross
  10.7 0.0 collective-permute-done.from_pair
  10.7 4.3 %combine.1 = (f32[48,2048]{1,0:T(8,128)S(1)}, f32[48,2048]{1,0:T(8,128)S(1)}, f32[8,128]{1,0:T(8,128)S(1)}) custom-call(f32[48,3712]{1,0:T(8,128)S(1)} %get-tuple-element.17.own, bf16[48,5760]{1,0:T(8,128)(2,1)S(1)} %collective-permute-done.from_pair, bf16[48,3712]{1,0:T(8,128)(2,1)S(1)} %collective-permute-done.1.from_cross, ...), custom_call_target="tpu_custom_call" | custom-call | tf_op jit(solution)/shard_map/combine/pallas_call | solution.py:282
  15.0 6.4 %collective-permute-start.4 = (f32[8,128]{1,0:T(8,128)S(1)}, f32[8,128]{1,0:T(8,128)S(1)}, u32[]{:S(2)}, u32[]{:S(2)}) collective-permute-start(f32[8,128]{1,0:T(8,128)S(1)} %get-tuple-element.25.after), channel_id=1, source_target_pairs={{0,3},{1,2},{2,1},{3,0},{4,7},{5,6},{6,5},{7,4},{8,11},{9,10},{10,... | collective-permute-start | bytes 12296 | tf_op jit(solution)/shard_map/ppermute | solution.py:205
  21.4 0.0 collective-permute-start.3
  21.4 0.2 collective-permute-start.2
  21.6 0.0 collective-permute-done.9.from_cross
  21.6 0.8 %project_near.3.refs_0_ = f32[1,7,144,128]{3,2,1,0:T(8,128)S(1)} custom-call(f32[8,128]{1,0:T(8,128)S(1)} %get-tuple-element.25.after, bf16[48,2048]{1,0:T(8,128)(2,1)S(1)} %get-tuple-element.20.half, bf16[48,5760]{1,0:T(8,128)(2,1)S(1)} %collective-permute-done.from_pair, bf16[48,2048]{1,0:T(8,128)(2,1)S(1)} %collective-permute-done.9.from_cross, ...), custom_call_target="tpu_custom_call" | custom-call | flops 528482304 | bytes 1048576 | tf_op jit(solution)/shard_map/project_near/pallas_call | solution.py:299
  22.4 0.3 collective-permute-done.4
  22.7 2.3 %collective-permute-done.3 = f32[8,128]{1,0:T(8,128)S(1)} collective-permute-done((f32[8,128]{1,0:T(8,128)S(1)}, f32[8,128]{1,0:T(8,128)S(1)}, u32[]{:S(2)}, u32[]{:S(2)}) %collective-permute-start.3) | collective-permute-done | bytes 4128 | tf_op jit(solution)/shard_map/ppermute | solution.py:205
  25.0 0.0 collective-permute-done.2
  25.0 3.5 %collective-permute-start.7 = (f32[8,128]{1,0:T(8,128)S(1)}, f32[8,128]{1,0:T(8,128)S(1)}, u32[]{:S(2)}, u32[]{:S(2)}) collective-permute-start(f32[8,128]{1,0:T(8,128)S(1)} %add_add_fusion.1.after), channel_id=1, source_target_pairs={{0,16},{1,17},{2,18},{3,19},{4,20},{5,21},{6,22},{7,23},{8,24},{9,... | collective-permute-start | bytes 12296 | tf_op jit(solution)/shard_map/ppermute | solution.py:205
  28.5 1.1 %collective-permute-start.6 = (f32[8,128]{1,0:T(8,128)S(1)}, f32[8,128]{1,0:T(8,128)S(1)}, u32[]{:S(2)}, u32[]{:S(2)}) collective-permute-start(f32[8,128]{1,0:T(8,128)S(1)} %add_add_fusion.1.after), channel_id=1, source_target_pairs={{0,24},{1,25},{2,26},{3,27},{4,28},{5,29},{6,30},{7,31},{8,16},{9,... | collective-permute-start | bytes 12296 | tf_op jit(solution)/shard_map/ppermute | solution.py:205
  29.7 0.0 collective-permute-start.5
  29.7 0.8 %project_near.4.refs_1_ = f32[1,7,144,128]{3,2,1,0:T(8,128)S(1)} custom-call(f32[8,128]{1,0:T(8,128)S(1)} %add_add_fusion.1.after, bf16[48,2048]{1,0:T(8,128)(2,1)S(1)} %get-tuple-element.20.half, bf16[48,5760]{1,0:T(8,128)(2,1)S(1)} %collective-permute-done.from_pair, bf16[48,2048]{1,0:T(8,128)(2,1)S(1)} %collective-permute-done.9.from_cross, ...), custom_call_target="tpu_custom_call" | custom-call | flops 528482304 | bytes 1048576 | tf_op jit(solution)/shard_map/project_near/pallas_call | solution.py:299
  30.5 0.0 collective-permute-done.7
  30.5 2.8 %collective-permute-done.6 = f32[8,128]{1,0:T(8,128)S(1)} collective-permute-done((f32[8,128]{1,0:T(8,128)S(1)}, f32[8,128]{1,0:T(8,128)S(1)}, u32[]{:S(2)}, u32[]{:S(2)}) %collective-permute-start.6) | collective-permute-done | bytes 4128 | tf_op jit(solution)/shard_map/ppermute | solution.py:205
  33.3 0.0 collective-permute-done.5
  33.4 0.0 copy-start
  33.4 0.0 copy-start.1
  33.4 0.0 copy-start.3
  33.4 3.9 %collective-permute-start.8 = (f32[8,128]{1,0:T(8,128)S(1)}, f32[8,128]{1,0:T(8,128)S(1)}, u32[]{:S(2)}, u32[]{:S(2)}) collective-permute-start(f32[8,128]{1,0:T(8,128)S(1)} %add_add_fusion.after), channel_id=1, source_target_pairs={{0,6},{1,7},{2,4},{3,5},{4,2},{5,3},{6,0},{7,1},{8,14},{9,15},{10,... | collective-permute-start | bytes 12296 | tf_op jit(solution)/shard_map/ppermute | solution.py:205
  37.3 1.5 %project_near.5.refs_2_ = f32[2,7,144,128]{3,2,1,0:T(8,128)S(1)} custom-call(f32[8,128]{1,0:T(8,128)S(1)} %add_add_fusion.after, bf16[48,2048]{1,0:T(8,128)(2,1)S(1)} %get-tuple-element.20.half, bf16[48,5760]{1,0:T(8,128)(2,1)S(1)} %collective-permute-done.from_pair, bf16[48,2048]{1,0:T(8,128)(2,1)S(1)} %collective-permute-done.9.from_cross, ...), custom_call_target="tpu_custom_call" | custom-call | flops 1056964608 | bytes 1048576 | tf_op jit(solution)/shard_map/project_near/pallas_call | solution.py:299
  38.8 0.1 collective-permute-done.8
  38.9 0.0 copy-done
  38.9 0.0 copy-done.1
  38.9 0.0 copy-done.3
  38.9 3.1 %finish.1 = (f32[48,2048]{1,0:T(8,128)}, f32[16,64,896]{2,1,0:T(8,128)}, f32[48,2048]{1,0:T(8,128)}, f32[48,2048]{1,0:T(8,128)}) custom-call(s32[16]{0:T(128)S(1)} %copy-done.3, f32[8,128]{1,0:T(8,128)S(1)} %add.27.sums, f32[48,2048]{1,0:T(8,128)S(1)} %copy-done.1, f32[48,2048]{1,0:T(8,128)S(1)} %copy-done, f32[48,2048]{1,0:T(8,128)S(1)} %get-tuple-element.26.residual_part, ...), custom_call_target="tpu_custom_call" | custom-call | tf_op jit(solution)/shard_map/finish/pallas_call | solution.py:316
  (3 shorter events, 0.0 us)
Async XLA Ops:
  0.6 3.3 %copy-start.2 = (f32[48,2048]{1,0:T(8,128)S(1)}, f32[48,2048]{1,0:T(8,128)}, u32[]{:S(2)}) copy-start(f32[48,2048]{1,0:T(8,128)} %gradient.1) | copy-start | bytes 1179652
  3.2 7.5 %collective-permute-start = (bf16[48,5760]{1,0:T(8,128)(2,1)S(1)}, bf16[48,5760]{1,0:T(8,128)(2,1)S(1)}, u32[]{:S(2)}, u32[]{:S(2)}) collective-permute-start(bf16[48,5760]{1,0:T(8,128)(2,1)S(1)} %get-tuple-element.18), channel_id=1, source_target_pairs={{0,1},{1,0},{2,3},{3,2},{4,5},{5,4},{6,7},{7,6},{8,9},{9,8},{10,11... | collective-permute-start | bytes 1658888 | tf_op jit(solution)/shard_map/ppermute | solution.py:259
  3.2 7.4 %collective-permute-start.1 = (bf16[48,3712]{1,0:T(8,128)(2,1)S(1)}, bf16[48,3712]{1,0:T(8,128)(2,1)S(1)}, u32[]{:S(2)}, u32[]{:S(2)}) collective-permute-start(bf16[48,3712]{1,0:T(8,128)(2,1)S(1)} %get-tuple-element.19), channel_id=1, source_target_pairs={{1,2},{3,4},{5,6},{7,8},{9,10},{11,12},{13,14},{15,16},{17,18},{19... | collective-permute-start | bytes 1069064 | tf_op jit(solution)/shard_map/ppermute | solution.py:258
  10.0 11.6 %collective-permute-start.9 = (bf16[48,2048]{1,0:T(8,128)(2,1)S(1)}, bf16[48,2048]{1,0:T(8,128)(2,1)S(1)}, u32[]{:S(2)}, u32[]{:S(2)}) collective-permute-start(bf16[48,2048]{1,0:T(8,128)(2,1)S(1)} %get-tuple-element.28), channel_id=1, source_target_pairs={{1,2},{3,4},{5,6},{7,8},{9,10},{11,12},{13,14},{15,16},{17,18},{19... | collective-permute-start | bytes 589832 | tf_op jit(solution)/shard_map/ppermute | solution.py:280
  15.0 7.7 %collective-permute-start.4 = (f32[8,128]{1,0:T(8,128)S(1)}, f32[8,128]{1,0:T(8,128)S(1)}, u32[]{:S(2)}, u32[]{:S(2)}) collective-permute-start(f32[8,128]{1,0:T(8,128)S(1)} %get-tuple-element.25.after), channel_id=1, source_target_pairs={{0,3},{1,2},{2,1},{3,0},{4,7},{5,6},{6,5},{7,4},{8,11},{9,10},{10,... | collective-permute-start | bytes 12296 | tf_op jit(solution)/shard_map/ppermute | solution.py:205
  21.4 3.6 %collective-permute-start.3 = (f32[8,128]{1,0:T(8,128)S(1)}, f32[8,128]{1,0:T(8,128)S(1)}, u32[]{:S(2)}, u32[]{:S(2)}) collective-permute-start(f32[8,128]{1,0:T(8,128)S(1)} %get-tuple-element.25.after), channel_id=1, source_target_pairs={{0,2},{1,3},{2,0},{3,1},{4,6},{5,7},{6,4},{7,5},{8,10},{9,11},{10,... | collective-permute-start | bytes 12296 | tf_op jit(solution)/shard_map/ppermute | solution.py:205
  21.4 3.6 %collective-permute-start.2 = (f32[8,128]{1,0:T(8,128)S(1)}, f32[8,128]{1,0:T(8,128)S(1)}, u32[]{:S(2)}, u32[]{:S(2)}) collective-permute-start(f32[8,128]{1,0:T(8,128)S(1)} %get-tuple-element.25.after), channel_id=1, source_target_pairs={{0,1},{1,0},{2,3},{3,2},{4,5},{5,4},{6,7},{7,6},{8,9},{9,8},{10,11... | collective-permute-start | bytes 12296 | tf_op jit(solution)/shard_map/ppermute | solution.py:205
  25.0 5.5 %collective-permute-start.7 = (f32[8,128]{1,0:T(8,128)S(1)}, f32[8,128]{1,0:T(8,128)S(1)}, u32[]{:S(2)}, u32[]{:S(2)}) collective-permute-start(f32[8,128]{1,0:T(8,128)S(1)} %add_add_fusion.1.after), channel_id=1, source_target_pairs={{0,16},{1,17},{2,18},{3,19},{4,20},{5,21},{6,22},{7,23},{8,24},{9,... | collective-permute-start | bytes 12296 | tf_op jit(solution)/shard_map/ppermute | solution.py:205
  28.5 4.8 %collective-permute-start.6 = (f32[8,128]{1,0:T(8,128)S(1)}, f32[8,128]{1,0:T(8,128)S(1)}, u32[]{:S(2)}, u32[]{:S(2)}) collective-permute-start(f32[8,128]{1,0:T(8,128)S(1)} %add_add_fusion.1.after), channel_id=1, source_target_pairs={{0,24},{1,25},{2,26},{3,27},{4,28},{5,29},{6,30},{7,31},{8,16},{9,... | collective-permute-start | bytes 12296 | tf_op jit(solution)/shard_map/ppermute | solution.py:205
  29.7 3.7 %collective-permute-start.5 = (f32[8,128]{1,0:T(8,128)S(1)}, f32[8,128]{1,0:T(8,128)S(1)}, u32[]{:S(2)}, u32[]{:S(2)}) collective-permute-start(f32[8,128]{1,0:T(8,128)S(1)} %add_add_fusion.1.after), channel_id=1, source_target_pairs={{0,8},{1,9},{2,10},{3,11},{4,12},{5,13},{6,14},{7,15},{8,0},{9,1},... | collective-permute-start | bytes 12296 | tf_op jit(solution)/shard_map/ppermute | solution.py:205
  33.4 5.5 %copy-start = (f32[48,2048]{1,0:T(8,128)S(1)}, f32[48,2048]{1,0:T(8,128)}, u32[]{:S(2)}) copy-start(f32[48,2048]{1,0:T(8,128)} %direction.1) | copy-start | bytes 1179652
  33.4 5.5 %copy-start.1 = (f32[48,2048]{1,0:T(8,128)S(1)}, f32[48,2048]{1,0:T(8,128)}, u32[]{:S(2)}) copy-start(f32[48,2048]{1,0:T(8,128)} %solution.1) | copy-start | bytes 1179652
  33.4 5.5 %copy-start.3 = (s32[16]{0:T(128)S(1)}, s32[16]{0:T(128)}, u32[]{:S(2)}) copy-start(s32[16]{0:T(128)} %offsets.1) | copy-start | bytes 196
  33.4 5.5 %collective-permute-start.8 = (f32[8,128]{1,0:T(8,128)S(1)}, f32[8,128]{1,0:T(8,128)S(1)}, u32[]{:S(2)}, u32[]{:S(2)}) collective-permute-start(f32[8,128]{1,0:T(8,128)S(1)} %add_add_fusion.after), channel_id=1, source_target_pairs={{0,6},{1,7},{2,4},{3,5},{4,2},{5,3},{6,0},{7,1},{8,14},{9,15},{10,... | collective-permute-start | bytes 12296 | tf_op jit(solution)/shard_map/ppermute | solution.py:205
